TPU v7x, 32 devices: a whole 2x2x4 slice. The times are simulated.
32 devices in a mesh: panel: 2 (over core), lat: 4 (over y, x), lon: 4 (over z).
Axes of the slice: x: 2, y: 2, z: 4, core: 2. Of those that a mesh axis runs over, the one named last changes fastest.
Arguments:
- mass_per_volume: float32 [2, 16, 128, 1536], P('panel', None, 'lat', 'lon'), may hold values from 0.5 to 2
- flow_speed: float32 [2, 3, 16, 128, 1536], P('panel', None, None, 'lat', 'lon'), may hold values from -3 to 3
- heat_measure: float32 [2, 16, 128, 1536], P('panel', None, 'lat', 'lon'), may hold values from 0.5 to 2
- fields_at_outset: float32 [2, 5, 16, 128, 1536], P('panel', None, None, 'lat', 'lon'), may hold values from -6 to 6
- opposite_block: int32 [2, 4, 4, 1664], P('panel', 'lat', 'lon'), may hold values from 0 to 3, as said below
- donor_lower_corner: int32 [2, 4, 4, 1664], P('panel', 'lat', 'lon'), may hold values from 0 to 11902, as said below
- blend_factors: float32 [2, 4, 4, 4, 1664], P('panel', 'lat', 'lon'), may hold values from 0 to 1, as said below
- frame_turning: float32 [2, 4, 4, 2, 1664], P('panel', 'lat', 'lon'), may hold values from -1 to 1, as said below
Outputs:
- section_rate: float32 [2, 5, 16, 128, 1536], P('panel', None, None, 'lat', 'lon')
- new_state: float32 [2, 5, 16, 128, 1536], P('panel', None, None, 'lat', 'lon')
Inputs may be any that keep to these rules, and one draw needn't show every extreme that they name: `opposite_block`: within each side of a block's slots (768, 768, 64, 64 slots), the slots fall into 4 runs of equal length in order, and the runs name different partners. `donor_lower_corner`: the source corners i, i + 1 and j, j + 1 lie inside the partner block. `blend_factors`: Nonnegative, summing to one over the four corners. `frame_turning`: cosine and sine of one angle.
All inputs are finite; a program needn't handle non-finite values.
Results may differ from a plain program's by a relative error of at most 0.0003.
Values sent between devices are 32-bit elements; how exact they have to be, the bound alone decides.
No kernel may reach another device: no remote copies, remote signals or barrier semaphores. Data moves between devices by JAX's collectives and lax.ppermute only.
A program may use at most 128 MiB of HBM per device.

v0:
```python
import functools
import math

import jax
import jax.numpy as jnp
from jax import lax
from jax.experimental import pallas as pl
from jax.experimental.pallas import tpu as pltpu
from jax.sharding import PartitionSpec as P

OMEGA = 0.5
GRAVITY = 1.0
VISCOSITY = 0.2
DIFFUSIVITY = 0.2
GAMMA = 1.4
TIME_STEP = 0.05
LANES = 128
SUB = 8
ANY = pl.BlockSpec(memory_space=pl.ANY)
VMEM = pl.BlockSpec(memory_space=pltpu.VMEM)
SMEM = pl.BlockSpec(memory_space=pltpu.SMEM)


def pair_partner(i, count, odd):
    if not odd:
        return i ^ 1
    return (i + 1) % count if i % 2 else (i - 1) % count


def swap_pairs(value, axis, odd):
    count = lax.axis_size(axis)
    return lax.ppermute(value, axis, [(i, pair_partner(i, count, odd)) for i in range(count)])


def swap_panels(value, distance):
    n_lat = lax.axis_size("lat")
    pairs = [
        (p * n_lat + a, (1 - p) * n_lat + (a ^ distance)) for p in range(2) for a in range(n_lat)
    ]
    return lax.ppermute(value, ("panel", "lat"), pairs)


def window_of(run, cols):
    tiles = cols // LANES
    for width in range(1, tiles + 1):
        if all(
            start - min(start // LANES, tiles - width) * LANES + run <= width * LANES
            for start in range(0, cols, run)
        ):
            return width
    return tiles


def edge_rows_kernel(rho, flow, heat, even_out, odd_out, tops, bottoms, sems):
    levels = rho.shape[1]
    rows = rho.shape[2]
    copies = []
    for side, buf, start in ((0, tops, 0), (1, bottoms, rows - SUB)):
        span = pl.ds(start, SUB)
        copies.append(pltpu.make_async_copy(rho.at[0, :, span], buf.at[0], sems.at[side, 0]))
        copies.append(
            pltpu.make_async_copy(flow.at[0, :, :, span], buf.at[pl.ds(1, 3)], sems.at[side, 1])
        )
        copies.append(pltpu.make_async_copy(heat.at[0, :, span], buf.at[4], sems.at[side, 2]))
    for copy in copies:
        copy.start()
    for copy in copies:
        copy.wait()
    even = lax.rem(lax.axis_index("lat"), 2) == 0
    for row in range(2):
        for field in range(5):
            for tile in range(even_out.shape[2]):
                lanes = slice(tile * LANES, (tile + 1) * LANES)
                top = tops[field, :, row, lanes]
                bottom = bottoms[field, :, SUB - 2 + row, lanes]
                even_out[row, field, tile] = jnp.where(even, bottom, top)
                odd_out[row, field, tile] = jnp.where(even, top, bottom)


def edge_rows(rho, flow, heat):
    levels, rows, cols = rho.shape[1:]
    shape = jax.ShapeDtypeStruct((2, 5, cols // LANES, levels, LANES), jnp.float32)
    return pl.pallas_call(
        edge_rows_kernel,
        out_shape=(shape, shape),
        in_specs=[ANY] * 3,
        out_specs=(VMEM, VMEM),
        scratch_shapes=[
            pltpu.VMEM((5, levels, SUB, cols), jnp.float32),
            pltpu.VMEM((5, levels, SUB, cols), jnp.float32),
            pltpu.SemaphoreType.DMA((2, 3)),
        ],
        name="edge_rows",
    )(rho, flow, heat)


def cell_major_kernel(rho, flow, heat, cells, even_out, odd_out):
    levels = rho.shape[1]
    cols = rho.shape[3]
    field_rows = 5 * levels
    for row in range(SUB):
        for start in range(0, cols, LANES):
            span = slice(start, start + LANES)
            stack = jnp.concatenate(
                [rho[0, :, row, span]]
                + [flow[0, part, :, row, span] for part in range(3)]
                + [heat[0, :, row, span]],
                axis=0,
            )
            at = row * cols + start
            cells[at : at + LANES, 0:field_rows] = stack.T
    even = lax.rem(lax.axis_index("lon"), 2) == 0
    for row in range(SUB):
        for layer in range(2):
            west = cells[row * cols + layer : row * cols + layer + 1, :]
            at = row * cols + cols - 2 + layer
            east = cells[at : at + 1, :]
            even_out[layer, row : row + 1, :] = jnp.where(even, east, west)
            odd_out[layer, row : row + 1, :] = jnp.where(even, west, east)


def cell_major(rho, flow, heat):
    levels, rows, cols = rho.shape[1:]
    column = jax.ShapeDtypeStruct((2, rows, LANES), jnp.float32)
    column_spec = pl.BlockSpec((2, SUB, LANES), lambda i: (0, i, 0))
    return pl.pallas_call(
        cell_major_kernel,
        grid=(rows // SUB,),
        out_shape=(jax.ShapeDtypeStruct((rows * cols, LANES), jnp.float32), column, column),
        in_specs=[
            pl.BlockSpec((1, levels, SUB, cols), lambda i: (0, 0, i, 0)),
            pl.BlockSpec((1, 3, levels, SUB, cols), lambda i: (0, 0, 0, i, 0)),
            pl.BlockSpec((1, levels, SUB, cols), lambda i: (0, 0, i, 0)),
        ],
        out_specs=(
            pl.BlockSpec((SUB * cols, LANES), lambda i: (i, 0)),
            column_spec,
            column_spec,
        ),
        name="cell_major",
    )(rho, flow, heat)


def donate_kernel(n_lat, n_lon, rows, cols, field_rows, *refs):
    requests = refs[:n_lat]
    cells = refs[n_lat]
    replies = refs[n_lat + 1 : 2 * n_lat + 1]
    gathered = refs[2 * n_lat + 1]
    lat_len, lon_len = 2 * cols, 2 * rows
    run_lat, run_lon = lat_len // n_lat, lon_len // n_lat
    tiles = cols // LANES
    width = window_of(run_lat, cols)
    lat_here = lax.axis_index("lat")
    lon_here = lax.axis_index("lon")

    def find_run(request, start, run):
        found = jnp.int32(0)
        for r in range(1, n_lat):
            match = request[0, start + r * run].astype(jnp.int32) == lat_here
            found = jnp.where(match, jnp.int32(r), found)
        return found

    def blend(request, slot):
        cell = request[1, slot].astype(jnp.int32)
        total = request[2, slot] * cells[pl.ds(cell, 1), :]
        total += request[3, slot] * cells[pl.ds(cell + cols, 1), :]
        total += request[4, slot] * cells[pl.ds(cell + 1, 1), :]
        total += request[5, slot] * cells[pl.ds(cell + cols + 1, 1), :]
        return total

    for distance in range(n_lat):
        request, reply = requests[distance], replies[distance]
        asker = jnp.bitwise_xor(lat_here, distance)

        @pl.when((asker == 0) | (asker == n_lat - 1))
        def _():
            run = find_run(request, 0, run_lat)
            start = lax.rem(run * run_lat, cols)
            base = jnp.minimum(lax.div(start, LANES), tiles - width)
            offset = start - base * LANES

            def step(t, carry):
                gathered[pl.ds(offset + t, 1), :] = blend(request, run * run_lat + t)
                return carry

            lax.fori_loop(0, run_lat, step, 0, unroll=8)
            for tile in range(width):
                block = gathered[tile * LANES : (tile + 1) * LANES, :]
                reply[0:field_rows, tile * LANES : (tile + 1) * LANES] = block.T[0:field_rows]

        @pl.when((lon_here == 0) | (lon_here == n_lon - 1))
        def _():
            run = find_run(request, lat_len, run_lon)

            def step(t, carry):
                gathered[pl.ds(t, 1), :] = blend(request, lat_len + run * run_lon + t)
                return carry

            lax.fori_loop(0, run_lon, step, 0, unroll=8)
            reply[field_rows : field_rows + run_lon, 0:LANES] = gathered[0:run_lon, :]


def donate(requests, cells, rows, cols, field_rows):
    n_lat, n_lon = lax.axis_size("lat"), lax.axis_size("lon")
    width = window_of(2 * cols // n_lat, cols)
    reply = jax.ShapeDtypeStruct(
        (field_rows + 2 * rows // n_lat, max(width, 1) * LANES), jnp.float32
    )
    return pl.pallas_call(
        functools.partial(donate_kernel, n_lat, n_lon, rows, cols, field_rows),
        out_shape=(reply,) * n_lat,
        in_specs=[SMEM] * n_lat + [VMEM],
        out_specs=(VMEM,) * n_lat,
        scratch_shapes=[pltpu.VMEM((width * LANES, LANES), jnp.float32)],
        name="donate",
    )(*requests, cells)


def stencil_kernel(geometry, groups, chunk, aliased, *refs):
    n_panel, n_lat, n_lon, levels, rows, cols = geometry
    tiles = cols // LANES
    field_rows = 5 * levels
    (partners, turn_lat, turn_lon) = refs[:3]
    replies = refs[3 : 3 + n_lat]
    at = 3 + n_lat
    lat_even, lat_odd, lon_even, lon_odd = refs[at : at + 4]
    rho, flow, heat, outset = refs[at + 4 : at + 8]
    at += 8 + (2 if aliased else 0)
    rate_out, state_out = refs[at : at + 2]
    (
        block,
        start_box,
        rate_box,
        state_box,
        reply_box,
        halo,
        side,
        mixed,
        row_box,
        spin_box,
        in_sems,
        start_sems,
        out_sems,
        edge_sems,
    ) = refs[at + 2 :]
    lat_here = lax.axis_index("lat")
    lon_here = lax.axis_index("lon")
    panel_here = lax.axis_index("panel")
    lat_len, lon_len = 2 * cols, 2 * rows
    run_lat, run_lon = lat_len // n_lat, lon_len // n_lat
    width = window_of(run_lat, cols)
    step_lat = math.pi / 2.0 / (rows * n_lat)
    step_lon = 1.5 * math.pi / (cols * n_lon)
    chunks = levels // chunk

    def load_copies(c):
        span = pl.ds(c * chunk, chunk)
        out = []
        for t in range(tiles):
            lanes = pl.ds(t * LANES, LANES)
            body = pl.ds(SUB, rows)
            out.append(
                pltpu.make_async_copy(
                    rho.at[0, span, :, lanes], block.at[0, t, span, body], in_sems.at[c, t, 0]
                )
            )
            out.append(
                pltpu.make_async_copy(
                    flow.at[0, :, span, :, lanes],
                    block.at[pl.ds(1, 3), t, span, body],
                    in_sems.at[c, t, 1],
                )
            )
            out.append(
                pltpu.make_async_copy(
                    heat.at[0, span, :, lanes], block.at[4, t, span, body], in_sems.at[c, t, 2]
                )
            )
        return out

    def start_copies(c):
        span = pl.ds(c * chunk, chunk)
        return [
            pltpu.make_async_copy(
                outset.at[0, :, span, pl.ds(first, count)],
                start_box.at[:, span, pl.ds(first, count)],
                start_sems.at[c, g],
            )
            for g, (first, count) in enumerate(groups)
        ]

    def out_copies(c):
        span = pl.ds(c * chunk, chunk)
        out = []
        for g, (first, count) in enumerate(groups):
            part = pl.ds(first, count)
            out.append(
                pltpu.make_async_copy(
                    rate_box.at[:, span, part], rate_out.at[0, :, span, part], out_sems.at[c, g, 0]
                )
            )
            out.append(
                pltpu.make_async_copy(
                    state_box.at[:, span, part],
                    state_out.at[0, :, span, part],
                    out_sems.at[c, g, 1],
                )
            )
        return out

    for copy in load_copies(0):
        copy.start()
    reply_copies = [
        pltpu.make_async_copy(replies[d], reply_box.at[d], edge_sems.at[d]) for d in range(n_lat)
    ]
    for copy in reply_copies:
        copy.start()
    lat_is_even = lax.rem(lat_here, 2) == 0
    lon_is_even = lax.rem(lon_here, 2) == 0

    def halo_copies(which):
        even_at = jnp.where(which == 0, 1, 0)
        return (
            pltpu.make_async_copy(lat_even, halo.at[even_at], edge_sems.at[n_lat]),
            pltpu.make_async_copy(lat_odd, halo.at[1 - even_at], edge_sems.at[n_lat + 1]),
            pltpu.make_async_copy(lon_even, side.at[0], edge_sems.at[n_lat + 2]),
            pltpu.make_async_copy(lon_odd, side.at[1], edge_sems.at[n_lat + 3]),
        )

    edge_copies = halo_copies(lax.rem(lat_here, 2))
    for copy in edge_copies:
        copy.start()
    for copy in start_copies(0):
        copy.start()
    for c in range(1, chunks):
        for copy in load_copies(c) + start_copies(c):
            copy.start()

    @pl.when(True)
    def _():
        sub = lax.broadcasted_iota(jnp.int32, (rows, LANES), 0)
        row_global = (lat_here * rows + sub).astype(jnp.float32)
        theta = math.pi / 4.0 + (row_global + 0.5) * step_lat
        sin_lat, cos_lat = jnp.sin(theta), jnp.cos(theta)
        row_box[0] = 1.0 / sin_lat
        row_box[1] = cos_lat / sin_lat
        yang = panel_here.astype(jnp.float32)
        yin = 1.0 - yang
        for t in range(tiles):
            lane = lax.broadcasted_iota(jnp.int32, (SUB, LANES), 1) + t * LANES
            col_global = (lon_here * cols + lane).astype(jnp.float32)
            longitude = -0.75 * math.pi + (col_global + 0.5) * step_lon
            sin_lon = jnp.sin(longitude)[0:1]
            cos_lon = jnp.cos(longitude)[0:1]
            spin_box[0, t] = 2.0 * OMEGA * (yin * cos_lat + yang * sin_lat * sin_lon)
            spin_box[1, t] = 2.0 * OMEGA * (yang * cos_lat * sin_lon - yin * sin_lat)
            spin_box[2, t] = jnp.broadcast_to(2.0 * OMEGA * yang * cos_lon, (rows, LANES))

    for copy in reply_copies:
        copy.wait()
    for copy in edge_copies:
        copy.wait()

    lane8 = lax.broadcasted_iota(jnp.int32, (SUB, LANES), 1)
    sub8 = lax.broadcasted_iota(jnp.int32, (SUB, LANES), 0)

    for which, slot0 in ((0, 0), (1, lat_len)):

        @pl.when(lat_here == (0 if which == 0 else n_lat - 1))
        def _(which=which, slot0=slot0):
            sources = [
                jnp.bitwise_xor(partners[0, slot0 + r * run_lat], lat_here) for r in range(n_lat)
            ]
            for layer in range(2):
                for t in range(tiles):
                    lane = lax.broadcasted_iota(jnp.int32, (field_rows, LANES), 1) + t * LANES
                    value = None
                    for r in range(n_lat):
                        first = r * run_lat - layer * cols
                        if first < 0 or first >= cols:
                            continue
                        if first >= (t + 1) * LANES or first + run_lat <= t * LANES:
                            continue
                        base = min(first // LANES, tiles - width)
                        here = (t - base) * LANES
                        piece = reply_box[sources[r], 0:field_rows, here : here + LANES]
                        value = piece if value is None else jnp.where(lane >= first, piece, value)
                    spot = slot0 + layer * cols + t * LANES
                    cosine = turn_lat[0:1, spot : spot + LANES]
                    sine = turn_lat[1:2, spot : spot + LANES]
                    parts = [value[f * levels : (f + 1) * levels] for f in range(5)]
                    parts[2], parts[3] = (
                        cosine * parts[2] + sine * parts[3],
                        cosine * parts[3] - sine * parts[2],
                    )
                    for f in range(5):
                        halo[which, layer, f, t] = parts[f]

    for which, slot0 in ((0, 2 * lat_len), (1, 2 * lat_len + lon_len)):
        mine = jnp.where(lon_is_even, 1, 0) if which == 0 else jnp.where(lon_is_even, 0, 1)

        @pl.when(lon_here != (0 if which == 0 else n_lon - 1))
        def _(which=which, mine=mine):
            side[2 + which] = side[mine]

        @pl.when(lon_here == (0 if which == 0 else n_lon - 1))
        def _(which=which, slot0=slot0):
            lane = lax.broadcasted_iota(jnp.int32, (run_lon, LANES), 1)
            is_lat = (lane >= 2 * levels) & (lane < 3 * levels)
            is_lon = (lane >= 3 * levels) & (lane < 4 * levels)
            for r in range(n_lat):
                source = jnp.bitwise_xor(partners[0, slot0 + r * run_lon], lat_here)
                layer, first = r * run_lon // rows, r * run_lon % rows
                value = reply_box[source, field_rows : field_rows + run_lon, 0:LANES]
                slots = slice(which * lon_len + r * run_lon, which * lon_len + (r + 1) * run_lon)
                cosine = jnp.broadcast_to(turn_lon[slots, 0:1], (run_lon, LANES))
                sine = jnp.broadcast_to(turn_lon[slots, 1:2], (run_lon, LANES))
                later = pltpu.roll(value, LANES - levels, 1)
                earlier = pltpu.roll(value, levels, 1)
                value = jnp.where(
                    is_lat,
                    cosine * value + sine * later,
                    jnp.where(is_lon, cosine * value - sine * earlier, value),
                )
                side[2 + which, layer, first : first + run_lon] = value

    lane_all = lax.broadcasted_iota(jnp.int32, (rows, LANES), 1)
    columns = [side[3, 0], side[3, 1], side[2, 0], side[2, 1]]
    columns = [columns[0]] + [pltpu.roll(columns[j], j, 1) for j in range(1, 4)]
    for q in range(4):
        pick = jnp.bitwise_and(lane_all - q, 3)
        value = columns[0]
        for j in range(1, 4):
            value = jnp.where(pick == j, columns[j], value)
        mixed[q] = value

    for copy in load_copies(0):
        copy.wait()

    by_lat = 1.0 / (12.0 * step_lat)
    by_lon = 1.0 / (12.0 * step_lon)

    def one_level(k):
        below = jnp.maximum(k - 1, 0)
        above = jnp.minimum(k + 1, levels - 1)
        quarter = jnp.bitwise_and(k, 3)
        radius = jnp.broadcast_to(
            1.0 / step_lat + k.astype(jnp.float32), (SUB, LANES)
        )
        inv_radius = 1.0 / radius
        lat_scale = inv_radius * by_lat
        for first, count in groups:
            for top in range(first, first + count, SUB):
                one_strip(k, below, above, quarter, inv_radius, lat_scale, top)

    def one_strip(k, below, above, quarter, inv_radius, lat_scale, top):
        strip = slice(top, top + SUB)
        inv_sin, cot = row_box[0, strip], row_box[1, strip]
        inv_arc = inv_radius * inv_sin
        lon_scale = inv_arc * by_lon
        cot_r = cot * inv_radius
        two_r = 2.0 * inv_radius
        curve_lat = (VISCOSITY / (12.0 * step_lat * step_lat)) * inv_radius * inv_radius
        curve_lon = (VISCOSITY / (12.0 * step_lon * step_lon)) * inv_arc * inv_arc
        slope_extra = (VISCOSITY * by_lat) * inv_radius * cot_r
        radial_extra = VISCOSITY * inv_radius
        center_weight = 2.0 * VISCOSITY + 30.0 * (curve_lat + curve_lon)
        north, south = top == 0, top == rows - SUB

        def derive(f, full):
            here = [block[f, t, k, SUB + top : 2 * SUB + top] for t in range(tiles)]
            shift = LANES - 2 - f * levels - k
            ghost = pltpu.roll(mixed[quarter, strip], shift, 1)
            ghost_w, ghost_e = pltpu.roll(ghost, LANES - 1, 1), pltpu.roll(ghost, 1, 1)
            w1s = [pltpu.roll(x, 1, 1) for x in here]
            w2s = [pltpu.roll(x, 2, 1) for x in here]
            e1s = [pltpu.roll(x, LANES - 1, 1) for x in here]
            e2s = [pltpu.roll(x, LANES - 2, 1) for x in here]
            out = []
            for t in range(tiles):
                at = SUB + top
                n1, n2 = block[f, t, k, at - 1 : at + 7], block[f, t, k, at - 2 : at + 6]
                s1, s2 = block[f, t, k, at + 1 : at + 9], block[f, t, k, at + 2 : at + 10]
                if north:
                    g2 = jnp.broadcast_to(halo[0, 0, f, t, pl.ds(k, 1), :], (SUB, LANES))
                    g1 = jnp.broadcast_to(halo[0, 1, f, t, pl.ds(k, 1), :], (SUB, LANES))
                    n1 = jnp.where(sub8 == 0, g1, n1)
                    n2 = jnp.where(sub8 == 0, g2, jnp.where(sub8 == 1, g1, n2))
                if south:
                    g1 = jnp.broadcast_to(halo[1, 0, f, t, pl.ds(k, 1), :], (SUB, LANES))
                    g2 = jnp.broadcast_to(halo[1, 1, f, t, pl.ds(k, 1), :], (SUB, LANES))
                    s1 = jnp.where(sub8 == SUB - 1, g1, s1)
                    s2 = jnp.where(sub8 == SUB - 1, g2, jnp.where(sub8 == SUB - 2, g1, s2))
                w1 = jnp.where(lane8 == 0, w1s[t - 1] if t else ghost_w, w1s[t])
                w2 = jnp.where(lane8 < 2, w2s[t - 1] if t else ghost, w2s[t])
                last = t == tiles - 1
                e1 = jnp.where(lane8 == LANES - 1, ghost_e if last else e1s[t + 1], e1s[t])
                e2 = jnp.where(lane8 >= LANES - 2, ghost if last else e2s[t + 1], e2s[t])
                low = block[f, t, below, SUB + top : 2 * SUB + top]
                high = block[f, t, above, SUB + top : 2 * SUB + top]
                rad = high - low
                lat = 8.0 * (s1 - n1) - (s2 - n2)
                lon = 8.0 * (e1 - w1) - (e2 - w2)
                bend = None
                if full:
                    bend = (
                        VISCOSITY * (high + low)
                        + curve_lat * (16.0 * (s1 + n1) - (s2 + n2))
                        + curve_lon * (16.0 * (e1 + w1) - (e2 + w2))
                        - center_weight * here[t]
                    )
                out.append((rad, lat, lon, bend))
            return here, out

        wind_rad = [block[1, t, k, SUB + top : 2 * SUB + top] for t in range(tiles)]
        wind_lat = [block[2, t, k, SUB + top : 2 * SUB + top] for t in range(tiles)]
        wind_lon = [block[3, t, k, SUB + top : 2 * SUB + top] for t in range(tiles)]
        go_rad = [0.5 * x for x in wind_rad]
        go_lat = [lat_scale * x for x in wind_lat]
        go_lon = [lon_scale * x for x in wind_lon]

        def put(f, t, center, rate):
            lanes = slice(t * LANES, (t + 1) * LANES)
            rate_box[f, k, strip, lanes] = rate
            state_box[f, k, strip, lanes] = (
                0.75 * start_box[f, k, strip, lanes] + 0.25 * center
            ) + (0.25 * TIME_STEP) * rate

        rho_here, rho_d = derive(0, False)
        heat_here, heat_d = derive(4, True)
        ratio = [heat_here[t] / rho_here[t] for t in range(tiles)]
        press, rho_rate, heat_rate = [], [], []
        for t in range(tiles):
            (a, b, c, _), (d, e, g, bend) = rho_d[t], heat_d[t]
            press.append(
                (
                    0.5 * (ratio[t] * a + d),
                    lat_scale * (ratio[t] * b + e),
                    lon_scale * (ratio[t] * c + g),
                )
            )
            rho_rate.append(go_rad[t] * a + go_lat[t] * b + go_lon[t] * c)
            heat_rate.append(
                bend
                + (radial_extra - go_rad[t]) * d
                + (slope_extra - go_lat[t]) * e
                - go_lon[t] * g
            )
        diverge = [two_r * wind_rad[t] + cot_r * wind_lat[t] for t in range(tiles)]
        for f in (1, 2, 3):
            here, d_all = derive(f, True)
            for t in range(tiles):
                d, e, g, bend = d_all[t]
                spin_rad, spin_lat = spin_box[0, t, strip], spin_box[1, t, strip]
                spin_lon = spin_box[2, t, strip]
                rate = (
                    bend
                    + (radial_extra - go_rad[t]) * d
                    + (slope_extra - go_lat[t]) * e
                    - go_lon[t] * g
                    - press[t][f - 1]
                )
                if f == 1:
                    diverge[t] += 0.5 * d
                    rate += inv_radius * (wind_lat[t] * wind_lat[t] + wind_lon[t] * wind_lon[t])
                    rate += spin_lon * wind_lat[t] - spin_lat * wind_lon[t] - GRAVITY
                elif f == 2:
                    diverge[t] += lat_scale * e
                    rate += cot_r * (wind_lon[t] * wind_lon[t])
                    rate -= inv_radius * (wind_rad[t] * wind_lat[t])
                    rate += spin_rad * wind_lon[t] - spin_lon * wind_rad[t]
                else:
                    diverge[t] += lon_scale * g
                    rate -= (inv_radius * wind_rad[t] + cot_r * wind_lat[t]) * wind_lon[t]
                    rate += spin_lat * wind_rad[t] - spin_rad * wind_lat[t]
                put(f, t, here[t], rate)
        for t in range(tiles):
            put(0, t, rho_here[t], -rho_rate[t] - rho_here[t] * diverge[t])
            put(
                4,
                t,
                heat_here[t],
                heat_rate[t] - (GAMMA - 1.0) * (heat_here[t] * diverge[t]),
            )

    for c in range(chunks):
        if c + 1 < chunks:
            for copy in load_copies(c + 1):
                copy.wait()
        for copy in start_copies(c):
            copy.wait()

        @pl.loop(c * chunk, (c + 1) * chunk)
        def _(k):
            one_level(k)

        for copy in out_copies(c):
            copy.start()
    for c in range(chunks):
        for copy in out_copies(c):
            copy.wait()


def stencil(
    groups, partners, turn_lat, turn_lon, replies, halos, sides, rho, flow, heat, outset, prior=None
):
    levels, rows, cols = rho.shape[1:]
    n_panel, n_lat, n_lon = (lax.axis_size(x) for x in ("panel", "lat", "lon"))
    tiles = cols // LANES
    chunk = 4
    chunks = levels // chunk
    out = jax.ShapeDtypeStruct(outset.shape, jnp.float32)
    prior = tuple(prior or ())
    box = pltpu.VMEM((5, levels, rows, cols), jnp.float32)
    share = sum(count for _, count in groups) / rows
    n_in = 3 + n_lat + 8
    return pl.pallas_call(
        functools.partial(
            stencil_kernel, (n_panel, n_lat, n_lon, levels, rows, cols), groups, chunk, bool(prior)
        ),
        out_shape=(out, out),
        in_specs=[SMEM, VMEM, VMEM] + [ANY] * (n_in - 3 + len(prior)),
        out_specs=(ANY, ANY),
        input_output_aliases={n_in: 0, n_in + 1: 1} if prior else {},
        scratch_shapes=[
            pltpu.VMEM((5, tiles, levels, rows + 2 * SUB, LANES), jnp.float32),
            box,
            box,
            box,
            pltpu.VMEM((n_lat,) + replies[0].shape, jnp.float32),
            pltpu.VMEM((2, 2, 5, tiles, levels, LANES), jnp.float32),
            pltpu.VMEM((4, 2, rows, LANES), jnp.float32),
            pltpu.VMEM((4, rows, LANES), jnp.float32),
            pltpu.VMEM((2, rows, LANES), jnp.float32),
            pltpu.VMEM((3, tiles, rows, LANES), jnp.float32),
            pltpu.SemaphoreType.DMA((chunks, tiles, 3)),
            pltpu.SemaphoreType.DMA((chunks, len(groups))),
            pltpu.SemaphoreType.DMA((chunks, len(groups), 2)),
            pltpu.SemaphoreType.DMA((n_lat + 4,)),
        ],
        compiler_params=pltpu.CompilerParams(vmem_limit_bytes=40 * 1024 * 1024),
        cost_estimate=pl.CostEstimate(
            flops=int(250 * share * levels * rows * cols),
            bytes_accessed=int(16 * share * levels * rows * cols * 5),
            transcendentals=0,
        ),
        name="stencil",
    )(
        partners,
        turn_lat,
        turn_lon,
        *replies,
        *halos,
        *sides,
        rho,
        flow,
        heat,
        outset,
        *prior,
    )


def shards(rho, flow, heat, outset, opposite_block, donor_lower_corner, blend, turning):
    levels, rows, cols = rho.shape[1:]
    n_lat, n_lon = lax.axis_size("lat"), lax.axis_size("lon")
    lat_here, lon_here = lax.axis_index("lat"), lax.axis_index("lon")
    slots = opposite_block.shape[-1]
    lat_len, lon_len = 2 * cols, 2 * rows
    partners = opposite_block.reshape(1, slots)
    meta = jnp.concatenate(
        [
            partners.astype(jnp.float32),
            donor_lower_corner.reshape(1, slots).astype(jnp.float32),
            blend.reshape(4, slots),
        ],
        axis=0,
    )
    request = jnp.concatenate(
        [
            jnp.where(lat_here == 0, meta[:, 0:lat_len], meta[:, lat_len : 2 * lat_len]),
            jnp.where(
                lon_here == 0,
                meta[:, 2 * lat_len : 2 * lat_len + lon_len],
                meta[:, 2 * lat_len + lon_len :],
            ),
        ],
        axis=1,
    )
    requests = [swap_panels(request, d) for d in range(n_lat)]
    even_rows, odd_rows = edge_rows(rho, flow, heat)
    halos = (swap_pairs(even_rows, "lat", False), swap_pairs(odd_rows, "lat", True))
    cells, even_cols, odd_cols = cell_major(rho, flow, heat)
    sides = (swap_pairs(even_cols, "lon", False), swap_pairs(odd_cols, "lon", True))
    replies = donate(requests, cells, rows, cols, 5 * levels)
    replies = [swap_panels(reply, d) for d, reply in enumerate(replies)]
    turn = turning.reshape(2, slots)
    turn_lon = turn[:, 2 * lat_len :].T
    return stencil(
        ((0, rows),), partners, turn, turn_lon, replies, halos, sides, rho, flow, heat, outset
    )


def solution(mesh):
    in_specs = (
        P("panel", None, "lat", "lon"),
        P("panel", None, None, "lat", "lon"),
        P("panel", None, "lat", "lon"),
        P("panel", None, None, "lat", "lon"),
        P("panel", "lat", "lon", None),
        P("panel", "lat", "lon", None),
        P("panel", "lat", "lon", None, None),
        P("panel", "lat", "lon", None, None),
    )
    out_specs = (P("panel", None, None, "lat", "lon"), P("panel", None, None, "lat", "lon"))
    return jax.shard_map(shards, mesh=mesh, in_specs=in_specs, out_specs=out_specs, check_vma=False)
```

profile of v0, /device:TPU:1, one launch (start us, length us, event | category | flops | bytes accessed | tf_op | source)
XLA Modules:
  0.0 76.2 jit_solution(17041022514355411871)
XLA Ops:
  0.6 0.7 convert_bitcast_fusion
  1.4 0.8 %pad_maximum_fusion = f32[6,1664]{1,0:T(8,128)S(1)} fusion(f32[4,1664]{1,0:T(4,128)} %bitcast.11, f32[1,1664]{1,0:T(1,128)S(1)} %get-tuple-element.20, f32[1,1664]{1,0:T(1,128)S(1)} %get-tuple-element.21), kind=kLoop, calls=%fused_computation.1 | loop fusion | flops 19968 | bytes 79872 | tf_op jit(solution)/shard_map/concatenate | solution.py:670
  2.1 0.8 %maximum_select_fusion = f32[6,64]{1,0:T(8,128)S(1)} fusion(f32[4,1664]{1,0:T(4,128)} %bitcast.12, f32[1,1664]{1,0:T(1,128)S(1)} %get-tuple-element.20, f32[1,1664]{1,0:T(1,128)S(1)} %get-tuple-element.21, pred[]{:T(512)S(6)} %eq.7), kind=kLoop, calls=%fused_computation.5 | loop fusion | flops 1920 | bytes 41473 | tf_op jit(solution)/shard_map/jit(_where)/select_n | solution.py:681
  3.0 3.6 %collective-permute-start.3 = (f32[6,832]{1,0:T(8,128)S(1)}, f32[6,832]{1,0:T(8,128)S(1)}, u32[]{:S(2)}, u32[]{:S(2)}) collective-permute-start(f32[6,832]{1,0:T(8,128)S(1)} %pad_maximum_fusion.1), channel_id=1, source_target_pairs={{0,28},{4,24},{8,20},{12,16},{16,12},{20,8},{24,4},{28,0},{1,29},{... | collective-permute-start | bytes 59912 | tf_op jit(solution)/shard_map/ppermute | solution.py:40
  6.6 0.1 collective-permute-start.1
  6.7 0.7 collective-permute-start
  7.4 6.1 %cell_major.1 = (f32[12288,128]{1,0:T(8,128)}, f32[2,32,128]{2,1,0:T(8,128)}, f32[2,32,128]{2,1,0:T(8,128)}) custom-call(f32[1,16,32,384]{3,2,1,0:T(8,128)} %refs_11_.1, f32[1,3,16,32,384]{4,3,2,1,0:T(8,128)} %refs_12_.1, f32[1,16,32,384]{3,2,1,0:T(8,128)} %refs_13_.1), custom_call_target="tpu_custom_call" | custom-call | tf_op jit(solution)/shard_map/cell_major/pallas_call | solution.py:126
  13.5 0.5 copy-done.10
  14.1 7.3 %donate.1 = (f32[96,256]{1,0:T(8,128)}, f32[96,256]{1,0:T(8,128)}, f32[96,256]{1,0:T(8,128)}, f32[96,256]{1,0:T(8,128)}) custom-call(f32[6,832]{1,0:T(8,128)} %copy-done.13, f32[6,832]{1,0:T(8,128)} %copy-done.12, f32[6,832]{1,0:T(8,128)} %copy-done.11, f32[6,832]{1,0:T(8,128)} %copy-done.10, f32[12288,128]{1,0:T(8,128)} %get-tuple-element.11.refs_4_), custom_call_target="tpu_custom_call" | custom-call | tf_op jit(solution)/shard_map/donate/pallas_call | solution.py:209
  21.5 0.1 collective-permute-start.4
  21.5 1.3 %collective-permute-start.10 = (f32[2,32,128]{2,1,0:T(8,128)}, f32[2,32,128]{2,1,0:T(8,128)S(1)}, u32[]{:S(2)}, u32[]{:S(2)}) collective-permute-start(f32[2,32,128]{2,1,0:T(8,128)} %get-tuple-element.18), channel_id=1, source_target_pairs={{0,1},{1,0},{2,3},{3,2},{4,5},{5,4},{6,7},{7,6},{8,9},{9,8},{10,11... | collective-permute-start | bytes 98312 | tf_op jit(solution)/shard_map/ppermute | solution.py:32
  22.8 2.6 %collective-permute-start.11 = (f32[2,32,128]{2,1,0:T(8,128)}, f32[2,32,128]{2,1,0:T(8,128)S(1)}, u32[]{:S(2)}, u32[]{:S(2)}) collective-permute-start(f32[2,32,128]{2,1,0:T(8,128)} %get-tuple-element.19), channel_id=1, source_target_pairs={{0,3},{1,2},{2,1},{3,0},{4,7},{5,6},{6,5},{7,4},{8,11},{9,10},{10,... | collective-permute-start | bytes 98312 | tf_op jit(solution)/shard_map/ppermute | solution.py:32
  25.4 2.6 %edge_rows.1 = (f32[2,5,3,16,128]{4,3,2,1,0:T(8,128)}, f32[2,5,3,16,128]{4,3,2,1,0:T(8,128)}) custom-call(f32[1,16,32,384]{3,2,1,0:T(8,128)} %refs_11_.1, f32[1,3,16,32,384]{4,3,2,1,0:T(8,128)} %refs_12_.1, f32[1,16,32,384]{3,2,1,0:T(8,128)} %refs_13_.1), custom_call_target="tpu_custom_call" | custom-call | tf_op jit(solution)/shard_map/edge_rows/pallas_call | solution.py:83
  27.9 1.3 %collective-permute-start.8 = (f32[2,5,3,16,128]{4,3,2,1,0:T(8,128)}, f32[2,5,3,16,128]{4,3,2,1,0:T(8,128)S(1)}, u32[]{:S(2)}, u32[]{:S(2)}) collective-permute-start(f32[2,5,3,16,128]{4,3,2,1,0:T(8,128)} %get-tuple-element.16), channel_id=1, source_target_pairs={{0,4},{4,0},{8,12},{12,8},{1,5},{5,1},{9,13},{13,9},{2,6},{6,2},{1... | collective-permute-start | bytes 737288 | tf_op jit(solution)/shard_map/ppermute | solution.py:32
  29.2 1.2 %collective-permute-start.9 = (f32[2,5,3,16,128]{4,3,2,1,0:T(8,128)}, f32[2,5,3,16,128]{4,3,2,1,0:T(8,128)}, u32[]{:S(2)}, u32[]{:S(2)}) collective-permute-start(f32[2,5,3,16,128]{4,3,2,1,0:T(8,128)} %get-tuple-element.17), channel_id=1, source_target_pairs={{0,12},{4,8},{8,4},{12,0},{1,13},{5,9},{9,5},{13,1},{2,14},{6,10},... | collective-permute-start | bytes 737288 | tf_op jit(solution)/shard_map/ppermute | solution.py:32
  30.4 1.9 %copy.10 = f32[1,1,1,2,1664]{3,4,2,1,0:T(8,128)} copy(f32[1,1,1,2,1664]{4,3,2,1,0:T(2,128)} %param.15) | data formatting | bytes 26624 | tf_op args[7]
  32.4 0.6 copy-done.5
  33.0 2.1 %collective-permute-start.5 = (f32[96,256]{1,0:T(8,128)}, f32[96,256]{1,0:T(8,128)}, u32[]{:S(2)}, u32[]{:S(2)}) collective-permute-start(f32[96,256]{1,0:T(8,128)} %get-tuple-element.13), channel_id=1, source_target_pairs={{0,20},{4,16},{8,28},{12,24},{16,4},{20,0},{24,12},{28,8},{1,21},{... | collective-permute-start | bytes 294920 | tf_op jit(solution)/shard_map/ppermute | solution.py:40
  35.1 0.6 copy-done.7
  35.7 1.7 %collective-permute-start.7 = (f32[96,256]{1,0:T(8,128)}, f32[96,256]{1,0:T(8,128)}, u32[]{:S(2)}, u32[]{:S(2)}) collective-permute-start(f32[96,256]{1,0:T(8,128)} %get-tuple-element.15), channel_id=1, source_target_pairs={{0,28},{4,24},{8,20},{12,16},{16,12},{20,8},{24,4},{28,0},{1,29},{... | collective-permute-start | bytes 294920 | tf_op jit(solution)/shard_map/ppermute | solution.py:40
  37.4 0.8 %slice_bitcast_fusion.refs_2_ = f32[128,2]{1,0:T(8,128)S(1)} fusion(f32[2,1664]{0,1:T(8,128)} %bitcast.9), kind=kLoop, calls=%fused_computation | loop fusion | bytes 2048 | tf_op jit(solution)/shard_map/transpose | solution.py:697
  38.3 2.0 %copy.11.refs_1_ = f32[2,1664]{1,0:T(2,128)} copy(f32[2,1664]{0,1:T(8,128)} %bitcast.10) | data formatting | bytes 26624 | tf_op jit(solution)/shard_map/reshape | solution.py:696
  40.3 4.3 %collective-permute-done.5.refs_4_ = f32[96,256]{1,0:T(8,128)} collective-permute-done((f32[96,256]{1,0:T(8,128)}, f32[96,256]{1,0:T(8,128)}, u32[]{:S(2)}, u32[]{:S(2)}) %collective-permute-start.5) | collective-permute-done | bytes 98336 | tf_op jit(solution)/shard_map/ppermute | solution.py:40
  44.6 0.8 %collective-permute-done.6.refs_5_ = f32[96,256]{1,0:T(8,128)} collective-permute-done((f32[96,256]{1,0:T(8,128)}, f32[96,256]{1,0:T(8,128)}, u32[]{:S(2)}, u32[]{:S(2)}) %collective-permute-start.6) | collective-permute-done | bytes 98336 | tf_op jit(solution)/shard_map/ppermute | solution.py:40
  45.4 1.1 %collective-permute-done.7.refs_6_ = f32[96,256]{1,0:T(8,128)} collective-permute-done((f32[96,256]{1,0:T(8,128)}, f32[96,256]{1,0:T(8,128)}, u32[]{:S(2)}, u32[]{:S(2)}) %collective-permute-start.7) | collective-permute-done | bytes 98336 | tf_op jit(solution)/shard_map/ppermute | solution.py:40
  46.5 1.1 %copy-done.2 = f32[1,16,32,384]{3,2,1,0:T(8,128)S(1)} copy-done((f32[1,16,32,384]{3,2,1,0:T(8,128)S(1)}, f32[1,16,32,384]{3,2,1,0:T(8,128)}, u32[]{:S(2)}) %copy-start.2) | copy-done | bytes 786456
  47.6 2.1 %copy-done.3 = f32[1,5,16,32,384]{4,3,2,1,0:T(8,128)S(1)} copy-done((f32[1,5,16,32,384]{4,3,2,1,0:T(8,128)S(1)}, f32[1,5,16,32,384]{4,3,2,1,0:T(8,128)}, u32[]{:S(2)}) %copy-start.3) | copy-done | bytes 3932184
  49.8 0.7 copy-done.4
  50.5 0.8 copy-done.6
  51.2 0.8 copy-done.8
  52.0 0.7 copy-done.9
  52.7 23.5 %stencil.1 = (f32[1,5,16,32,384]{4,3,2,1,0:T(8,128)}, f32[1,5,16,32,384]{4,3,2,1,0:T(8,128)}) custom-call(s32[1,1664]{1,0:T(1,128)S(1)} %bitcast.8, f32[2,1664]{1,0:T(2,128)S(1)} %copy-done.4, f32[128,2]{1,0:T(8,128)S(1)} %slice_bitcast_fusion.refs_2_, f32[96,256]{1,0:T(8,128)S(1)} %collective-permute-done.4.refs_3_, ...), custom_call_target="tpu_custom_call" | custom-call | flops 49152000 | bytes 15728640 | tf_op jit(solution)/shard_map/stencil/pallas_call | solution.py:617
  (32 shorter events, 0.1 us)
Async XLA Ops:
  3.0 10.5 %collective-permute-start.3 = (f32[6,832]{1,0:T(8,128)S(1)}, f32[6,832]{1,0:T(8,128)S(1)}, u32[]{:S(2)}, u32[]{:S(2)}) collective-permute-start(f32[6,832]{1,0:T(8,128)S(1)} %pad_maximum_fusion.1), channel_id=1, source_target_pairs={{0,28},{4,24},{8,20},{12,16},{16,12},{20,8},{24,4},{28,0},{1,29},{... | collective-permute-start | bytes 59912 | tf_op jit(solution)/shard_map/ppermute | solution.py:40
  6.6 6.9 %collective-permute-start.2 = (f32[6,832]{1,0:T(8,128)S(1)}, f32[6,832]{1,0:T(8,128)S(1)}, u32[]{:S(2)}, u32[]{:S(2)}) collective-permute-start(f32[6,832]{1,0:T(8,128)S(1)} %pad_maximum_fusion.1), channel_id=1, source_target_pairs={{0,24},{4,28},{8,16},{12,20},{16,8},{20,12},{24,0},{28,4},{1,25},{... | collective-permute-start | bytes 59912 | tf_op jit(solution)/shard_map/ppermute | solution.py:40
  6.6 6.9 %collective-permute-start.1 = (f32[6,832]{1,0:T(8,128)S(1)}, f32[6,832]{1,0:T(8,128)S(1)}, u32[]{:S(2)}, u32[]{:S(2)}) collective-permute-start(f32[6,832]{1,0:T(8,128)S(1)} %pad_maximum_fusion.1), channel_id=1, source_target_pairs={{0,20},{4,16},{8,28},{12,24},{16,4},{20,0},{24,12},{28,8},{1,21},{... | collective-permute-start | bytes 59912 | tf_op jit(solution)/shard_map/ppermute | solution.py:40
  6.7 6.8 %collective-permute-start = (f32[6,832]{1,0:T(8,128)S(1)}, f32[6,832]{1,0:T(8,128)S(1)}, u32[]{:S(2)}, u32[]{:S(2)}) collective-permute-start(f32[6,832]{1,0:T(8,128)S(1)} %pad_maximum_fusion.1), channel_id=1, source_target_pairs={{0,16},{4,20},{8,24},{12,28},{16,0},{20,4},{24,8},{28,12},{1,17},{... | collective-permute-start | bytes 59912 | tf_op jit(solution)/shard_map/ppermute | solution.py:40
  13.5 0.6 copy-start.10
  13.5 0.6 copy-start.11
  13.5 0.6 copy-start.12
  13.5 0.6 copy-start.13
  21.5 25.0 %copy-start = (f32[1,3,16,32,384]{4,3,2,1,0:T(8,128)S(1)}, f32[1,3,16,32,384]{4,3,2,1,0:T(8,128)}, u32[]{:S(2)}) copy-start(f32[1,3,16,32,384]{4,3,2,1,0:T(8,128)} %refs_12_.1) | copy-start | bytes 7077892
  21.5 25.0 %copy-start.1 = (f32[1,16,32,384]{3,2,1,0:T(8,128)S(1)}, f32[1,16,32,384]{3,2,1,0:T(8,128)}, u32[]{:S(2)}) copy-start(f32[1,16,32,384]{3,2,1,0:T(8,128)} %refs_11_.1) | copy-start | bytes 2359300
  21.5 14.2 %collective-permute-start.4 = (f32[96,256]{1,0:T(8,128)}, f32[96,256]{1,0:T(8,128)S(1)}, u32[]{:S(2)}, u32[]{:S(2)}) collective-permute-start(f32[96,256]{1,0:T(8,128)} %get-tuple-element.12), channel_id=1, source_target_pairs={{0,16},{4,20},{8,24},{12,28},{16,0},{20,4},{24,8},{28,12},{1,17},{... | collective-permute-start | bytes 294920 | tf_op jit(solution)/shard_map/ppermute | solution.py:40
  21.5 10.8 %collective-permute-start.10 = (f32[2,32,128]{2,1,0:T(8,128)}, f32[2,32,128]{2,1,0:T(8,128)S(1)}, u32[]{:S(2)}, u32[]{:S(2)}) collective-permute-start(f32[2,32,128]{2,1,0:T(8,128)} %get-tuple-element.18), channel_id=1, source_target_pairs={{0,1},{1,0},{2,3},{3,2},{4,5},{5,4},{6,7},{7,6},{8,9},{9,8},{10,11... | collective-permute-start | bytes 98312 | tf_op jit(solution)/shard_map/ppermute | solution.py:32
  22.8 12.3 %collective-permute-start.11 = (f32[2,32,128]{2,1,0:T(8,128)}, f32[2,32,128]{2,1,0:T(8,128)S(1)}, u32[]{:S(2)}, u32[]{:S(2)}) collective-permute-start(f32[2,32,128]{2,1,0:T(8,128)} %get-tuple-element.19), channel_id=1, source_target_pairs={{0,3},{1,2},{2,1},{3,0},{4,7},{5,6},{6,5},{7,4},{8,11},{9,10},{10,... | collective-permute-start | bytes 98312 | tf_op jit(solution)/shard_map/ppermute | solution.py:32
  27.9 18.5 %collective-permute-start.8 = (f32[2,5,3,16,128]{4,3,2,1,0:T(8,128)}, f32[2,5,3,16,128]{4,3,2,1,0:T(8,128)S(1)}, u32[]{:S(2)}, u32[]{:S(2)}) collective-permute-start(f32[2,5,3,16,128]{4,3,2,1,0:T(8,128)} %get-tuple-element.16), channel_id=1, source_target_pairs={{0,4},{4,0},{8,12},{12,8},{1,5},{5,1},{9,13},{13,9},{2,6},{6,2},{1... | collective-permute-start | bytes 737288 | tf_op jit(solution)/shard_map/ppermute | solution.py:32
  29.2 17.3 %collective-permute-start.9 = (f32[2,5,3,16,128]{4,3,2,1,0:T(8,128)}, f32[2,5,3,16,128]{4,3,2,1,0:T(8,128)}, u32[]{:S(2)}, u32[]{:S(2)}) collective-permute-start(f32[2,5,3,16,128]{4,3,2,1,0:T(8,128)} %get-tuple-element.17), channel_id=1, source_target_pairs={{0,12},{4,8},{8,4},{12,0},{1,13},{5,9},{9,5},{13,1},{2,14},{6,10},... | collective-permute-start | bytes 737288 | tf_op jit(solution)/shard_map/ppermute | solution.py:32
  32.4 0.6 copy-start.5
  33.0 11.6 %collective-permute-start.5 = (f32[96,256]{1,0:T(8,128)}, f32[96,256]{1,0:T(8,128)}, u32[]{:S(2)}, u32[]{:S(2)}) collective-permute-start(f32[96,256]{1,0:T(8,128)} %get-tuple-element.13), channel_id=1, source_target_pairs={{0,20},{4,16},{8,28},{12,24},{16,4},{20,0},{24,12},{28,8},{1,21},{... | collective-permute-start | bytes 294920 | tf_op jit(solution)/shard_map/ppermute | solution.py:40
  35.1 0.6 copy-start.7
  35.7 9.7 %collective-permute-start.6 = (f32[96,256]{1,0:T(8,128)}, f32[96,256]{1,0:T(8,128)}, u32[]{:S(2)}, u32[]{:S(2)}) collective-permute-start(f32[96,256]{1,0:T(8,128)} %get-tuple-element.14), channel_id=1, source_target_pairs={{0,24},{4,28},{8,16},{12,20},{16,8},{20,12},{24,0},{28,4},{1,25},{... | collective-permute-start | bytes 294920 | tf_op jit(solution)/shard_map/ppermute | solution.py:40
  35.7 10.8 %collective-permute-start.7 = (f32[96,256]{1,0:T(8,128)}, f32[96,256]{1,0:T(8,128)}, u32[]{:S(2)}, u32[]{:S(2)}) collective-permute-start(f32[96,256]{1,0:T(8,128)} %get-tuple-element.15), channel_id=1, source_target_pairs={{0,28},{4,24},{8,20},{12,16},{16,12},{20,8},{24,4},{28,0},{1,29},{... | collective-permute-start | bytes 294920 | tf_op jit(solution)/shard_map/ppermute | solution.py:40
  46.5 1.1 %copy-start.2 = (f32[1,16,32,384]{3,2,1,0:T(8,128)S(1)}, f32[1,16,32,384]{3,2,1,0:T(8,128)}, u32[]{:S(2)}) copy-start(f32[1,16,32,384]{3,2,1,0:T(8,128)} %refs_13_.1) | copy-start | bytes 2359300
  47.6 2.1 %copy-start.3 = (f32[1,5,16,32,384]{4,3,2,1,0:T(8,128)S(1)}, f32[1,5,16,32,384]{4,3,2,1,0:T(8,128)}, u32[]{:S(2)}) copy-start(f32[1,5,16,32,384]{4,3,2,1,0:T(8,128)} %refs_14_.1) | copy-start | bytes 11796484
  49.8 0.7 copy-start.4
  50.5 0.8 copy-start.6
  51.2 0.8 copy-start.8
  52.0 0.7 copy-start.9
where the time goes:
time: 77.1 us; the launch traced here: 76.2 us
  Pallas kernels  39.5 us (51%)
  starting transfers between devices  14.6 us (19%)
  local copies, waits for them, and re-layouts  12.8 us (17%)
  waiting for transfers between devices  6.22 us (8%)
  other arithmetic  2.34 us (3%)
    pallas_call x1, Pallas kernels, stencil(): pl.pallas_call(functools.partial(stencil_kernel, (n_panel, n_lat, n_lon,...  23.5 us
    unnamed x29, local copies, waits for them, and re-layouts  9.91 us
    ppermute x8, starting transfers between devices, swap_panels(): return lax.ppermute(value, ('panel', 'lat'), pairs)  8.26 us
    pallas_call x1, Pallas kernels, donate(): pl.pallas_call(functools.partial(donate_kernel, n_lat, n_lon, rows, cols,...  7.33 us
    ppermute x4, starting transfers between devices, swap_pairs(): lax.ppermute(value, axis, [(i, pair_partner(i, count, odd)) for i in rang...  6.31 us
    ppermute x8, waiting for transfers between devices, swap_panels(): return lax.ppermute(value, ('panel', 'lat'), pairs)  6.21 us
    pallas_call x1, Pallas kernels, cell_major(): pl.pallas_call(cell_major_kernel, grid=(rows // SUB,), out_shape=(jax.Sha...  6.09 us
    pallas_call x1, Pallas kernels, edge_rows(): pl.pallas_call(edge_rows_kernel, out_shape=(shape, shape), in_specs=[ANY]...  2.58 us
  transfers between devices with their start and end apart: 12, of which 3 were waited for; matrix products, arithmetic and copies ran while one was open for 6% of the time, Pallas kernels for 11%

commit v1 on v0

v1 whole, which is shorter than its diff:
```python
import functools
import math

import jax
import jax.numpy as jnp
from jax import lax
from jax.experimental import pallas as pl
from jax.experimental.pallas import tpu as pltpu
from jax.sharding import PartitionSpec as P

OMEGA = 0.5
GRAVITY = 1.0
VISCOSITY = 0.2
DIFFUSIVITY = 0.2
GAMMA = 1.4
TIME_STEP = 0.05
LANES = 128
SUB = 8
MIB = 1024 * 1024
ANY = pl.BlockSpec(memory_space=pl.ANY)
HBM = pl.BlockSpec(memory_space=pltpu.HBM)
VMEM = pl.BlockSpec(memory_space=pltpu.VMEM)
SMEM = pl.BlockSpec(memory_space=pltpu.SMEM)


def in_hbm(value):
    return pltpu.with_memory_space_constraint(value, pltpu.HBM)


def pair_partner(i, count, odd):
    if not odd:
        return i ^ 1
    return (i + 1) % count if i % 2 else (i - 1) % count


def swap_pairs(value, axis, odd):
    count = lax.axis_size(axis)
    return lax.ppermute(value, axis, [(i, pair_partner(i, count, odd)) for i in range(count)])


def swap_panels(value, distance):
    n_lat = lax.axis_size("lat")
    pairs = [
        (p * n_lat + a, (1 - p) * n_lat + (a ^ distance)) for p in range(2) for a in range(n_lat)
    ]
    return lax.ppermute(value, ("panel", "lat"), pairs)


def window_of(run, cols):
    tiles = cols // LANES
    for width in range(1, tiles + 1):
        if all(
            start - min(start // LANES, tiles - width) * LANES + run <= width * LANES
            for start in range(0, cols, run)
        ):
            return width
    return tiles


def ask_kernel(partners, corners, blend, request, partners_box, corners_box, blend_box, sems):
    lat_len = corners.shape[-1] - request.shape[-1]
    copies = [
        pltpu.make_async_copy(partners, partners_box, sems.at[0]),
        pltpu.make_async_copy(corners, corners_box, sems.at[1]),
        pltpu.make_async_copy(blend, blend_box, sems.at[2]),
    ]
    for copy in copies:
        copy.start()
    for copy in copies:
        copy.wait()
    north = lax.axis_index("lat") == 0
    for row, source in ((0, partners_box), (1, corners_box)):
        values = source[0, 0].astype(jnp.float32)
        request[row : row + 1, 0:lat_len] = jnp.where(
            north, values[:, 0:lat_len], values[:, lat_len : 2 * lat_len]
        )
        request[row : row + 1, lat_len:] = values[:, 2 * lat_len :]
    weights = blend_box[0, 0, 0]
    request[2:6, 0:lat_len] = jnp.where(
        north, weights[:, 0:lat_len], weights[:, lat_len : 2 * lat_len]
    )
    request[2:6, lat_len:] = weights[:, 2 * lat_len :]


def ask(partners, corners, blend, rows, cols):
    return pl.pallas_call(
        ask_kernel,
        out_shape=jax.ShapeDtypeStruct((SUB, 2 * cols + 4 * rows), jnp.float32),
        in_specs=[HBM] * 3,
        out_specs=VMEM,
        scratch_shapes=[
            pltpu.VMEM(partners.shape, jnp.int32),
            pltpu.VMEM(corners.shape, jnp.int32),
            pltpu.VMEM(blend.shape, jnp.float32),
            pltpu.SemaphoreType.DMA((3,)),
        ],
        compiler_params=pltpu.CompilerParams(vmem_limit_bytes=MIB),
        name="ask",
    )(*(in_hbm(x) for x in (partners, corners, blend)))


def prepare_kernel(
    n_lat,
    n_lon,
    rows,
    rho,
    flow,
    heat,
    cells,
    block,
    even_rows,
    odd_rows,
    even_cols,
    odd_cols,
    row_box,
    spin_box,
):
    levels = rho.shape[1]
    cols = rho.shape[3]
    tiles = cols // LANES
    step = pl.program_id(0)

    def field_tile(field, row, tile):
        lanes = slice(tile * LANES, (tile + 1) * LANES)
        if field == 0:
            return rho[0, :, row, lanes]
        if field == 4:
            return heat[0, :, row, lanes]
        return flow[0, field - 1, :, row, lanes]

    for tile in range(tiles):
        lanes = slice(tile * LANES, (tile + 1) * LANES)
        block[0, tile] = rho[0, :, :, lanes]
        for part in range(3):
            block[1 + part, tile] = flow[0, part, :, :, lanes]
        block[4, tile] = heat[0, :, :, lanes]

    step_lat = math.pi / 2.0 / (rows * n_lat)
    step_lon = 1.5 * math.pi / (cols * n_lon)
    sub = lax.broadcasted_iota(jnp.int32, (SUB, LANES), 0)
    row_global = (lax.axis_index("lat") * rows + step * SUB + sub).astype(jnp.float32)
    theta = math.pi / 4.0 + (row_global + 0.5) * step_lat
    sin_lat, cos_lat = jnp.sin(theta), jnp.cos(theta)
    row_box[0] = 1.0 / sin_lat
    row_box[1] = cos_lat / sin_lat
    yang = lax.axis_index("panel").astype(jnp.float32)
    yin = 1.0 - yang
    for tile in range(tiles):
        lane = lax.broadcasted_iota(jnp.int32, (SUB, LANES), 1) + tile * LANES
        col_global = (lax.axis_index("lon") * cols + lane).astype(jnp.float32)
        longitude = -0.75 * math.pi + (col_global + 0.5) * step_lon
        sin_lon, cos_lon = jnp.sin(longitude), jnp.cos(longitude)
        spin_box[0, tile] = 2.0 * OMEGA * (yin * cos_lat + yang * sin_lat * sin_lon)
        spin_box[1, tile] = 2.0 * OMEGA * (yang * cos_lat * sin_lon - yin * sin_lat)
        spin_box[2, tile] = 2.0 * OMEGA * yang * cos_lon

    lat_even = lax.rem(lax.axis_index("lat"), 2) == 0
    for first, at, to_even in (
        (0, 0, jnp.logical_not(lat_even)),
        (SUB - 2, pl.num_programs(0) - 1, lat_even),
    ):
        for keep, out in ((to_even, even_rows), (jnp.logical_not(to_even), odd_rows)):

            @pl.when((step == at) & keep)
            def _(first=first, out=out):
                for layer in range(2):
                    for field in range(5):
                        for tile in range(tiles):
                            out[layer, field, tile] = field_tile(field, first + layer, tile)

    for row in range(SUB):
        for tile in range(tiles):
            stack = jnp.concatenate([field_tile(f, row, tile) for f in range(5)], axis=0)
            at = row * cols + tile * LANES
            cells[at : at + LANES, 0 : 5 * levels] = stack.T
    lon_even = lax.rem(lax.axis_index("lon"), 2) == 0
    for row in range(SUB):
        for layer in range(2):
            at = row * cols + layer
            west = cells[at : at + 1, :]
            at = row * cols + cols - 2 + layer
            east = cells[at : at + 1, :]
            even_cols[layer, row : row + 1, :] = jnp.where(lon_even, east, west)
            odd_cols[layer, row : row + 1, :] = jnp.where(lon_even, west, east)


def prepare(rho, flow, heat):
    levels, rows, cols = rho.shape[1:]
    column = jax.ShapeDtypeStruct((2, rows, LANES), jnp.float32)
    column_spec = pl.BlockSpec((2, SUB, LANES), lambda i: (0, i, 0))
    tiles = cols // LANES
    edge = jax.ShapeDtypeStruct((2, 5, tiles, levels, LANES), jnp.float32)
    edge_spec = pl.BlockSpec(edge.shape, lambda i: (0, 0, 0, 0, 0))
    return pl.pallas_call(
        functools.partial(
            prepare_kernel, lax.axis_size("lat"), lax.axis_size("lon"), rows
        ),
        grid=(rows // SUB,),
        out_shape=(
            jax.ShapeDtypeStruct((rows * cols, LANES), jnp.float32),
            jax.ShapeDtypeStruct((5, tiles, levels, rows + 2 * SUB, LANES), jnp.float32),
            edge,
            edge,
            column,
            column,
            jax.ShapeDtypeStruct((2, rows, LANES), jnp.float32),
            jax.ShapeDtypeStruct((3, tiles, rows, LANES), jnp.float32),
        ),
        in_specs=[
            pl.BlockSpec((1, levels, SUB, cols), lambda i: (0, 0, i, 0)),
            pl.BlockSpec((1, 3, levels, SUB, cols), lambda i: (0, 0, 0, i, 0)),
            pl.BlockSpec((1, levels, SUB, cols), lambda i: (0, 0, i, 0)),
        ],
        out_specs=(
            pl.BlockSpec((SUB * cols, LANES), lambda i: (i, 0)),
            pl.BlockSpec((5, tiles, levels, SUB, LANES), lambda i: (0, 0, 0, i + 1, 0)),
            edge_spec,
            edge_spec,
            column_spec,
            column_spec,
            pl.BlockSpec((2, SUB, LANES), lambda i: (0, i, 0)),
            pl.BlockSpec((3, tiles, SUB, LANES), lambda i: (0, 0, i, 0)),
        ),
        compiler_params=pltpu.CompilerParams(vmem_limit_bytes=12 * MIB),
        name="prepare",
    )(*(in_hbm(x) for x in (rho, flow, heat)))


def donate_kernel(n_lat, n_lon, rows, cols, field_rows, *refs):
    weights = refs[:n_lat]
    cells = refs[n_lat]
    replies = refs[n_lat + 1 : 2 * n_lat + 1]
    corners, turned, gathered, whole_box, requests, sems = refs[2 * n_lat + 1 :]
    copies = []
    for distance in range(n_lat):
        whole_box[distance] = weights[distance][...].astype(jnp.int32)
        copies.append(
            pltpu.make_async_copy(
                whole_box.at[distance], requests.at[distance], sems.at[distance]
            )
        )
        copies[-1].start()
    for copy in copies:
        copy.wait()
    lat_len, lon_len = 2 * cols, 2 * rows
    run_lat, run_lon = lat_len // n_lat, lon_len // n_lat
    tiles = cols // LANES
    width = window_of(run_lat, cols)
    lat_here = lax.axis_index("lat")
    lon_here = lax.axis_index("lon")

    def find_run(request, start, run):
        found = jnp.int32(0)
        for r in range(1, n_lat):
            match = requests[request, 0, start + r * run] == lat_here
            found = jnp.where(match, jnp.int32(r), found)
        return found

    def gather(request, first, count):
        def step(i, carry):
            for u in range(SUB):
                t = i * SUB + u
                cell = requests[request, 1, first + t]
                for j, shift in enumerate((0, cols, 1, cols + 1)):
                    corners[j, pl.ds(t, 1), :] = cells[pl.ds(cell + shift, 1), :]
            return carry

        lax.fori_loop(0, count // SUB, step, 0)

    def blend(first, count):
        rows_here = pl.ds(pl.multiple_of(first, SUB), count)
        total = None
        for j in range(4):
            weight = jnp.broadcast_to(turned[rows_here, 2 + j : 3 + j], (count, LANES))
            part = weight * corners[j, 0:count, :]
            total = part if total is None else total + part
        return total

    for distance in range(n_lat):
        request, reply = distance, replies[distance]
        asker = jnp.bitwise_xor(lat_here, distance)

        @pl.when((asker == 0) | (asker == n_lat - 1))
        def _(distance=distance, request=request, reply=reply):
            for at in range(0, lat_len, LANES):
                turned[at : at + LANES, 0:SUB] = weights[distance][:, at : at + LANES].T
            run = find_run(request, 0, run_lat)
            start = lax.rem(run * run_lat, cols)
            base = jnp.minimum(lax.div(start, LANES), tiles - width)
            offset = pl.multiple_of(start - base * LANES, SUB)
            gather(request, run * run_lat, run_lat)
            gathered[pl.ds(offset, run_lat), :] = blend(run * run_lat, run_lat)
            for tile in range(width):
                block = gathered[tile * LANES : (tile + 1) * LANES, :]
                reply[0:field_rows, tile * LANES : (tile + 1) * LANES] = block.T[0:field_rows]

        @pl.when((lon_here == 0) | (lon_here == n_lon - 1))
        def _(distance=distance, request=request, reply=reply):
            for at in range(lat_len, lat_len + 2 * lon_len, LANES):
                turned[at : at + LANES, 0:SUB] = weights[distance][:, at : at + LANES].T
            first = lat_len + jnp.where(lon_here == 0, 0, lon_len)
            run = find_run(request, first, run_lon)
            gather(request, first + run * run_lon, run_lon)
            reply[field_rows : field_rows + run_lon, 0:LANES] = blend(
                first + run * run_lon, run_lon
            )


def donate(requests, cells, rows, cols, field_rows):
    n_lat, n_lon = lax.axis_size("lat"), lax.axis_size("lon")
    run_lat = 2 * cols // n_lat
    width = window_of(run_lat, cols)
    reply = jax.ShapeDtypeStruct((field_rows + 2 * rows // n_lat, width * LANES), jnp.float32)
    return pl.pallas_call(
        functools.partial(donate_kernel, n_lat, n_lon, rows, cols, field_rows),
        out_shape=(reply,) * n_lat,
        in_specs=[VMEM] * (n_lat + 1),
        out_specs=(VMEM,) * n_lat,
        scratch_shapes=[
            pltpu.VMEM((4, max(run_lat, 2 * rows // n_lat), LANES), jnp.float32),
            pltpu.VMEM((requests[0].shape[1], LANES), jnp.float32),
            pltpu.VMEM((width * LANES, LANES), jnp.float32),
            pltpu.VMEM((n_lat,) + requests[0].shape, jnp.int32),
            pltpu.SMEM((n_lat,) + requests[0].shape, jnp.int32),
            pltpu.SemaphoreType.DMA((n_lat,)),
        ],
        compiler_params=pltpu.CompilerParams(vmem_limit_bytes=9 * MIB),
        name="donate",
    )(*requests, cells)


def stencil_kernel(geometry, chunk, *refs):
    n_lat, n_lon, levels, rows, cols = geometry
    tiles = cols // LANES
    field_rows = 5 * levels
    partners, turning = refs[:2]
    reply_box = refs[2 : 2 + n_lat]
    (
        lon_even,
        lon_odd,
        lat_even,
        lat_odd,
        block,
        row_box,
        spin_box,
        outset,
        rate_out,
        state_out,
        rate_box,
        state_box,
        replies,
        halo,
        side,
        mixed,
        out_sems,
    ) = refs[2 + n_lat :]
    lat_here = lax.axis_index("lat")
    lon_here = lax.axis_index("lon")
    lat_len, lon_len = 2 * cols, 2 * rows
    run_lat, run_lon = lat_len // n_lat, lon_len // n_lat
    width = window_of(run_lat, cols)
    step_lat = math.pi / 2.0 / (rows * n_lat)
    step_lon = 1.5 * math.pi / (cols * n_lon)
    chunks = levels // chunk
    groups = ((0, rows),)

    def out_copies(c):
        span = pl.ds(c * chunk, chunk)
        return (
            pltpu.make_async_copy(
                rate_box.at[:, span], rate_out.at[0, :, span], out_sems.at[c, 0]
            ),
            pltpu.make_async_copy(
                state_box.at[:, span], state_out.at[0, :, span], out_sems.at[c, 1]
            ),
        )

    lat_is_even = lax.rem(lat_here, 2) == 0
    lon_is_even = lax.rem(lon_here, 2) == 0
    for even, north, south in ((True, lat_odd, lat_even), (False, lat_even, lat_odd)):

        @pl.when(lat_is_even == even)
        def _(north=north, south=south):
            halo[0] = north[...]
            halo[1] = south[...]

    for even, west, east in ((True, lon_odd, lon_even), (False, lon_even, lon_odd)):

        @pl.when(lon_is_even == even)
        def _(west=west, east=east):
            side[0] = west[...]
            side[1] = east[...]

    @pl.when((lat_here == 0) | (lat_here == n_lat - 1) | (lon_here == 0) | (lon_here == n_lon - 1))
    def _():
        for d in range(n_lat):
            replies[d] = reply_box[d][...]

    lane8 = lax.broadcasted_iota(jnp.int32, (SUB, LANES), 1)
    sub8 = lax.broadcasted_iota(jnp.int32, (SUB, LANES), 0)

    for which, slot0 in ((0, 0), (1, lat_len)):

        @pl.when(lat_here == (0 if which == 0 else n_lat - 1))
        def _(which=which, slot0=slot0):
            sources = [
                jnp.bitwise_xor(partners[0, 0, 0, slot0 + r * run_lat], lat_here) for r in range(n_lat)
            ]
            for layer in range(2):
                for t in range(tiles):
                    lane = lax.broadcasted_iota(jnp.int32, (field_rows, LANES), 1) + t * LANES
                    value = None
                    for r in range(n_lat):
                        first = r * run_lat - layer * cols
                        if first < 0 or first >= cols:
                            continue
                        if first >= (t + 1) * LANES or first + run_lat <= t * LANES:
                            continue
                        base = min(first // LANES, tiles - width)
                        here = (t - base) * LANES
                        piece = replies[sources[r], 0:field_rows, here : here + LANES]
                        value = piece if value is None else jnp.where(lane >= first, piece, value)
                    spot = slot0 + layer * cols + t * LANES
                    cosine = turning[0, 0, 0, 0:1, spot : spot + LANES]
                    sine = turning[0, 0, 0, 1:2, spot : spot + LANES]
                    parts = [value[f * levels : (f + 1) * levels] for f in range(5)]
                    parts[2], parts[3] = (
                        cosine * parts[2] + sine * parts[3],
                        cosine * parts[3] - sine * parts[2],
                    )
                    for f in range(5):
                        halo[which, layer, f, t] = parts[f]

    turn_lon = jnp.concatenate(
        [turning[0, 0, 0, :, 2 * lat_len :], jnp.zeros((SUB - 2, 2 * lon_len), jnp.float32)], axis=0
    ).T

    for which, slot0 in ((0, 2 * lat_len), (1, 2 * lat_len + lon_len)):
        @pl.when(lon_here == (0 if which == 0 else n_lon - 1))
        def _(which=which, slot0=slot0):
            lane = lax.broadcasted_iota(jnp.int32, (run_lon, LANES), 1)
            is_lat = (lane >= 2 * levels) & (lane < 3 * levels)
            is_lon = (lane >= 3 * levels) & (lane < 4 * levels)
            for r in range(n_lat):
                source = jnp.bitwise_xor(partners[0, 0, 0, slot0 + r * run_lon], lat_here)
                layer, first = r * run_lon // rows, r * run_lon % rows
                value = replies[source, field_rows : field_rows + run_lon, 0:LANES]
                slots = slice(which * lon_len + r * run_lon, which * lon_len + (r + 1) * run_lon)
                cosine = jnp.broadcast_to(turn_lon[slots, 0:1], (run_lon, LANES))
                sine = jnp.broadcast_to(turn_lon[slots, 1:2], (run_lon, LANES))
                later = pltpu.roll(value, LANES - levels, 1)
                earlier = pltpu.roll(value, levels, 1)
                value = jnp.where(
                    is_lat,
                    cosine * value + sine * later,
                    jnp.where(is_lon, cosine * value - sine * earlier, value),
                )
                side[which, layer, first : first + run_lon] = value

    lane_all = lax.broadcasted_iota(jnp.int32, (rows, LANES), 1)
    columns = [side[1, 0], side[1, 1], side[0, 0], side[0, 1]]
    columns = [columns[0]] + [pltpu.roll(columns[j], j, 1) for j in range(1, 4)]
    for q in range(4):
        pick = jnp.bitwise_and(lane_all - q, 3)
        value = columns[0]
        for j in range(1, 4):
            value = jnp.where(pick == j, columns[j], value)
        for first, count in groups:
            span = slice(first, first + count)
            for row in range(q, field_rows, 4):
                mixed[row // levels, row % levels, span] = pltpu.roll(
                    value[span], LANES - 2 - row, 1
                )

    by_lat = 1.0 / (12.0 * step_lat)
    by_lon = 1.0 / (12.0 * step_lon)

    def one_level(k):
        below = jnp.maximum(k - 1, 0)
        above = jnp.minimum(k + 1, levels - 1)
        radius = jnp.broadcast_to(
            1.0 / step_lat + k.astype(jnp.float32), (SUB, LANES)
        )
        inv_radius = 1.0 / radius
        lat_scale = inv_radius * by_lat
        for first, count in groups:
            for top in range(first, first + count, SUB):
                one_strip(k, below, above, inv_radius, lat_scale, top)

    def one_strip(k, below, above, inv_radius, lat_scale, top):
        strip = slice(top, top + SUB)
        inv_sin, cot = row_box[0, strip], row_box[1, strip]
        inv_arc = inv_radius * inv_sin
        lon_scale = inv_arc * by_lon
        cot_r = cot * inv_radius
        two_r = 2.0 * inv_radius
        curve_lat = (VISCOSITY / (12.0 * step_lat * step_lat)) * inv_radius * inv_radius
        curve_lon = (VISCOSITY / (12.0 * step_lon * step_lon)) * inv_arc * inv_arc
        slope_extra = (VISCOSITY * by_lat) * inv_radius * cot_r
        radial_extra = VISCOSITY * inv_radius
        center_weight = 2.0 * VISCOSITY + 30.0 * (curve_lat + curve_lon)
        north, south = top == 0, top == rows - SUB

        def derive(f, full):
            here = [block[f, t, k, SUB + top : 2 * SUB + top] for t in range(tiles)]
            ghost = mixed[f, k, strip]
            ghost_w, ghost_e = pltpu.roll(ghost, LANES - 1, 1), pltpu.roll(ghost, 1, 1)
            w1s = [pltpu.roll(x, 1, 1) for x in here]
            w2s = [pltpu.roll(x, 2, 1) for x in here]
            e1s = [pltpu.roll(x, LANES - 1, 1) for x in here]
            e2s = [pltpu.roll(x, LANES - 2, 1) for x in here]
            out = []
            for t in range(tiles):
                at = SUB + top
                n1, n2 = block[f, t, k, at - 1 : at + 7], block[f, t, k, at - 2 : at + 6]
                s1, s2 = block[f, t, k, at + 1 : at + 9], block[f, t, k, at + 2 : at + 10]
                if north:
                    g2 = jnp.broadcast_to(halo[0, 0, f, t, pl.ds(k, 1), :], (SUB, LANES))
                    g1 = jnp.broadcast_to(halo[0, 1, f, t, pl.ds(k, 1), :], (SUB, LANES))
                    n1 = jnp.where(sub8 == 0, g1, n1)
                    n2 = jnp.where(sub8 == 0, g2, jnp.where(sub8 == 1, g1, n2))
                if south:
                    g1 = jnp.broadcast_to(halo[1, 0, f, t, pl.ds(k, 1), :], (SUB, LANES))
                    g2 = jnp.broadcast_to(halo[1, 1, f, t, pl.ds(k, 1), :], (SUB, LANES))
                    s1 = jnp.where(sub8 == SUB - 1, g1, s1)
                    s2 = jnp.where(sub8 == SUB - 1, g2, jnp.where(sub8 == SUB - 2, g1, s2))
                w1 = jnp.where(lane8 == 0, w1s[t - 1] if t else ghost_w, w1s[t])
                w2 = jnp.where(lane8 < 2, w2s[t - 1] if t else ghost, w2s[t])
                last = t == tiles - 1
                e1 = jnp.where(lane8 == LANES - 1, ghost_e if last else e1s[t + 1], e1s[t])
                e2 = jnp.where(lane8 >= LANES - 2, ghost if last else e2s[t + 1], e2s[t])
                low = block[f, t, below, SUB + top : 2 * SUB + top]
                high = block[f, t, above, SUB + top : 2 * SUB + top]
                rad = high - low
                lat = 8.0 * (s1 - n1) - (s2 - n2)
                lon = 8.0 * (e1 - w1) - (e2 - w2)
                bend = None
                if full:
                    bend = (
                        VISCOSITY * (high + low)
                        + curve_lat * (16.0 * (s1 + n1) - (s2 + n2))
                        + curve_lon * (16.0 * (e1 + w1) - (e2 + w2))
                        - center_weight * here[t]
                    )
                out.append((rad, lat, lon, bend))
            return here, out

        wind_rad = [block[1, t, k, SUB + top : 2 * SUB + top] for t in range(tiles)]
        wind_lat = [block[2, t, k, SUB + top : 2 * SUB + top] for t in range(tiles)]
        wind_lon = [block[3, t, k, SUB + top : 2 * SUB + top] for t in range(tiles)]
        go_rad = [0.5 * x for x in wind_rad]
        go_lat = [lat_scale * x for x in wind_lat]
        go_lon = [lon_scale * x for x in wind_lon]

        def put(f, t, center, rate):
            lanes = slice(t * LANES, (t + 1) * LANES)
            rate_box[f, k, strip, lanes] = rate
            state_box[f, k, strip, lanes] = (
                0.75 * outset[0, f, k, strip, lanes] + 0.25 * center
            ) + (0.25 * TIME_STEP) * rate

        rho_here, rho_d = derive(0, False)
        heat_here, heat_d = derive(4, True)
        ratio = [heat_here[t] / rho_here[t] for t in range(tiles)]
        press, rho_rate, heat_rate = [], [], []
        for t in range(tiles):
            (a, b, c, _), (d, e, g, bend) = rho_d[t], heat_d[t]
            press.append(
                (
                    0.5 * (ratio[t] * a + d),
                    lat_scale * (ratio[t] * b + e),
                    lon_scale * (ratio[t] * c + g),
                )
            )
            rho_rate.append(go_rad[t] * a + go_lat[t] * b + go_lon[t] * c)
            heat_rate.append(
                bend
                + (radial_extra - go_rad[t]) * d
                + (slope_extra - go_lat[t]) * e
                - go_lon[t] * g
            )
        diverge = [two_r * wind_rad[t] + cot_r * wind_lat[t] for t in range(tiles)]
        for f in (1, 2, 3):
            here, d_all = derive(f, True)
            for t in range(tiles):
                d, e, g, bend = d_all[t]
                spin_rad, spin_lat = spin_box[0, t, strip], spin_box[1, t, strip]
                spin_lon = spin_box[2, t, strip]
                rate = (
                    bend
                    + (radial_extra - go_rad[t]) * d
                    + (slope_extra - go_lat[t]) * e
                    - go_lon[t] * g
                    - press[t][f - 1]
                )
                if f == 1:
                    diverge[t] += 0.5 * d
                    rate += inv_radius * (wind_lat[t] * wind_lat[t] + wind_lon[t] * wind_lon[t])
                    rate += spin_lon * wind_lat[t] - spin_lat * wind_lon[t] - GRAVITY
                elif f == 2:
                    diverge[t] += lat_scale * e
                    rate += cot_r * (wind_lon[t] * wind_lon[t])
                    rate -= inv_radius * (wind_rad[t] * wind_lat[t])
                    rate += spin_rad * wind_lon[t] - spin_lon * wind_rad[t]
                else:
                    diverge[t] += lon_scale * g
                    rate -= (inv_radius * wind_rad[t] + cot_r * wind_lat[t]) * wind_lon[t]
                    rate += spin_lat * wind_rad[t] - spin_rad * wind_lat[t]
                put(f, t, here[t], rate)
        for t in range(tiles):
            put(0, t, rho_here[t], -rho_rate[t] - rho_here[t] * diverge[t])
            put(
                4,
                t,
                heat_here[t],
                heat_rate[t] - (GAMMA - 1.0) * (heat_here[t] * diverge[t]),
            )

    for c in range(chunks):
        @pl.loop(c * chunk, (c + 1) * chunk)
        def _(k):
            one_level(k)

        for copy in out_copies(c):
            copy.start()
    for c in range(chunks):
        for copy in out_copies(c):
            copy.wait()


def stencil(partners, turning, replies, sides, halos, block, row_box, spin_box, outset):
    levels, rows, cols = outset.shape[2:]
    n_lat, n_lon = lax.axis_size("lat"), lax.axis_size("lon")
    chunk = 4
    out = jax.ShapeDtypeStruct(outset.shape, jnp.float32)
    box = pltpu.VMEM(outset.shape[1:], jnp.float32)
    return pl.pallas_call(
        functools.partial(stencil_kernel, (n_lat, n_lon, levels, rows, cols), chunk),
        out_shape=(out, out),
        in_specs=[SMEM] + [VMEM] * (n_lat + 9),
        out_specs=(ANY, ANY),
        scratch_shapes=[
            box,
            box,
            pltpu.VMEM((n_lat,) + replies[0].shape, jnp.float32),
            pltpu.VMEM((2,) + halos[0].shape, jnp.float32),
            pltpu.VMEM((2, 2, rows, LANES), jnp.float32),
            pltpu.VMEM((5, levels, rows, LANES), jnp.float32),
            pltpu.SemaphoreType.DMA((levels // chunk, 2)),
        ],
        compiler_params=pltpu.CompilerParams(vmem_limit_bytes=25 * MIB),
        cost_estimate=pl.CostEstimate(
            flops=250 * levels * rows * cols,
            bytes_accessed=80 * levels * rows * cols,
            transcendentals=0,
        ),
        name="stencil",
    )(partners, turning, *replies, *sides, *halos, block, row_box, spin_box, outset)


def shards(rho, flow, heat, outset, opposite_block, donor_lower_corner, blend, turning):
    levels, rows, cols = rho.shape[1:]
    n_lat = lax.axis_size("lat")
    request = ask(opposite_block, donor_lower_corner, blend, rows, cols)
    requests = [swap_panels(request, d) for d in range(n_lat)]
    cells, block, even_rows, odd_rows, even_cols, odd_cols, row_box, spin_box = prepare(
        rho, flow, heat
    )
    *requests, even_rows, odd_rows, even_cols, odd_cols = lax.optimization_barrier(
        (*requests, even_rows, odd_rows, even_cols, odd_cols)
    )
    sides = (swap_pairs(even_cols, "lon", False), swap_pairs(odd_cols, "lon", True))
    halos = (swap_pairs(even_rows, "lat", False), swap_pairs(odd_rows, "lat", True))
    replies = donate(requests, cells, rows, cols, 5 * levels)
    replies = [swap_panels(reply, d) for d, reply in enumerate(replies)]
    return stencil(
        opposite_block, turning, replies, sides, halos, block, row_box, spin_box, outset
    )


def solution(mesh):
    in_specs = (
        P("panel", None, "lat", "lon"),
        P("panel", None, None, "lat", "lon"),
        P("panel", None, "lat", "lon"),
        P("panel", None, None, "lat", "lon"),
        P("panel", "lat", "lon", None),
        P("panel", "lat", "lon", None),
        P("panel", "lat", "lon", None, None),
        P("panel", "lat", "lon", None, None),
    )
    out_specs = (P("panel", None, None, "lat", "lon"), P("panel", None, None, "lat", "lon"))
    return jax.shard_map(shards, mesh=mesh, in_specs=in_specs, out_specs=out_specs, check_vma=False)
```

time: 77.1 us -> 44.5 us (0.58)
  the two profiles are of different devices: /device:TPU:1 before, /device:TPU:0 now
where the time goes in v1:
time: 44.5 us; the launch traced here: 44.2 us
  Pallas kernels  22.2 us (50%)
  starting transfers between devices  15.4 us (35%)
  waiting for transfers between devices  5.85 us (13%)
  between operations  0.75 us (2%)
    pallas_call x1, Pallas kernels, stencil(): pl.pallas_call(functools.partial(stencil_kernel, (n_lat, n_lon, levels, r...  11 us
    ppermute x8, starting transfers between devices, swap_panels(): return lax.ppermute(value, ('panel', 'lat'), pairs)  8.12 us
    ppermute x4, starting transfers between devices, swap_pairs(): lax.ppermute(value, axis, [(i, pair_partner(i, count, odd)) for i in rang...  7.31 us
    pallas_call x1, Pallas kernels, donate(): pl.pallas_call(functools.partial(donate_kernel, n_lat, n_lon, rows, cols,...  5.53 us
    pallas_call x1, Pallas kernels, prepare(): pl.pallas_call(functools.partial(prepare_kernel, lax.axis_size('lat'), la...  4.84 us
    ppermute x8, waiting for transfers between devices, swap_panels(): return lax.ppermute(value, ('panel', 'lat'), pairs)  4.06 us
    ppermute x4, waiting for transfers between devices, swap_pairs(): lax.ppermute(value, axis, [(i, pair_partner(i, count, odd)) for i in rang...  1.79 us
  transfers between devices with their start and end apart: 12, of which 3 were waited for; matrix products, arithmetic and copies ran while one was open for 0% of the time, Pallas kernels for 23%

profile of v1, /device:TPU:0, one launch (start us, length us, event | category | flops | bytes accessed | tf_op | source)
XLA Modules:
  0.0 44.2 jit_solution(14534497183220721588)
XLA Ops:
  0.6 0.8 %ask.1 = f32[8,896]{1,0:T(8,128)S(1)} custom-call(s32[1,1,1,1664]{3,2,1,0:T(1,128)} %refs_0_.1, s32[1,1,1,1664]{3,2,1,0:T(1,128)} %corners.1, f32[1,1,1,4,1664]{4,3,2,1,0:T(4,128)} %blend.1), custom_call_target="tpu_custom_call" | custom-call | tf_op jit(solution)/shard_map/ask/pallas_call | solution.py:86
  1.4 3.4 %collective-permute-start.3 = (f32[8,896]{1,0:T(8,128)S(1)}, f32[8,896]{1,0:T(8,128)S(1)}, u32[]{:S(2)}, u32[]{:S(2)}) collective-permute-start(f32[8,896]{1,0:T(8,128)S(1)} %ask.1), channel_id=1, source_target_pairs={{0,28},{4,24},{8,20},{12,16},{16,12},{20,8},{24,4},{28,0},{1,29},{... | collective-permute-start | bytes 86024 | tf_op jit(solution)/shard_map/ppermute | solution.py:46
  4.8 0.8 %collective-permute-start.2 = (f32[8,896]{1,0:T(8,128)S(1)}, f32[8,896]{1,0:T(8,128)S(1)}, u32[]{:S(2)}, u32[]{:S(2)}) collective-permute-start(f32[8,896]{1,0:T(8,128)S(1)} %ask.1), channel_id=1, source_target_pairs={{0,24},{4,28},{8,16},{12,20},{16,8},{20,12},{24,0},{28,4},{1,25},{... | collective-permute-start | bytes 86024 | tf_op jit(solution)/shard_map/ppermute | solution.py:46
  5.6 0.1 collective-permute-start.1
  5.8 0.0 collective-permute-start
  5.8 4.8 %prepare.1 = (f32[12288,128]{1,0:T(8,128)S(1)}, f32[5,3,16,48,128]{4,3,2,1,0:T(8,128)S(1)}, f32[2,5,3,16,128]{4,3,2,1,0:T(8,128)S(1)}, f32[2,5,3,16,128]{4,3,2,1...) custom-call(f32[1,16,32,384]{3,2,1,0:T(8,128)} %rho.1, ...), custom_call_target="tpu_custom_call" | custom-call | tf_op jit(solution)/shard_map/prepare/pallas_call | solution.py:194
  10.6 0.0 copy-start
  10.6 0.0 copy-start.1
  10.6 0.0 copy-start.2
  10.7 0.0 collective-permute-done.3.refs_3_
  10.7 0.0 collective-permute-done.2.refs_2_
  10.7 0.0 collective-permute-done.1.refs_1_
  10.7 0.0 collective-permute-done.refs_0_
  10.7 2.1 %collective-permute-start.10 = (f32[2,5,3,16,128]{4,3,2,1,0:T(8,128)S(1)}, f32[2,5,3,16,128]{4,3,2,1,0:T(8,128)S(1)}, u32[]{:S(2)}, u32[]{:S(2)}) collective-permute-start(f32[2,5,3,16,128]{4,3,2,1,0:T(8,128)S(1)} %get-tuple-element.37), channel_id=1, source_target_pairs={{0,4},{4,0},{8,12},{12,8},{1,5},{5,1},{9,13},{13,9},{2,6},{6,2},{1... | collective-permute-start | bytes 737288 | tf_op jit(solution)/shard_map/ppermute | solution.py:38
  12.8 1.5 %collective-permute-start.11 = (f32[2,5,3,16,128]{4,3,2,1,0:T(8,128)S(1)}, f32[2,5,3,16,128]{4,3,2,1,0:T(8,128)S(1)}, u32[]{:S(2)}, u32[]{:S(2)}) collective-permute-start(f32[2,5,3,16,128]{4,3,2,1,0:T(8,128)S(1)} %get-tuple-element.38), channel_id=1, source_target_pairs={{0,12},{4,8},{8,4},{12,0},{1,13},{5,9},{9,5},{13,1},{2,14},{6,10},... | collective-permute-start | bytes 737288 | tf_op jit(solution)/shard_map/ppermute | solution.py:38
  14.3 5.5 %donate.1 = (f32[96,256]{1,0:T(8,128)S(1)}, f32[96,256]{1,0:T(8,128)S(1)}, f32[96,256]{1,0:T(8,128)S(1)}, f32[96,256]{1,0:T(8,128)S(1)}) custom-call(f32[8,896]{1,0:T(8,128)S(1)} %collective-permute-done.refs_0_, f32[8,896]{1,0:T(8,128)S(1)} %collective-permute-done.1.refs_1_, f32[8,896]{1,0:T(8,128)S(1)} %collective-permute-done.2.refs_2_, ...), custom_call_target="tpu_custom_call" | custom-call | tf_op jit(solution)/shard_map/donate/pallas_call | solution.py:314
  19.8 0.1 collective-permute-start.4
  19.9 0.8 %collective-permute-start.8 = (f32[2,32,128]{2,1,0:T(8,128)S(1)}, f32[2,32,128]{2,1,0:T(8,128)S(1)}, u32[]{:S(2)}, u32[]{:S(2)}) collective-permute-start(f32[2,32,128]{2,1,0:T(8,128)S(1)} %get-tuple-element.35), channel_id=1, source_target_pairs={{0,1},{1,0},{2,3},{3,2},{4,5},{5,4},{6,7},{7,6},{8,9},{9,8},{10,11... | collective-permute-start | bytes 98312 | tf_op jit(solution)/shard_map/ppermute | solution.py:38
  20.7 3.0 %collective-permute-start.9 = (f32[2,32,128]{2,1,0:T(8,128)S(1)}, f32[2,32,128]{2,1,0:T(8,128)S(1)}, u32[]{:S(2)}, u32[]{:S(2)}) collective-permute-start(f32[2,32,128]{2,1,0:T(8,128)S(1)} %get-tuple-element.36), channel_id=1, source_target_pairs={{0,3},{1,2},{2,1},{3,0},{4,7},{5,6},{6,5},{7,4},{8,11},{9,10},{10,... | collective-permute-start | bytes 98312 | tf_op jit(solution)/shard_map/ppermute | solution.py:38
  23.6 0.2 collective-permute-done.8.refs_6_
  23.9 1.0 %collective-permute-start.5 = (f32[96,256]{1,0:T(8,128)S(1)}, f32[96,256]{1,0:T(8,128)S(1)}, u32[]{:S(2)}, u32[]{:S(2)}) collective-permute-start(f32[96,256]{1,0:T(8,128)S(1)} %get-tuple-element.32), channel_id=1, source_target_pairs={{0,20},{4,16},{8,28},{12,24},{16,4},{20,0},{24,12},{28,8},{1,21},{... | collective-permute-start | bytes 294920 | tf_op jit(solution)/shard_map/ppermute | solution.py:46
  24.9 1.6 %collective-permute-done.9.refs_7_ = f32[2,32,128]{2,1,0:T(8,128)S(1)} collective-permute-done((f32[2,32,128]{2,1,0:T(8,128)S(1)}, f32[2,32,128]{2,1,0:T(8,128)S(1)}, u32[]{:S(2)}, u32[]{:S(2)}) %collective-permute-start.9) | collective-permute-done | bytes 32800 | tf_op jit(solution)/shard_map/ppermute | solution.py:38
  26.4 0.0 collective-permute-start.6
  26.4 0.0 collective-permute-done.4.refs_2_
  26.4 2.7 %collective-permute-start.7 = (f32[96,256]{1,0:T(8,128)S(1)}, f32[96,256]{1,0:T(8,128)S(1)}, u32[]{:S(2)}, u32[]{:S(2)}) collective-permute-start(f32[96,256]{1,0:T(8,128)S(1)} %get-tuple-element.34), channel_id=1, source_target_pairs={{0,28},{4,24},{8,20},{12,16},{16,12},{20,8},{24,4},{28,0},{1,29},{... | collective-permute-start | bytes 294920 | tf_op jit(solution)/shard_map/ppermute | solution.py:46
  29.1 0.0 collective-permute-done.5.refs_3_
  29.1 4.0 %collective-permute-done.6.refs_4_ = f32[96,256]{1,0:T(8,128)S(1)} collective-permute-done((f32[96,256]{1,0:T(8,128)S(1)}, f32[96,256]{1,0:T(8,128)S(1)}, u32[]{:S(2)}, u32[]{:S(2)}) %collective-permute-start.6) | collective-permute-done | bytes 98336 | tf_op jit(solution)/shard_map/ppermute | solution.py:46
  33.2 0.0 collective-permute-done.7.refs_5_
  33.2 0.0 collective-permute-done.10.refs_8_
  33.2 0.0 collective-permute-done.11.refs_9_
  33.2 0.0 copy-done
  33.2 11.0 %stencil.1 = (f32[1,5,16,32,384]{4,3,2,1,0:T(8,128)}, f32[1,5,16,32,384]{4,3,2,1,0:T(8,128)}) custom-call(s32[1,1,1,1664]{3,2,1,0:T(1,128)S(1)} %copy-done.1, f32[1,1,1,2,1664]{4,3,2,1,0:T(2,128)S(1)} %copy-done.2, f32[96,256]{1,0:T(8,128)S(1)} %collective-permute-done.4.refs_2_, f32[96,256]{1,0:T(8,128)S(1)} %collective-permute-done.5.refs_3_, ...), custom_call_target="tpu_custom_call" | custom-call | flops 49152000 | bytes 15728640 | tf_op jit(solution)/shard_map/stencil/pallas_call | solution.py:637
  (2 shorter events, 0.0 us)
Async XLA Ops:
  1.4 9.2 %collective-permute-start.3 = (f32[8,896]{1,0:T(8,128)S(1)}, f32[8,896]{1,0:T(8,128)S(1)}, u32[]{:S(2)}, u32[]{:S(2)}) collective-permute-start(f32[8,896]{1,0:T(8,128)S(1)} %ask.1), channel_id=1, source_target_pairs={{0,28},{4,24},{8,20},{12,16},{16,12},{20,8},{24,4},{28,0},{1,29},{... | collective-permute-start | bytes 86024 | tf_op jit(solution)/shard_map/ppermute | solution.py:46
  4.8 5.8 %collective-permute-start.2 = (f32[8,896]{1,0:T(8,128)S(1)}, f32[8,896]{1,0:T(8,128)S(1)}, u32[]{:S(2)}, u32[]{:S(2)}) collective-permute-start(f32[8,896]{1,0:T(8,128)S(1)} %ask.1), channel_id=1, source_target_pairs={{0,24},{4,28},{8,16},{12,20},{16,8},{20,12},{24,0},{28,4},{1,25},{... | collective-permute-start | bytes 86024 | tf_op jit(solution)/shard_map/ppermute | solution.py:46
  5.6 5.0 %collective-permute-start.1 = (f32[8,896]{1,0:T(8,128)S(1)}, f32[8,896]{1,0:T(8,128)S(1)}, u32[]{:S(2)}, u32[]{:S(2)}) collective-permute-start(f32[8,896]{1,0:T(8,128)S(1)} %ask.1), channel_id=1, source_target_pairs={{0,20},{4,16},{8,28},{12,24},{16,4},{20,0},{24,12},{28,8},{1,21},{... | collective-permute-start | bytes 86024 | tf_op jit(solution)/shard_map/ppermute | solution.py:46
  5.8 4.9 %collective-permute-start = (f32[8,896]{1,0:T(8,128)S(1)}, f32[8,896]{1,0:T(8,128)S(1)}, u32[]{:S(2)}, u32[]{:S(2)}) collective-permute-start(f32[8,896]{1,0:T(8,128)S(1)} %ask.1), channel_id=1, source_target_pairs={{0,16},{4,20},{8,24},{12,28},{16,0},{20,4},{24,8},{28,12},{1,17},{... | collective-permute-start | bytes 86024 | tf_op jit(solution)/shard_map/ppermute | solution.py:46
  10.6 22.6 %copy-start = (f32[1,5,16,32,384]{4,3,2,1,0:T(8,128)S(1)}, f32[1,5,16,32,384]{4,3,2,1,0:T(8,128)}, u32[]{:S(2)}) copy-start(f32[1,5,16,32,384]{4,3,2,1,0:T(8,128)} %refs_13_.1) | copy-start | bytes 11796484
  10.6 22.6 %copy-start.1 = (s32[1,1,1,1664]{3,2,1,0:T(1,128)S(1)}, s32[1,1,1,1664]{3,2,1,0:T(1,128)}, u32[]{:S(2)}) copy-start(s32[1,1,1,1664]{3,2,1,0:T(1,128)} %refs_0_.1) | copy-start | bytes 19972
  10.6 22.6 %copy-start.2 = (f32[1,1,1,2,1664]{4,3,2,1,0:T(2,128)S(1)}, f32[1,1,1,2,1664]{4,3,2,1,0:T(2,128)}, u32[]{:S(2)}) copy-start(f32[1,1,1,2,1664]{4,3,2,1,0:T(2,128)} %refs_1_.1) | copy-start | bytes 39940
  10.7 22.5 %collective-permute-start.10 = (f32[2,5,3,16,128]{4,3,2,1,0:T(8,128)S(1)}, f32[2,5,3,16,128]{4,3,2,1,0:T(8,128)S(1)}, u32[]{:S(2)}, u32[]{:S(2)}) collective-permute-start(f32[2,5,3,16,128]{4,3,2,1,0:T(8,128)S(1)} %get-tuple-element.37), channel_id=1, source_target_pairs={{0,4},{4,0},{8,12},{12,8},{1,5},{5,1},{9,13},{13,9},{2,6},{6,2},{1... | collective-permute-start | bytes 737288 | tf_op jit(solution)/shard_map/ppermute | solution.py:38
  12.8 20.4 %collective-permute-start.11 = (f32[2,5,3,16,128]{4,3,2,1,0:T(8,128)S(1)}, f32[2,5,3,16,128]{4,3,2,1,0:T(8,128)S(1)}, u32[]{:S(2)}, u32[]{:S(2)}) collective-permute-start(f32[2,5,3,16,128]{4,3,2,1,0:T(8,128)S(1)} %get-tuple-element.38), channel_id=1, source_target_pairs={{0,12},{4,8},{8,4},{12,0},{1,13},{5,9},{9,5},{13,1},{2,14},{6,10},... | collective-permute-start | bytes 737288 | tf_op jit(solution)/shard_map/ppermute | solution.py:38
  19.8 6.6 %collective-permute-start.4 = (f32[96,256]{1,0:T(8,128)S(1)}, f32[96,256]{1,0:T(8,128)S(1)}, u32[]{:S(2)}, u32[]{:S(2)}) collective-permute-start(f32[96,256]{1,0:T(8,128)S(1)} %get-tuple-element.31), channel_id=1, source_target_pairs={{0,16},{4,20},{8,24},{12,28},{16,0},{20,4},{24,8},{28,12},{1,17},{... | collective-permute-start | bytes 294920 | tf_op jit(solution)/shard_map/ppermute | solution.py:46
  19.9 4.0 %collective-permute-start.8 = (f32[2,32,128]{2,1,0:T(8,128)S(1)}, f32[2,32,128]{2,1,0:T(8,128)S(1)}, u32[]{:S(2)}, u32[]{:S(2)}) collective-permute-start(f32[2,32,128]{2,1,0:T(8,128)S(1)} %get-tuple-element.35), channel_id=1, source_target_pairs={{0,1},{1,0},{2,3},{3,2},{4,5},{5,4},{6,7},{7,6},{8,9},{9,8},{10,11... | collective-permute-start | bytes 98312 | tf_op jit(solution)/shard_map/ppermute | solution.py:38
  20.7 5.8 %collective-permute-start.9 = (f32[2,32,128]{2,1,0:T(8,128)S(1)}, f32[2,32,128]{2,1,0:T(8,128)S(1)}, u32[]{:S(2)}, u32[]{:S(2)}) collective-permute-start(f32[2,32,128]{2,1,0:T(8,128)S(1)} %get-tuple-element.36), channel_id=1, source_target_pairs={{0,3},{1,2},{2,1},{3,0},{4,7},{5,6},{6,5},{7,4},{8,11},{9,10},{10,... | collective-permute-start | bytes 98312 | tf_op jit(solution)/shard_map/ppermute | solution.py:38
  23.9 5.3 %collective-permute-start.5 = (f32[96,256]{1,0:T(8,128)S(1)}, f32[96,256]{1,0:T(8,128)S(1)}, u32[]{:S(2)}, u32[]{:S(2)}) collective-permute-start(f32[96,256]{1,0:T(8,128)S(1)} %get-tuple-element.32), channel_id=1, source_target_pairs={{0,20},{4,16},{8,28},{12,24},{16,4},{20,0},{24,12},{28,8},{1,21},{... | collective-permute-start | bytes 294920 | tf_op jit(solution)/shard_map/ppermute | solution.py:46
  26.4 6.8 %collective-permute-start.6 = (f32[96,256]{1,0:T(8,128)S(1)}, f32[96,256]{1,0:T(8,128)S(1)}, u32[]{:S(2)}, u32[]{:S(2)}) collective-permute-start(f32[96,256]{1,0:T(8,128)S(1)} %get-tuple-element.33), channel_id=1, source_target_pairs={{0,24},{4,28},{8,16},{12,20},{16,8},{20,12},{24,0},{28,4},{1,25},{... | collective-permute-start | bytes 294920 | tf_op jit(solution)/shard_map/ppermute | solution.py:46
  26.4 6.8 %collective-permute-start.7 = (f32[96,256]{1,0:T(8,128)S(1)}, f32[96,256]{1,0:T(8,128)S(1)}, u32[]{:S(2)}, u32[]{:S(2)}) collective-permute-start(f32[96,256]{1,0:T(8,128)S(1)} %get-tuple-element.34), channel_id=1, source_target_pairs={{0,28},{4,24},{8,20},{12,16},{16,12},{20,8},{24,4},{28,0},{1,29},{... | collective-permute-start | bytes 294920 | tf_op jit(solution)/shard_map/ppermute | solution.py:46

commit v2 on v1

v2 whole, which is shorter than its diff:
```python
import functools
import math

import jax
import jax.numpy as jnp
from jax import lax
from jax.experimental import pallas as pl
from jax.experimental.pallas import tpu as pltpu
from jax.sharding import PartitionSpec as P

OMEGA = 0.5
GRAVITY = 1.0
VISCOSITY = 0.2
DIFFUSIVITY = 0.2
GAMMA = 1.4
TIME_STEP = 0.05
LANES = 128
SUB = 8
MIB = 1024 * 1024
ANY = pl.BlockSpec(memory_space=pl.ANY)
HBM = pl.BlockSpec(memory_space=pltpu.HBM)
VMEM = pl.BlockSpec(memory_space=pltpu.VMEM)
SMEM = pl.BlockSpec(memory_space=pltpu.SMEM)


def in_hbm(value):
    return pltpu.with_memory_space_constraint(value, pltpu.HBM)


def pair_partner(i, count, odd):
    if not odd:
        return i ^ 1
    return (i + 1) % count if i % 2 else (i - 1) % count


def swap_pairs(value, axis, odd):
    count = lax.axis_size(axis)
    return lax.ppermute(value, axis, [(i, pair_partner(i, count, odd)) for i in range(count)])


def swap_panels(value, distance):
    n_lat = lax.axis_size("lat")
    pairs = [
        (p * n_lat + a, (1 - p) * n_lat + (a ^ distance)) for p in range(2) for a in range(n_lat)
    ]
    return lax.ppermute(value, ("panel", "lat"), pairs)


def window_of(run, cols):
    tiles = cols // LANES
    for width in range(1, tiles + 1):
        if all(
            start - min(start // LANES, tiles - width) * LANES + run <= width * LANES
            for start in range(0, cols, run)
        ):
            return width
    return tiles


def ask_kernel(partners, corners, blend, request, partners_box, corners_box, blend_box, sems):
    lat_len = corners.shape[-1] - request.shape[-1]
    copies = [
        pltpu.make_async_copy(partners, partners_box, sems.at[0]),
        pltpu.make_async_copy(corners, corners_box, sems.at[1]),
        pltpu.make_async_copy(blend, blend_box, sems.at[2]),
    ]
    for copy in copies:
        copy.start()
    for copy in copies:
        copy.wait()
    north = lax.axis_index("lat") == 0
    for row, source in ((0, partners_box), (1, corners_box)):
        values = source[0, 0].astype(jnp.float32)
        request[row : row + 1, 0:lat_len] = jnp.where(
            north, values[:, 0:lat_len], values[:, lat_len : 2 * lat_len]
        )
        request[row : row + 1, lat_len:] = values[:, 2 * lat_len :]
    weights = blend_box[0, 0, 0]
    request[2:6, 0:lat_len] = jnp.where(
        north, weights[:, 0:lat_len], weights[:, lat_len : 2 * lat_len]
    )
    request[2:6, lat_len:] = weights[:, 2 * lat_len :]


def ask(partners, corners, blend, rows, cols):
    return pl.pallas_call(
        ask_kernel,
        out_shape=jax.ShapeDtypeStruct((SUB, 2 * cols + 4 * rows), jnp.float32),
        in_specs=[HBM] * 3,
        out_specs=VMEM,
        scratch_shapes=[
            pltpu.VMEM(partners.shape, jnp.int32),
            pltpu.VMEM(corners.shape, jnp.int32),
            pltpu.VMEM(blend.shape, jnp.float32),
            pltpu.SemaphoreType.DMA((3,)),
        ],
        compiler_params=pltpu.CompilerParams(vmem_limit_bytes=MIB),
        name="ask",
    )(*(in_hbm(x) for x in (partners, corners, blend)))


def prepare_kernel(
    n_lat,
    n_lon,
    rho,
    flow,
    heat,
    cells,
    block,
    even_rows,
    odd_rows,
    even_cols,
    odd_cols,
    row_box,
    spin_box,
    staged,
    sems,
):
    levels, rows, cols = rho.shape[1:]
    tiles = cols // LANES
    strips = rows // SUB

    def load_copies(strip):
        here = pl.ds(strip * SUB, SUB)
        return (
            pltpu.make_async_copy(rho.at[0, :, here], staged.at[0, :, here], sems.at[strip, 0]),
            pltpu.make_async_copy(
                flow.at[0, :, :, here], staged.at[pl.ds(1, 3), :, here], sems.at[strip, 1]
            ),
            pltpu.make_async_copy(heat.at[0, :, here], staged.at[4, :, here], sems.at[strip, 2]),
        )

    for strip in range(strips):
        for copy in load_copies(strip):
            copy.start()

    zero = jnp.zeros((levels, SUB, LANES), jnp.float32)
    for field in range(5):
        for tile in range(tiles):
            block[field, tile, :, 0:SUB] = zero
            block[field, tile, :, rows + SUB :] = zero

    step_lat = math.pi / 2.0 / (rows * n_lat)
    step_lon = 1.5 * math.pi / (cols * n_lon)
    sub = lax.broadcasted_iota(jnp.int32, (rows, LANES), 0)
    row_global = (lax.axis_index("lat") * rows + sub).astype(jnp.float32)
    theta = math.pi / 4.0 + (row_global + 0.5) * step_lat
    sin_lat, cos_lat = jnp.sin(theta), jnp.cos(theta)
    row_box[0] = 1.0 / sin_lat
    row_box[1] = cos_lat / sin_lat
    yang = lax.axis_index("panel").astype(jnp.float32)
    yin = 1.0 - yang
    for tile in range(tiles):
        lane = lax.broadcasted_iota(jnp.int32, (SUB, LANES), 1) + tile * LANES
        col_global = (lax.axis_index("lon") * cols + lane).astype(jnp.float32)
        longitude = -0.75 * math.pi + (col_global + 0.5) * step_lon
        sin_lon, cos_lon = jnp.sin(longitude)[0:1], jnp.cos(longitude)[0:1]
        spin_box[0, tile] = 2.0 * OMEGA * (yin * cos_lat + yang * sin_lat * sin_lon)
        spin_box[1, tile] = 2.0 * OMEGA * (yang * cos_lat * sin_lon - yin * sin_lat)
        spin_box[2, tile] = jnp.broadcast_to(2.0 * OMEGA * yang * cos_lon, (rows, LANES))

    for strip in range(strips):
        for copy in load_copies(strip):
            copy.wait()

        here, there = strip * SUB, (strip + 1) * SUB
        for field in range(5):
            for tile in range(tiles):
                block[field, tile, :, there : there + SUB] = staged[
                    field, :, here:there, tile * LANES : (tile + 1) * LANES
                ]
        for row in range(here, there):
            for tile in range(tiles):
                stack = jnp.concatenate(
                    [
                        staged[f, :, row, tile * LANES : (tile + 1) * LANES] for f in range(5)
                    ],
                    axis=0,
                )
                at = row * cols + tile * LANES
                cells[at : at + LANES, 0 : 5 * levels] = stack.T

    lat_even = lax.rem(lax.axis_index("lat"), 2) == 0
    for first, to_even in ((0, jnp.logical_not(lat_even)), (rows - 2, lat_even)):
        for keep, out in ((to_even, even_rows), (jnp.logical_not(to_even), odd_rows)):

            @pl.when(keep)
            def _(first=first, out=out):
                for layer in range(2):
                    for field in range(5):
                        for tile in range(tiles):
                            out[layer, field, tile] = block[field, tile, :, SUB + first + layer, :]

    lon_even = lax.rem(lax.axis_index("lon"), 2) == 0
    for first, to_even in ((0, jnp.logical_not(lon_even)), (cols - 2, lon_even)):
        for keep, out in ((to_even, even_cols), (jnp.logical_not(to_even), odd_cols)):

            @pl.when(keep)
            def _(first=first, out=out):
                for layer in range(2):
                    for row in range(rows):
                        at = row * cols + first + layer
                        out[layer, row : row + 1, :] = cells[at : at + 1, :]


def prepare(rho, flow, heat):
    levels, rows, cols = rho.shape[1:]
    tiles = cols // LANES
    shapes = (
        (rows * cols, LANES),
        (5, tiles, levels, rows + 2 * SUB, LANES),
        (2, 5, tiles, levels, LANES),
        (2, 5, tiles, levels, LANES),
        (2, rows, LANES),
        (2, rows, LANES),
        (2, rows, LANES),
        (3, tiles, rows, LANES),
    )
    return pl.pallas_call(
        functools.partial(prepare_kernel, lax.axis_size("lat"), lax.axis_size("lon")),
        out_shape=tuple(jax.ShapeDtypeStruct(shape, jnp.float32) for shape in shapes),
        in_specs=[ANY] * 3,
        out_specs=(VMEM,) * len(shapes),
        scratch_shapes=[
            pltpu.VMEM((5, levels, rows, cols), jnp.float32),
            pltpu.SemaphoreType.DMA((rows // SUB, 3)),
        ],
        compiler_params=pltpu.CompilerParams(vmem_limit_bytes=16 * MIB),
        name="prepare",
    )(*(in_hbm(x) for x in (rho, flow, heat)))


def donate_kernel(n_lat, n_lon, rows, cols, field_rows, *refs):
    weights = refs[:n_lat]
    cells = refs[n_lat]
    replies = refs[n_lat + 1 : 2 * n_lat + 1]
    corners, turned, gathered, whole_box, requests, sems = refs[2 * n_lat + 1 :]
    slots = weights[0].shape[1]
    for distance in range(n_lat):
        for row in range(2):
            for tile in range(slots // LANES):
                lanes = slice(tile * LANES, (tile + 1) * LANES)
                whole_box[distance, row, tile : tile + 1] = weights[distance][
                    row : row + 1, lanes
                ].astype(jnp.int32)
    copy = pltpu.make_async_copy(whole_box, requests, sems.at[0])
    copy.start()
    for distance in range(n_lat):
        for at in range(0, slots, LANES):
            turned[distance, at : at + LANES, 0:SUB] = weights[distance][:, at : at + LANES].T
    copy.wait()
    lat_len, lon_len = 2 * cols, 2 * rows
    run_lat, run_lon = lat_len // n_lat, lon_len // n_lat
    tiles = cols // LANES
    width = window_of(run_lat, cols)
    lat_here = lax.axis_index("lat")
    lon_here = lax.axis_index("lon")

    def word(request, row, slot):
        return requests[request, row, lax.shift_right_logical(slot, 7), jnp.bitwise_and(slot, 127)]

    def find_run(request, start, run):
        start = jnp.int32(start)
        found = jnp.int32(0)
        for r in range(1, n_lat):
            match = word(request, 0, start + r * run) == lat_here
            found = jnp.where(match, jnp.int32(r), found)
        return found

    def gather(request, first, count):
        def step(i, carry):
            for u in range(SUB):
                t = i * SUB + u
                cell = word(request, 1, first + t)
                for j, shift in enumerate((0, cols, 1, cols + 1)):
                    corners[j, pl.ds(t, 1), :] = cells[pl.ds(cell + shift, 1), :]
            return carry

        lax.fori_loop(0, count // SUB, step, 0)

    def blend(distance, first, count):
        rows_here = pl.ds(pl.multiple_of(first, SUB), count)
        total = None
        for j in range(4):
            weight = jnp.broadcast_to(turned[distance, rows_here, 2 + j : 3 + j], (count, LANES))
            part = weight * corners[j, 0:count, :]
            total = part if total is None else total + part
        return total

    for distance in range(n_lat):
        request, reply = distance, replies[distance]
        asker = jnp.bitwise_xor(lat_here, distance)

        @pl.when((asker == 0) | (asker == n_lat - 1))
        def _(distance=distance, request=request, reply=reply):
            run = find_run(request, 0, run_lat)
            start = lax.rem(run * run_lat, cols)
            base = jnp.minimum(lax.div(start, LANES), tiles - width)
            offset = pl.multiple_of(start - base * LANES, SUB)
            gather(request, run * run_lat, run_lat)
            gathered[pl.ds(offset, run_lat), :] = blend(distance, run * run_lat, run_lat)
            for tile in range(width):
                block = gathered[tile * LANES : (tile + 1) * LANES, :]
                reply[0:field_rows, tile * LANES : (tile + 1) * LANES] = block.T[0:field_rows]

        @pl.when((lon_here == 0) | (lon_here == n_lon - 1))
        def _(distance=distance, request=request, reply=reply):
            first = lat_len + jnp.where(lon_here == 0, 0, lon_len)
            run = find_run(request, first, run_lon)
            gather(request, first + run * run_lon, run_lon)
            reply[field_rows : field_rows + run_lon, 0:LANES] = blend(
                distance, first + run * run_lon, run_lon
            )


def donate(requests, cells, rows, cols, field_rows):
    n_lat, n_lon = lax.axis_size("lat"), lax.axis_size("lon")
    run_lat = 2 * cols // n_lat
    width = window_of(run_lat, cols)
    slots = requests[0].shape[1]
    words = (pl.cdiv(slots, SUB * LANES) * SUB, LANES)
    reply = jax.ShapeDtypeStruct((field_rows + 2 * rows // n_lat, width * LANES), jnp.float32)
    return pl.pallas_call(
        functools.partial(donate_kernel, n_lat, n_lon, rows, cols, field_rows),
        out_shape=(reply,) * n_lat,
        in_specs=[VMEM] * (n_lat + 1),
        out_specs=(VMEM,) * n_lat,
        scratch_shapes=[
            pltpu.VMEM((4, max(run_lat, 2 * rows // n_lat), LANES), jnp.float32),
            pltpu.VMEM((n_lat, slots, LANES), jnp.float32),
            pltpu.VMEM((width * LANES, LANES), jnp.float32),
            pltpu.VMEM((n_lat, 2) + words, jnp.int32),
            pltpu.SMEM((n_lat, 2) + words, jnp.int32),
            pltpu.SemaphoreType.DMA((1,)),
        ],
        compiler_params=pltpu.CompilerParams(vmem_limit_bytes=9 * MIB),
        name="donate",
    )(*requests, cells)


def core_parts(rows, tiles):
    return (SUB, rows - 2 * SUB, LANES, (tiles - 2) * LANES)


def edge_parts(rows, tiles):
    cols = tiles * LANES
    return (
        (0, SUB, 0, cols),
        (rows - SUB, SUB, 0, cols),
        (SUB, rows - 2 * SUB, 0, LANES),
        (SUB, rows - 2 * SUB, cols - LANES, LANES),
    )


def part_copies(boxes, outs, part, span, sems):
    first, count, lane, lanes = part
    at = (span, pl.ds(first, count), pl.ds(lane, lanes))
    return [
        pltpu.make_async_copy(box.at[(slice(None),) + at], out.at[(0, slice(None)) + at], sems.at[n])
        for n, (box, out) in enumerate(zip(boxes, outs))
    ]


def stencil_kernel(
    geometry, chunk, block, row_box, spin_box, outset, rate_out, state_out, rate_box, state_box, sems
):
    n_lat, n_lon, levels, rows, cols = geometry
    tiles = cols // LANES
    step_lat = math.pi / 2.0 / (rows * n_lat)
    step_lon = 1.5 * math.pi / (cols * n_lon)
    chunks = levels // chunk
    by_lat = 1.0 / (12.0 * step_lat)
    by_lon = 1.0 / (12.0 * step_lon)
    lane8 = lax.broadcasted_iota(jnp.int32, (SUB, LANES), 1)

    def out_copies(c):
        return part_copies(
            (rate_box, state_box),
            (rate_out, state_out),
            core_parts(rows, tiles),
            pl.ds(c * chunk, chunk),
            sems.at[c],
        )

    def one_level(k):
        below = jnp.maximum(k - 1, 0)
        above = jnp.minimum(k + 1, levels - 1)
        radius = jnp.broadcast_to(1.0 / step_lat + k.astype(jnp.float32), (SUB, LANES))
        inv_radius = 1.0 / radius
        for top in range(0, rows, SUB):
            one_strip(k, below, above, inv_radius, inv_radius * by_lat, top)

    def one_strip(k, below, above, inv_radius, lat_scale, top):
        strip = slice(top, top + SUB)
        inv_sin, cot = row_box[0, strip], row_box[1, strip]
        inv_arc = inv_radius * inv_sin
        lon_scale = inv_arc * by_lon
        cot_r = cot * inv_radius
        two_r = 2.0 * inv_radius
        curve_lat = (VISCOSITY / (12.0 * step_lat * step_lat)) * inv_radius * inv_radius
        curve_lon = (VISCOSITY / (12.0 * step_lon * step_lon)) * inv_arc * inv_arc
        slope_extra = (VISCOSITY * by_lat) * inv_radius * cot_r
        radial_extra = VISCOSITY * inv_radius
        center_weight = 2.0 * VISCOSITY + 30.0 * (curve_lat + curve_lon)

        def derive(f, full):
            here = [block[f, t, k, SUB + top : 2 * SUB + top] for t in range(tiles)]
            w1s = [pltpu.roll(x, 1, 1) for x in here]
            w2s = [pltpu.roll(x, 2, 1) for x in here]
            e1s = [pltpu.roll(x, LANES - 1, 1) for x in here]
            e2s = [pltpu.roll(x, LANES - 2, 1) for x in here]
            out = []
            for t in range(tiles):
                at = SUB + top
                n1, n2 = block[f, t, k, at - 1 : at + 7], block[f, t, k, at - 2 : at + 6]
                s1, s2 = block[f, t, k, at + 1 : at + 9], block[f, t, k, at + 2 : at + 10]
                w1 = jnp.where(lane8 == 0, w1s[t - 1] if t else 0.0, w1s[t])
                w2 = jnp.where(lane8 < 2, w2s[t - 1] if t else 0.0, w2s[t])
                last = t == tiles - 1
                e1 = jnp.where(lane8 == LANES - 1, 0.0 if last else e1s[t + 1], e1s[t])
                e2 = jnp.where(lane8 >= LANES - 2, 0.0 if last else e2s[t + 1], e2s[t])
                low = block[f, t, below, SUB + top : 2 * SUB + top]
                high = block[f, t, above, SUB + top : 2 * SUB + top]
                rad = high - low
                lat = 8.0 * (s1 - n1) - (s2 - n2)
                lon = 8.0 * (e1 - w1) - (e2 - w2)
                bend = None
                if full:
                    bend = (
                        VISCOSITY * (high + low)
                        + curve_lat * (16.0 * (s1 + n1) - (s2 + n2))
                        + curve_lon * (16.0 * (e1 + w1) - (e2 + w2))
                        - center_weight * here[t]
                    )
                out.append((rad, lat, lon, bend))
            return here, out

        wind_rad = [block[1, t, k, SUB + top : 2 * SUB + top] for t in range(tiles)]
        wind_lat = [block[2, t, k, SUB + top : 2 * SUB + top] for t in range(tiles)]
        wind_lon = [block[3, t, k, SUB + top : 2 * SUB + top] for t in range(tiles)]
        go_rad = [0.5 * x for x in wind_rad]
        go_lat = [lat_scale * x for x in wind_lat]
        go_lon = [lon_scale * x for x in wind_lon]

        def put(f, t, center, rate):
            lanes = slice(t * LANES, (t + 1) * LANES)
            rate_box[f, k, strip, lanes] = rate
            state_box[f, k, strip, lanes] = (
                0.75 * outset[0, f, k, strip, lanes] + 0.25 * center
            ) + (0.25 * TIME_STEP) * rate

        rho_here, rho_d = derive(0, False)
        heat_here, heat_d = derive(4, True)
        ratio = [heat_here[t] / rho_here[t] for t in range(tiles)]
        press, rho_rate, heat_rate = [], [], []
        for t in range(tiles):
            (a, b, c, _), (d, e, g, bend) = rho_d[t], heat_d[t]
            press.append(
                (
                    0.5 * (ratio[t] * a + d),
                    lat_scale * (ratio[t] * b + e),
                    lon_scale * (ratio[t] * c + g),
                )
            )
            rho_rate.append(go_rad[t] * a + go_lat[t] * b + go_lon[t] * c)
            heat_rate.append(
                bend
                + (radial_extra - go_rad[t]) * d
                + (slope_extra - go_lat[t]) * e
                - go_lon[t] * g
            )
        diverge = [two_r * wind_rad[t] + cot_r * wind_lat[t] for t in range(tiles)]
        for f in (1, 2, 3):
            here, d_all = derive(f, True)
            for t in range(tiles):
                d, e, g, bend = d_all[t]
                spin_rad, spin_lat = spin_box[0, t, strip], spin_box[1, t, strip]
                spin_lon = spin_box[2, t, strip]
                rate = (
                    bend
                    + (radial_extra - go_rad[t]) * d
                    + (slope_extra - go_lat[t]) * e
                    - go_lon[t] * g
                    - press[t][f - 1]
                )
                if f == 1:
                    diverge[t] += 0.5 * d
                    rate += inv_radius * (wind_lat[t] * wind_lat[t] + wind_lon[t] * wind_lon[t])
                    rate += spin_lon * wind_lat[t] - spin_lat * wind_lon[t] - GRAVITY
                elif f == 2:
                    diverge[t] += lat_scale * e
                    rate += cot_r * (wind_lon[t] * wind_lon[t])
                    rate -= inv_radius * (wind_rad[t] * wind_lat[t])
                    rate += spin_rad * wind_lon[t] - spin_lon * wind_rad[t]
                else:
                    diverge[t] += lon_scale * g
                    rate -= (inv_radius * wind_rad[t] + cot_r * wind_lat[t]) * wind_lon[t]
                    rate += spin_lat * wind_rad[t] - spin_rad * wind_lat[t]
                put(f, t, here[t], rate)
        for t in range(tiles):
            put(0, t, rho_here[t], -rho_rate[t] - rho_here[t] * diverge[t])
            put(
                4,
                t,
                heat_here[t],
                heat_rate[t] - (GAMMA - 1.0) * (heat_here[t] * diverge[t]),
            )

    for c in range(chunks):

        @pl.loop(c * chunk, (c + 1) * chunk)
        def _(k):
            one_level(k)

        for copy in out_copies(c):
            copy.start()
    for c in range(chunks):
        for copy in out_copies(c):
            copy.wait()


def stencil(block, row_box, spin_box, outset):
    levels, rows, cols = outset.shape[2:]
    n_lat, n_lon = lax.axis_size("lat"), lax.axis_size("lon")
    chunk = 4
    out = jax.ShapeDtypeStruct(outset.shape, jnp.float32)
    box = jax.ShapeDtypeStruct(outset.shape[1:], jnp.float32)
    return pl.pallas_call(
        functools.partial(stencil_kernel, (n_lat, n_lon, levels, rows, cols), chunk),
        out_shape=(out, out, box, box),
        in_specs=[VMEM] * 4,
        out_specs=(ANY, ANY, VMEM, VMEM),
        scratch_shapes=[pltpu.SemaphoreType.DMA((levels // chunk, 2))],
        compiler_params=pltpu.CompilerParams(vmem_limit_bytes=20 * MIB),
        cost_estimate=pl.CostEstimate(
            flops=250 * levels * rows * cols,
            bytes_accessed=80 * levels * rows * cols,
            transcendentals=0,
        ),
        name="stencil",
    )(block, row_box, spin_box, outset)


def edges_kernel(geometry, chunk, *refs):
    n_lat, n_lon, levels, rows, cols = geometry
    tiles = cols // LANES
    field_rows = 5 * levels
    partners, turning = refs[:2]
    reply_box = refs[2 : 2 + n_lat]
    (
        lon_even,
        lon_odd,
        lat_even,
        lat_odd,
        block,
        row_box,
        rate_in,
        state_in,
        _,
        _,
        rate_out,
        state_out,
        rate_box,
        state_box,
        replies,
        halo,
        side,
        mixed,
        sems,
    ) = refs[2 + n_lat :]
    lat_here = lax.axis_index("lat")
    lon_here = lax.axis_index("lon")
    lat_len, lon_len = 2 * cols, 2 * rows
    run_lat, run_lon = lat_len // n_lat, lon_len // n_lat
    width = window_of(run_lat, cols)
    step_lat = math.pi / 2.0 / (rows * n_lat)
    step_lon = 1.5 * math.pi / (cols * n_lon)
    by_lat = 1.0 / (12.0 * step_lat)
    by_lon = 1.0 / (12.0 * step_lon)
    chunks = levels // chunk
    parts = edge_parts(rows, tiles)

    def out_copies(c):
        out = []
        for n, part in enumerate(parts):
            out += part_copies(
                (rate_box, state_box),
                (rate_out, state_out),
                part,
                pl.ds(c * chunk, chunk),
                sems.at[c, n],
            )
        return out

    lat_is_even = lax.rem(lat_here, 2) == 0
    lon_is_even = lax.rem(lon_here, 2) == 0
    for even, north, south in ((True, lat_odd, lat_even), (False, lat_even, lat_odd)):

        @pl.when(lat_is_even == even)
        def _(north=north, south=south):
            halo[0] = north[...]
            halo[1] = south[...]

    for even, west, east in ((True, lon_odd, lon_even), (False, lon_even, lon_odd)):

        @pl.when(lon_is_even == even)
        def _(west=west, east=east):
            side[0] = west[...]
            side[1] = east[...]

    @pl.when((lat_here == 0) | (lat_here == n_lat - 1) | (lon_here == 0) | (lon_here == n_lon - 1))
    def _():
        for d in range(n_lat):
            replies[d] = reply_box[d][...]

    lane8 = lax.broadcasted_iota(jnp.int32, (SUB, LANES), 1)
    sub8 = lax.broadcasted_iota(jnp.int32, (SUB, LANES), 0)

    for which, slot0 in ((0, 0), (1, lat_len)):

        @pl.when(lat_here == (0 if which == 0 else n_lat - 1))
        def _(which=which, slot0=slot0):
            sources = [
                jnp.bitwise_xor(partners[0, 0, 0, slot0 + r * run_lat], lat_here) for r in range(n_lat)
            ]
            for layer in range(2):
                for t in range(tiles):
                    lane = lax.broadcasted_iota(jnp.int32, (field_rows, LANES), 1) + t * LANES
                    value = None
                    for r in range(n_lat):
                        first = r * run_lat - layer * cols
                        if first < 0 or first >= cols:
                            continue
                        if first >= (t + 1) * LANES or first + run_lat <= t * LANES:
                            continue
                        base = min(first // LANES, tiles - width)
                        here = (t - base) * LANES
                        piece = replies[sources[r], 0:field_rows, here : here + LANES]
                        value = piece if value is None else jnp.where(lane >= first, piece, value)
                    spot = slot0 + layer * cols + t * LANES
                    cosine = turning[0, 0, 0, 0:1, spot : spot + LANES]
                    sine = turning[0, 0, 0, 1:2, spot : spot + LANES]
                    parts = [value[f * levels : (f + 1) * levels] for f in range(5)]
                    parts[2], parts[3] = (
                        cosine * parts[2] + sine * parts[3],
                        cosine * parts[3] - sine * parts[2],
                    )
                    for f in range(5):
                        halo[which, layer, f, t] = parts[f]

    turn_lon = jnp.concatenate(
        [turning[0, 0, 0, :, 2 * lat_len :], jnp.zeros((SUB - 2, 2 * lon_len), jnp.float32)], axis=0
    ).T

    for which, slot0 in ((0, 2 * lat_len), (1, 2 * lat_len + lon_len)):
        @pl.when(lon_here == (0 if which == 0 else n_lon - 1))
        def _(which=which, slot0=slot0):
            lane = lax.broadcasted_iota(jnp.int32, (run_lon, LANES), 1)
            is_lat = (lane >= 2 * levels) & (lane < 3 * levels)
            is_lon = (lane >= 3 * levels) & (lane < 4 * levels)
            for r in range(n_lat):
                source = jnp.bitwise_xor(partners[0, 0, 0, slot0 + r * run_lon], lat_here)
                layer, first = r * run_lon // rows, r * run_lon % rows
                value = replies[source, field_rows : field_rows + run_lon, 0:LANES]
                slots = slice(which * lon_len + r * run_lon, which * lon_len + (r + 1) * run_lon)
                cosine = jnp.broadcast_to(turn_lon[slots, 0:1], (run_lon, LANES))
                sine = jnp.broadcast_to(turn_lon[slots, 1:2], (run_lon, LANES))
                later = pltpu.roll(value, LANES - levels, 1)
                earlier = pltpu.roll(value, levels, 1)
                value = jnp.where(
                    is_lat,
                    cosine * value + sine * later,
                    jnp.where(is_lon, cosine * value - sine * earlier, value),
                )
                side[which, layer, first : first + run_lon] = value

    lane_all = lax.broadcasted_iota(jnp.int32, (rows, LANES), 1)
    columns = [side[1, 0], side[1, 1], side[0, 0], side[0, 1]]
    columns = [columns[0]] + [pltpu.roll(columns[j], j, 1) for j in range(1, 4)]
    for q in range(4):
        pick = jnp.bitwise_and(lane_all - q, 3)
        value = columns[0]
        for j in range(1, 4):
            value = jnp.where(pick == j, columns[j], value)
        for row in range(q, field_rows, 4):
            mixed[row // levels, row % levels] = pltpu.roll(value, LANES - 2 - row, 1)

    def one_level(k):
        radius = jnp.broadcast_to(1.0 / step_lat + k.astype(jnp.float32), (SUB, LANES))
        inv_radius = 1.0 / radius
        for top in range(0, rows, SUB):
            for t in range(tiles):
                if top in (0, rows - SUB) or t in (0, tiles - 1):
                    one_tile(k, inv_radius, top, t)

    def one_tile(k, inv_radius, top, t):
        strip, lanes = slice(top, top + SUB), slice(t * LANES, (t + 1) * LANES)
        inv_arc = inv_radius * row_box[0, strip]
        lat_scale, lon_scale = inv_radius * by_lat, inv_arc * by_lon
        curve_lat = (VISCOSITY / (12.0 * step_lat * step_lat)) * inv_radius * inv_radius
        curve_lon = (VISCOSITY / (12.0 * step_lon * step_lon)) * inv_arc * inv_arc
        slope_extra = (VISCOSITY * by_lat) * inv_radius * (row_box[1, strip] * inv_radius)
        rho, _, wind_lat, wind_lon, heat = (
            block[f, t, k, SUB + top : 2 * SUB + top] for f in range(5)
        )
        go_lat, go_lon = lat_scale * wind_lat, lon_scale * wind_lon
        ratio = heat / rho

        def add(total, value):
            return value if total is None else total + value

        lat_d, lat_b, lon_d, lon_b = ([None] * 5 for _ in range(4))
        for f in range(5):
            if top == 0:
                far = jnp.broadcast_to(halo[0, 0, f, t, pl.ds(k, 1), :], (SUB, LANES))
                near = jnp.broadcast_to(halo[0, 1, f, t, pl.ds(k, 1), :], (SUB, LANES))
                second = jnp.where(sub8 == 0, far, jnp.where(sub8 == 1, near, 0.0))
                near = 8.0 * jnp.where(sub8 == 0, near, 0.0)
                lat_d[f] = add(lat_d[f], second - near)
                lat_b[f] = add(lat_b[f], 2.0 * near - second)
            if top == rows - SUB:
                near = jnp.broadcast_to(halo[1, 0, f, t, pl.ds(k, 1), :], (SUB, LANES))
                far = jnp.broadcast_to(halo[1, 1, f, t, pl.ds(k, 1), :], (SUB, LANES))
                second = jnp.where(sub8 == SUB - 1, far, jnp.where(sub8 == SUB - 2, near, 0.0))
                near = 8.0 * jnp.where(sub8 == SUB - 1, near, 0.0)
                lat_d[f] = add(lat_d[f], near - second)
                lat_b[f] = add(lat_b[f], 2.0 * near - second)
            ghost = mixed[f, k, strip]
            if t == 0:
                second = jnp.where(lane8 < 2, ghost, 0.0)
                near = 8.0 * jnp.where(lane8 == 0, pltpu.roll(ghost, LANES - 1, 1), 0.0)
                lon_d[f] = add(lon_d[f], second - near)
                lon_b[f] = add(lon_b[f], 2.0 * near - second)
            if t == tiles - 1:
                second = jnp.where(lane8 >= LANES - 2, ghost, 0.0)
                near = 8.0 * jnp.where(lane8 == LANES - 1, pltpu.roll(ghost, 1, 1), 0.0)
                lon_d[f] = add(lon_d[f], near - second)
                lon_b[f] = add(lon_b[f], 2.0 * near - second)

        rates = [None] * 5
        diverge = None
        if lat_d[0] is not None:
            diverge = add(diverge, lat_scale * lat_d[2])
            rates[0] = add(rates[0], -go_lat * lat_d[0])
            for f in range(1, 5):
                rates[f] = add(
                    rates[f], curve_lat * lat_b[f] + (slope_extra - go_lat) * lat_d[f]
                )
            rates[2] -= lat_scale * (ratio * lat_d[0] + lat_d[4])
        if lon_d[0] is not None:
            diverge = add(diverge, lon_scale * lon_d[3])
            rates[0] = add(rates[0], -go_lon * lon_d[0])
            for f in range(1, 5):
                rates[f] = add(rates[f], curve_lon * lon_b[f] - go_lon * lon_d[f])
            rates[3] -= lon_scale * (ratio * lon_d[0] + lon_d[4])
        rates[0] -= rho * diverge
        rates[4] -= (GAMMA - 1.0) * (heat * diverge)
        for f in range(5):
            rate_box[f, k, strip, lanes] = rate_in[f, k, strip, lanes] + rates[f]
            state_box[f, k, strip, lanes] = (
                state_in[f, k, strip, lanes] + (0.25 * TIME_STEP) * rates[f]
            )

    for c in range(chunks):

        @pl.loop(c * chunk, (c + 1) * chunk)
        def _(k):
            one_level(k)

        for copy in out_copies(c):
            copy.start()
    for c in range(chunks):
        for copy in out_copies(c):
            copy.wait()


def edges(partners, turning, replies, sides, halos, block, row_box, inner):
    rate_out, state_out, rate_box, state_box = inner
    levels, rows, cols = rate_box.shape[1:]
    n_lat, n_lon = lax.axis_size("lat"), lax.axis_size("lon")
    chunk = 4
    out = jax.ShapeDtypeStruct(rate_out.shape, jnp.float32)
    box = pltpu.VMEM(rate_box.shape, jnp.float32)
    n_in = n_lat + 10
    return pl.pallas_call(
        functools.partial(edges_kernel, (n_lat, n_lon, levels, rows, cols), chunk),
        out_shape=(out, out),
        in_specs=[SMEM] + [VMEM] * (n_in - 1) + [ANY] * 2,
        out_specs=(ANY, ANY),
        input_output_aliases={n_in: 0, n_in + 1: 1},
        scratch_shapes=[
            box,
            box,
            pltpu.VMEM((n_lat,) + replies[0].shape, jnp.float32),
            pltpu.VMEM((2,) + halos[0].shape, jnp.float32),
            pltpu.VMEM((2, 2, rows, LANES), jnp.float32),
            pltpu.VMEM((5, levels, rows, LANES), jnp.float32),
            pltpu.SemaphoreType.DMA((levels // chunk, 4, 2)),
        ],
        compiler_params=pltpu.CompilerParams(vmem_limit_bytes=20 * MIB),
        cost_estimate=pl.CostEstimate(
            flops=40 * levels * rows * cols,
            bytes_accessed=40 * levels * rows * cols,
            transcendentals=0,
        ),
        name="edges",
    )(
        partners,
        turning,
        *replies,
        *sides,
        *halos,
        block,
        row_box,
        rate_box,
        state_box,
        rate_out,
        state_out,
    )


def shards(rho, flow, heat, outset, opposite_block, donor_lower_corner, blend, turning):
    levels, rows, cols = rho.shape[1:]
    n_lat = lax.axis_size("lat")
    request = ask(opposite_block, donor_lower_corner, blend, rows, cols)
    requests = [swap_panels(request, d) for d in range(n_lat)]
    cells, block, even_rows, odd_rows, even_cols, odd_cols, row_box, spin_box = prepare(
        rho, flow, heat
    )
    *requests, even_rows, odd_rows, even_cols, odd_cols = lax.optimization_barrier(
        (*requests, even_rows, odd_rows, even_cols, odd_cols)
    )
    sides = (swap_pairs(even_cols, "lon", False), swap_pairs(odd_cols, "lon", True))
    halos = (swap_pairs(even_rows, "lat", False), swap_pairs(odd_rows, "lat", True))
    replies = donate(requests, cells, rows, cols, 5 * levels)
    *replies, spin_box = lax.optimization_barrier((*replies, spin_box))
    replies = [swap_panels(reply, d) for d, reply in enumerate(replies)]
    inner = stencil(block, row_box, spin_box, outset)
    return edges(opposite_block, turning, replies, sides, halos, block, row_box, inner)


def solution(mesh):
    in_specs = (
        P("panel", None, "lat", "lon"),
        P("panel", None, None, "lat", "lon"),
        P("panel", None, "lat", "lon"),
        P("panel", None, None, "lat", "lon"),
        P("panel", "lat", "lon", None),
        P("panel", "lat", "lon", None),
        P("panel", "lat", "lon", None, None),
        P("panel", "lat", "lon", None, None),
    )
    out_specs = (P("panel", None, None, "lat", "lon"), P("panel", None, None, "lat", "lon"))
    return jax.shard_map(shards, mesh=mesh, in_specs=in_specs, out_specs=out_specs, check_vma=False)
```

time: 44.5 us -> 41.6 us (0.935)
  waiting for transfers between devices: 5.85 us -> 2.12 us
  Pallas kernels: 22.2 us -> 23 us
    pallas_call x0 -> x1, Pallas kernels: none -> 5.31 us  [edges(): pl.pallas_call(functools.partial(edges_kernel, (n_lat, n_lon, levels, row...]
    ppermute x8, waiting for transfers between devices: 4.06 us -> 0.02 us  [swap_panels(): return lax.ppermute(value, ('panel', 'lat'), pairs)]
    pallas_call x1, Pallas kernels: 11 us -> 8.46 us  [stencil(): pl.pallas_call(functools.partial(stencil_kernel, (n_lat, n_lon, levels, r...]
    pallas_call x1, Pallas kernels: 5.53 us -> 4.09 us  [donate(): pl.pallas_call(functools.partial(donate_kernel, n_lat, n_lon, rows, cols,...]
    pallas_call x1, Pallas kernels: 4.84 us -> 4.33 us  [prepare(): pl.pallas_call(functools.partial(prepare_kernel, lax.axis_size('lat'), la...]
  transfers between devices with their start and end apart: 12 -> 12, of which waited for: 3 -> 2; matrix products, arithmetic and copies ran while one was open for 0% -> 0% of each run, Pallas kernels for 23% -> 41%
where the time goes in v2:
time: 41.6 us; the launch traced here: 41.4 us
  Pallas kernels  23 us (55%)
  starting transfers between devices  15.5 us (37%)
  waiting for transfers between devices  2.12 us (5%)
  between operations  0.77 us (2%)
    pallas_call x1, Pallas kernels, stencil(): pl.pallas_call(functools.partial(stencil_kernel, (n_lat, n_lon, levels, r...  8.46 us
    ppermute x8, starting transfers between devices, swap_panels(): return lax.ppermute(value, ('panel', 'lat'), pairs)  8.17 us
    ppermute x4, starting transfers between devices, swap_pairs(): lax.ppermute(value, axis, [(i, pair_partner(i, count, odd)) for i in rang...  7.31 us
    pallas_call x1, Pallas kernels, edges(): pl.pallas_call(functools.partial(edges_kernel, (n_lat, n_lon, levels, row...  5.31 us
    pallas_call x1, Pallas kernels, prepare(): pl.pallas_call(functools.partial(prepare_kernel, lax.axis_size('lat'), la...  4.33 us
    pallas_call x1, Pallas kernels, donate(): pl.pallas_call(functools.partial(donate_kernel, n_lat, n_lon, rows, cols,...  4.09 us
    ppermute x4, waiting for transfers between devices, swap_pairs(): lax.ppermute(value, axis, [(i, pair_partner(i, count, odd)) for i in rang...  2.1 us
  transfers between devices with their start and end apart: 12, of which 2 were waited for; matrix products, arithmetic and copies ran while one was open for 0% of the time, Pallas kernels for 41%

profile of v2, /device:TPU:0, one launch (start us, length us, event | category | flops | bytes accessed | tf_op | source)
XLA Modules:
  0.0 41.4 jit_solution(6315170447357440846)
XLA Ops:
  0.6 0.8 %ask.1 = f32[8,896]{1,0:T(8,128)S(1)} custom-call(s32[1,1,1,1664]{3,2,1,0:T(1,128)} %refs_0_.1, s32[1,1,1,1664]{3,2,1,0:T(1,128)} %corners.1, f32[1,1,1,4,1664]{4,3,2,1,0:T(4,128)} %blend.1), custom_call_target="tpu_custom_call" | custom-call | tf_op jit(solution)/shard_map/ask/pallas_call | solution.py:86
  1.4 3.4 %collective-permute-start.3 = (f32[8,896]{1,0:T(8,128)S(1)}, f32[8,896]{1,0:T(8,128)S(1)}, u32[]{:S(2)}, u32[]{:S(2)}) collective-permute-start(f32[8,896]{1,0:T(8,128)S(1)} %ask.1), channel_id=1, source_target_pairs={{0,28},{4,24},{8,20},{12,16},{16,12},{20,8},{24,4},{28,0},{1,29},{... | collective-permute-start | bytes 86024 | tf_op jit(solution)/shard_map/ppermute | solution.py:46
  4.8 0.8 %collective-permute-start.2 = (f32[8,896]{1,0:T(8,128)S(1)}, f32[8,896]{1,0:T(8,128)S(1)}, u32[]{:S(2)}, u32[]{:S(2)}) collective-permute-start(f32[8,896]{1,0:T(8,128)S(1)} %ask.1), channel_id=1, source_target_pairs={{0,24},{4,28},{8,16},{12,20},{16,8},{20,12},{24,0},{28,4},{1,25},{... | collective-permute-start | bytes 86024 | tf_op jit(solution)/shard_map/ppermute | solution.py:46
  5.6 0.1 collective-permute-start.1
  5.8 0.0 collective-permute-start
  5.8 4.3 %prepare.1 = (f32[12288,128]{1,0:T(8,128)S(1)}, f32[5,3,16,48,128]{4,3,2,1,0:T(8,128)S(1)}, f32[2,5,3,16,128]{4,3,2,1,0:T(8,128)S(1)}, f32[2,5,3,16,128]{4,3,2,1...) custom-call(f32[1,16,32,384]{3,2,1,0:T(8,128)} %rho.1, ...), custom_call_target="tpu_custom_call" | custom-call | tf_op jit(solution)/shard_map/prepare/pallas_call | solution.py:219
  10.1 0.0 copy-start
  10.1 0.0 collective-permute-done.3.refs_3_
  10.1 0.0 collective-permute-done.2.refs_2_
  10.1 0.0 collective-permute-done.1.refs_1_
  10.2 0.0 collective-permute-done.refs_0_
  10.2 2.1 %collective-permute-start.10 = (f32[2,5,3,16,128]{4,3,2,1,0:T(8,128)S(1)}, f32[2,5,3,16,128]{4,3,2,1,0:T(8,128)S(1)}, u32[]{:S(2)}, u32[]{:S(2)}) collective-permute-start(f32[2,5,3,16,128]{4,3,2,1,0:T(8,128)S(1)} %get-tuple-element.51), channel_id=1, source_target_pairs={{0,4},{4,0},{8,12},{12,8},{1,5},{5,1},{9,13},{13,9},{2,6},{6,2},{1... | collective-permute-start | bytes 737288 | tf_op jit(solution)/shard_map/ppermute | solution.py:38
  12.2 1.5 %collective-permute-start.11 = (f32[2,5,3,16,128]{4,3,2,1,0:T(8,128)S(1)}, f32[2,5,3,16,128]{4,3,2,1,0:T(8,128)S(1)}, u32[]{:S(2)}, u32[]{:S(2)}) collective-permute-start(f32[2,5,3,16,128]{4,3,2,1,0:T(8,128)S(1)} %get-tuple-element.52), channel_id=1, source_target_pairs={{0,12},{4,8},{8,4},{12,0},{1,13},{5,9},{9,5},{13,1},{2,14},{6,10},... | collective-permute-start | bytes 737288 | tf_op jit(solution)/shard_map/ppermute | solution.py:38
  13.7 4.1 %donate.1 = (f32[96,256]{1,0:T(8,128)S(1)}, f32[96,256]{1,0:T(8,128)S(1)}, f32[96,256]{1,0:T(8,128)S(1)}, f32[96,256]{1,0:T(8,128)S(1)}) custom-call(f32[8,896]{1,0:T(8,128)S(1)} %collective-permute-done.refs_0_, f32[8,896]{1,0:T(8,128)S(1)} %collective-permute-done.1.refs_1_, f32[8,896]{1,0:T(8,128)S(1)} %collective-permute-done.2.refs_2_, ...), custom_call_target="tpu_custom_call" | custom-call | tf_op jit(solution)/shard_map/donate/pallas_call | solution.py:323
  17.8 0.1 collective-permute-start.4
  17.9 1.2 %collective-permute-start.8 = (f32[2,32,128]{2,1,0:T(8,128)S(1)}, f32[2,32,128]{2,1,0:T(8,128)S(1)}, u32[]{:S(2)}, u32[]{:S(2)}) collective-permute-start(f32[2,32,128]{2,1,0:T(8,128)S(1)} %get-tuple-element.49), channel_id=1, source_target_pairs={{0,1},{1,0},{2,3},{3,2},{4,5},{5,4},{6,7},{7,6},{8,9},{9,8},{10,11... | collective-permute-start | bytes 98312 | tf_op jit(solution)/shard_map/ppermute | solution.py:38
  19.1 2.6 %collective-permute-start.9 = (f32[2,32,128]{2,1,0:T(8,128)S(1)}, f32[2,32,128]{2,1,0:T(8,128)S(1)}, u32[]{:S(2)}, u32[]{:S(2)}) collective-permute-start(f32[2,32,128]{2,1,0:T(8,128)S(1)} %get-tuple-element.50), channel_id=1, source_target_pairs={{0,3},{1,2},{2,1},{3,0},{4,7},{5,6},{6,5},{7,4},{8,11},{9,10},{10,... | collective-permute-start | bytes 98312 | tf_op jit(solution)/shard_map/ppermute | solution.py:38
  21.7 0.2 collective-permute-done.8.refs_6_
  21.9 1.0 %collective-permute-start.5 = (f32[96,256]{1,0:T(8,128)S(1)}, f32[96,256]{1,0:T(8,128)S(1)}, u32[]{:S(2)}, u32[]{:S(2)}) collective-permute-start(f32[96,256]{1,0:T(8,128)S(1)} %get-tuple-element.46), channel_id=1, source_target_pairs={{0,20},{4,16},{8,28},{12,24},{16,4},{20,0},{24,12},{28,8},{1,21},{... | collective-permute-start | bytes 294920 | tf_op jit(solution)/shard_map/ppermute | solution.py:46
  22.9 1.9 %collective-permute-done.9.refs_7_ = f32[2,32,128]{2,1,0:T(8,128)S(1)} collective-permute-done((f32[2,32,128]{2,1,0:T(8,128)S(1)}, f32[2,32,128]{2,1,0:T(8,128)S(1)}, u32[]{:S(2)}, u32[]{:S(2)}) %collective-permute-start.9) | collective-permute-done | bytes 32800 | tf_op jit(solution)/shard_map/ppermute | solution.py:38
  24.8 0.0 collective-permute-start.6
  24.8 0.0 collective-permute-done.4.refs_2_
  24.8 2.7 %collective-permute-start.7 = (f32[96,256]{1,0:T(8,128)S(1)}, f32[96,256]{1,0:T(8,128)S(1)}, u32[]{:S(2)}, u32[]{:S(2)}) collective-permute-start(f32[96,256]{1,0:T(8,128)S(1)} %get-tuple-element.48), channel_id=1, source_target_pairs={{0,28},{4,24},{8,20},{12,16},{16,12},{20,8},{24,4},{28,0},{1,29},{... | collective-permute-start | bytes 294920 | tf_op jit(solution)/shard_map/ppermute | solution.py:46
  27.5 0.0 copy-done
  27.5 8.5 %stencil.1 = (f32[1,5,16,32,384]{4,3,2,1,0:T(8,128)}, f32[1,5,16,32,384]{4,3,2,1,0:T(8,128)}, f32[5,16,32,384]{3,2,1,0:T(8,128)S(1)}, f32[5,16,32,384]{3,2,1,0:T(8,128)S(1)}) custom-call(f32[5,3,16,48,128]{4,3,2,1,0:T(8,128)S(1)} %get-tuple-element.53.block.refs_10_, f32[2,32,128]{2,1,0:T(8,128)S(1)} %get-tuple-element.54.row_box.refs_11_, ...), custom_call_target="tpu_custom_call" | custom-call | flops 49152000 | bytes 15728640 | tf_op jit(solution)/shard_map/stencil/pallas_call | solution.py:528
  36.0 0.0 collective-permute-done.5.refs_3_
  36.0 0.0 collective-permute-done.6.refs_4_
  36.0 0.0 collective-permute-done.7.refs_5_
  36.0 0.0 collective-permute-done.10.refs_8_
  36.0 0.0 collective-permute-done.11.refs_9_
  36.1 0.0 copy-done.1
  36.1 5.3 %edges.1 = (f32[1,5,16,32,384]{4,3,2,1,0:T(8,128)}, f32[1,5,16,32,384]{4,3,2,1,0:T(8,128)}) custom-call(s32[1,1,1,1664]{3,2,1,0:T(1,128)S(1)} %copy-done.1, f32[1,1,1,2,1664]{4,3,2,1,0:T(2,128)S(1)} %copy-done.2, f32[96,256]{1,0:T(8,128)S(1)} %collective-permute-done.4.refs_2_, ...), custom_call_target="tpu_custom_call", output_to_operand_aliasing={{0}: (14, {}), {1}: (15, {})} | custom-call | flops 7864320 | bytes 7864320 | tf_op jit(solution)/shard_map/edges/pallas_call | solution.py:785
  (3 shorter events, 0.0 us)
Async XLA Ops:
  1.4 8.7 %collective-permute-start.3 = (f32[8,896]{1,0:T(8,128)S(1)}, f32[8,896]{1,0:T(8,128)S(1)}, u32[]{:S(2)}, u32[]{:S(2)}) collective-permute-start(f32[8,896]{1,0:T(8,128)S(1)} %ask.1), channel_id=1, source_target_pairs={{0,28},{4,24},{8,20},{12,16},{16,12},{20,8},{24,4},{28,0},{1,29},{... | collective-permute-start | bytes 86024 | tf_op jit(solution)/shard_map/ppermute | solution.py:46
  4.8 5.3 %collective-permute-start.2 = (f32[8,896]{1,0:T(8,128)S(1)}, f32[8,896]{1,0:T(8,128)S(1)}, u32[]{:S(2)}, u32[]{:S(2)}) collective-permute-start(f32[8,896]{1,0:T(8,128)S(1)} %ask.1), channel_id=1, source_target_pairs={{0,24},{4,28},{8,16},{12,20},{16,8},{20,12},{24,0},{28,4},{1,25},{... | collective-permute-start | bytes 86024 | tf_op jit(solution)/shard_map/ppermute | solution.py:46
  5.6 4.5 %collective-permute-start.1 = (f32[8,896]{1,0:T(8,128)S(1)}, f32[8,896]{1,0:T(8,128)S(1)}, u32[]{:S(2)}, u32[]{:S(2)}) collective-permute-start(f32[8,896]{1,0:T(8,128)S(1)} %ask.1), channel_id=1, source_target_pairs={{0,20},{4,16},{8,28},{12,24},{16,4},{20,0},{24,12},{28,8},{1,21},{... | collective-permute-start | bytes 86024 | tf_op jit(solution)/shard_map/ppermute | solution.py:46
  5.8 4.4 %collective-permute-start = (f32[8,896]{1,0:T(8,128)S(1)}, f32[8,896]{1,0:T(8,128)S(1)}, u32[]{:S(2)}, u32[]{:S(2)}) collective-permute-start(f32[8,896]{1,0:T(8,128)S(1)} %ask.1), channel_id=1, source_target_pairs={{0,16},{4,20},{8,24},{12,28},{16,0},{20,4},{24,8},{28,12},{1,17},{... | collective-permute-start | bytes 86024 | tf_op jit(solution)/shard_map/ppermute | solution.py:46
  10.1 17.4 %copy-start = (f32[1,5,16,32,384]{4,3,2,1,0:T(8,128)S(1)}, f32[1,5,16,32,384]{4,3,2,1,0:T(8,128)}, u32[]{:S(2)}) copy-start(f32[1,5,16,32,384]{4,3,2,1,0:T(8,128)} %outset.1) | copy-start | bytes 11796484
  10.2 25.9 %collective-permute-start.10 = (f32[2,5,3,16,128]{4,3,2,1,0:T(8,128)S(1)}, f32[2,5,3,16,128]{4,3,2,1,0:T(8,128)S(1)}, u32[]{:S(2)}, u32[]{:S(2)}) collective-permute-start(f32[2,5,3,16,128]{4,3,2,1,0:T(8,128)S(1)} %get-tuple-element.51), channel_id=1, source_target_pairs={{0,4},{4,0},{8,12},{12,8},{1,5},{5,1},{9,13},{13,9},{2,6},{6,2},{1... | collective-permute-start | bytes 737288 | tf_op jit(solution)/shard_map/ppermute | solution.py:38
  12.2 23.8 %collective-permute-start.11 = (f32[2,5,3,16,128]{4,3,2,1,0:T(8,128)S(1)}, f32[2,5,3,16,128]{4,3,2,1,0:T(8,128)S(1)}, u32[]{:S(2)}, u32[]{:S(2)}) collective-permute-start(f32[2,5,3,16,128]{4,3,2,1,0:T(8,128)S(1)} %get-tuple-element.52), channel_id=1, source_target_pairs={{0,12},{4,8},{8,4},{12,0},{1,13},{5,9},{9,5},{13,1},{2,14},{6,10},... | collective-permute-start | bytes 737288 | tf_op jit(solution)/shard_map/ppermute | solution.py:38
  17.8 7.0 %collective-permute-start.4 = (f32[96,256]{1,0:T(8,128)S(1)}, f32[96,256]{1,0:T(8,128)S(1)}, u32[]{:S(2)}, u32[]{:S(2)}) collective-permute-start(f32[96,256]{1,0:T(8,128)S(1)} %get-tuple-element.45), channel_id=1, source_target_pairs={{0,16},{4,20},{8,24},{12,28},{16,0},{20,4},{24,8},{28,12},{1,17},{... | collective-permute-start | bytes 294920 | tf_op jit(solution)/shard_map/ppermute | solution.py:46
  17.9 4.0 %collective-permute-start.8 = (f32[2,32,128]{2,1,0:T(8,128)S(1)}, f32[2,32,128]{2,1,0:T(8,128)S(1)}, u32[]{:S(2)}, u32[]{:S(2)}) collective-permute-start(f32[2,32,128]{2,1,0:T(8,128)S(1)} %get-tuple-element.49), channel_id=1, source_target_pairs={{0,1},{1,0},{2,3},{3,2},{4,5},{5,4},{6,7},{7,6},{8,9},{9,8},{10,11... | collective-permute-start | bytes 98312 | tf_op jit(solution)/shard_map/ppermute | solution.py:38
  19.1 5.7 %collective-permute-start.9 = (f32[2,32,128]{2,1,0:T(8,128)S(1)}, f32[2,32,128]{2,1,0:T(8,128)S(1)}, u32[]{:S(2)}, u32[]{:S(2)}) collective-permute-start(f32[2,32,128]{2,1,0:T(8,128)S(1)} %get-tuple-element.50), channel_id=1, source_target_pairs={{0,3},{1,2},{2,1},{3,0},{4,7},{5,6},{6,5},{7,4},{8,11},{9,10},{10,... | collective-permute-start | bytes 98312 | tf_op jit(solution)/shard_map/ppermute | solution.py:38
  21.9 14.1 %collective-permute-start.5 = (f32[96,256]{1,0:T(8,128)S(1)}, f32[96,256]{1,0:T(8,128)S(1)}, u32[]{:S(2)}, u32[]{:S(2)}) collective-permute-start(f32[96,256]{1,0:T(8,128)S(1)} %get-tuple-element.46), channel_id=1, source_target_pairs={{0,20},{4,16},{8,28},{12,24},{16,4},{20,0},{24,12},{28,8},{1,21},{... | collective-permute-start | bytes 294920 | tf_op jit(solution)/shard_map/ppermute | solution.py:46
  24.8 11.2 %collective-permute-start.6 = (f32[96,256]{1,0:T(8,128)S(1)}, f32[96,256]{1,0:T(8,128)S(1)}, u32[]{:S(2)}, u32[]{:S(2)}) collective-permute-start(f32[96,256]{1,0:T(8,128)S(1)} %get-tuple-element.47), channel_id=1, source_target_pairs={{0,24},{4,28},{8,16},{12,20},{16,8},{20,12},{24,0},{28,4},{1,25},{... | collective-permute-start | bytes 294920 | tf_op jit(solution)/shard_map/ppermute | solution.py:46
  24.8 11.3 %collective-permute-start.7 = (f32[96,256]{1,0:T(8,128)S(1)}, f32[96,256]{1,0:T(8,128)S(1)}, u32[]{:S(2)}, u32[]{:S(2)}) collective-permute-start(f32[96,256]{1,0:T(8,128)S(1)} %get-tuple-element.48), channel_id=1, source_target_pairs={{0,28},{4,24},{8,20},{12,16},{16,12},{20,8},{24,4},{28,0},{1,29},{... | collective-permute-start | bytes 294920 | tf_op jit(solution)/shard_map/ppermute | solution.py:46
  27.5 8.5 %copy-start.1 = (s32[1,1,1,1664]{3,2,1,0:T(1,128)S(1)}, s32[1,1,1,1664]{3,2,1,0:T(1,128)}, u32[]{:S(2)}) copy-start(s32[1,1,1,1664]{3,2,1,0:T(1,128)} %refs_0_.1) | copy-start | bytes 19972
  27.5 8.5 %copy-start.2 = (f32[1,1,1,2,1664]{4,3,2,1,0:T(2,128)S(1)}, f32[1,1,1,2,1664]{4,3,2,1,0:T(2,128)}, u32[]{:S(2)}) copy-start(f32[1,1,1,2,1664]{4,3,2,1,0:T(2,128)} %refs_1_.1) | copy-start | bytes 39940

commit v3 on v2

--- a/solution.py
+++ b/solution.py
@@ -27,15 +27,16 @@
     return pltpu.with_memory_space_constraint(value, pltpu.HBM)
 
 
-def pair_partner(i, count, odd):
-    if not odd:
-        return i ^ 1
-    return (i + 1) % count if i % 2 else (i - 1) % count
+def pair_partner(i, count, odd, wrap):
+    partner = i ^ 1 if not odd else (i + 1 if i % 2 else i - 1)
+    if 0 <= partner < count:
+        return partner
+    return partner % count if wrap else i
 
 
 def swap_pairs(value, axis, odd):
     count = lax.axis_size(axis)
-    return lax.ppermute(value, axis, [(i, pair_partner(i, count, odd)) for i in range(count)])
+    return lax.ppermute(value, axis, [(i, pair_partner(i, count, odd, axis == "lat")) for i in range(count)])
 
 
 def swap_panels(value, distance):
@@ -134,6 +135,12 @@
         for copy in load_copies(strip):
             copy.start()
 
+    pitch = rows + 2 * SUB
+    flat = block.reshape(5, tiles, levels * pitch, LANES)
+
+    def level_rows(field, tile, row):
+        return flat[field, tile, pl.ds(SUB + row, levels, stride=pitch), :]
+
     zero = jnp.zeros((levels, SUB, LANES), jnp.float32)
     for field in range(5):
         for tile in range(tiles):
@@ -162,7 +169,6 @@
     for strip in range(strips):
         for copy in load_copies(strip):
             copy.wait()
-
         here, there = strip * SUB, (strip + 1) * SUB
         for field in range(5):
             for tile in range(tiles):
@@ -171,12 +177,7 @@
                 ]
         for row in range(here, there):
             for tile in range(tiles):
-                stack = jnp.concatenate(
-                    [
-                        staged[f, :, row, tile * LANES : (tile + 1) * LANES] for f in range(5)
-                    ],
-                    axis=0,
-                )
+                stack = jnp.concatenate([level_rows(f, tile, row) for f in range(5)], axis=0)
                 at = row * cols + tile * LANES
                 cells[at : at + LANES, 0 : 5 * levels] = stack.T
 
@@ -189,7 +190,7 @@
                 for layer in range(2):
                     for field in range(5):
                         for tile in range(tiles):
-                            out[layer, field, tile] = block[field, tile, :, SUB + first + layer, :]
+                            out[layer, field, tile] = level_rows(field, tile, first + layer)
 
     lon_even = lax.rem(lax.axis_index("lon"), 2) == 0
     for first, to_even in ((0, jnp.logical_not(lon_even)), (cols - 2, lon_even)):
@@ -236,6 +237,7 @@
     replies = refs[n_lat + 1 : 2 * n_lat + 1]
     corners, turned, gathered, whole_box, requests, sems = refs[2 * n_lat + 1 :]
     slots = weights[0].shape[1]
+    lat_len, lon_len = 2 * cols, 2 * rows
     for distance in range(n_lat):
         for row in range(2):
             for tile in range(slots // LANES):
@@ -246,8 +248,15 @@
     copy = pltpu.make_async_copy(whole_box, requests, sems.at[0])
     copy.start()
     for distance in range(n_lat):
-        for at in range(0, slots, LANES):
+        for at in range(lat_len, slots, LANES):
             turned[distance, at : at + LANES, 0:SUB] = weights[distance][:, at : at + LANES].T
+        asker = jnp.bitwise_xor(lax.axis_index("lat"), distance)
+
+        @pl.when((asker == 0) | (asker == n_lat - 1))
+        def _(distance=distance):
+            for at in range(0, lat_len, LANES):
+                turned[distance, at : at + LANES, 0:SUB] = weights[distance][:, at : at + LANES].T
+
     copy.wait()
     lat_len, lon_len = 2 * cols, 2 * rows
     run_lat, run_lon = lat_len // n_lat, lon_len // n_lat
@@ -778,7 +787,7 @@
     rate_out, state_out, rate_box, state_box = inner
     levels, rows, cols = rate_box.shape[1:]
     n_lat, n_lon = lax.axis_size("lat"), lax.axis_size("lon")
-    chunk = 4
+    chunk = 2
     out = jax.ShapeDtypeStruct(rate_out.shape, jnp.float32)
     box = pltpu.VMEM(rate_box.shape, jnp.float32)
     n_in = n_lat + 10
@@ -834,6 +843,7 @@
     halos = (swap_pairs(even_rows, "lat", False), swap_pairs(odd_rows, "lat", True))
     replies = donate(requests, cells, rows, cols, 5 * levels)
     *replies, spin_box = lax.optimization_barrier((*replies, spin_box))
+    *sides, spin_box = lax.optimization_barrier((*sides, spin_box))
     replies = [swap_panels(reply, d) for d, reply in enumerate(replies)]
     inner = stencil(block, row_box, spin_box, outset)
     return edges(opposite_block, turning, replies, sides, halos, block, row_box, inner)

time: 41.6 us -> 40.1 us (0.964)
  the two profiles are of different devices: /device:TPU:0 before, /device:TPU:16 now
where the time goes in v3:
time: 40.1 us; the launch traced here: 39.9 us
  Pallas kernels  21.9 us (55%)
  starting transfers between devices  14.8 us (37%)
  waiting for transfers between devices  2.5 us (6%)
  between operations  0.78 us (2%)
    pallas_call x1, Pallas kernels, stencil(): pl.pallas_call(functools.partial(stencil_kernel, (n_lat, n_lon, levels, r...  8.46 us
    ppermute x8, starting transfers between devices, swap_panels(): return lax.ppermute(value, ('panel', 'lat'), pairs)  7.67 us
    ppermute x4, starting transfers between devices, swap_pairs(): lax.ppermute(value, axis, [(i, pair_partner(i, count, odd, axis == 'lat')...  7.09 us
    pallas_call x1, Pallas kernels, edges(): pl.pallas_call(functools.partial(edges_kernel, (n_lat, n_lon, levels, row...  5.39 us
    pallas_call x1, Pallas kernels, prepare(): pl.pallas_call(functools.partial(prepare_kernel, lax.axis_size('lat'), la...  3.96 us
    pallas_call x1, Pallas kernels, donate(): pl.pallas_call(functools.partial(donate_kernel, n_lat, n_lon, rows, cols,...  3.24 us
    ppermute x4, waiting for transfers between devices, swap_pairs(): lax.ppermute(value, axis, [(i, pair_partner(i, count, odd, axis == 'lat')...  2.48 us
    pallas_call x1, Pallas kernels, ask(): pl.pallas_call(ask_kernel, out_shape=jax.ShapeDtypeStruct((SUB, 2 * cols...  0.81 us
  transfers between devices with their start and end apart: 12, of which 2 were waited for; matrix products, arithmetic and copies ran while one was open for 0% of the time, Pallas kernels for 39%

profile of v3, /device:TPU:16, one launch (start us, length us, event | category | flops | bytes accessed | tf_op | source)
XLA Modules:
  0.0 39.9 jit_solution(18177309956372439256)
XLA Ops:
  0.6 0.8 %ask.1 = f32[8,896]{1,0:T(8,128)S(1)} custom-call(s32[1,1,1,1664]{3,2,1,0:T(1,128)} %refs_0_.1, s32[1,1,1,1664]{3,2,1,0:T(1,128)} %corners.1, f32[1,1,1,4,1664]{4,3,2,1,0:T(4,128)} %blend.1), custom_call_target="tpu_custom_call" | custom-call | tf_op jit(solution)/shard_map/ask/pallas_call | solution.py:87
  1.4 2.0 %collective-permute-start.3 = (f32[8,896]{1,0:T(8,128)S(1)}, f32[8,896]{1,0:T(8,128)S(1)}, u32[]{:S(2)}, u32[]{:S(2)}) collective-permute-start(f32[8,896]{1,0:T(8,128)S(1)} %ask.1), channel_id=1, source_target_pairs={{0,28},{4,24},{8,20},{12,16},{16,12},{20,8},{24,4},{28,0},{1,29},{... | collective-permute-start | bytes 86024 | tf_op jit(solution)/shard_map/ppermute | solution.py:47
  3.4 0.8 %collective-permute-start.2 = (f32[8,896]{1,0:T(8,128)S(1)}, f32[8,896]{1,0:T(8,128)S(1)}, u32[]{:S(2)}, u32[]{:S(2)}) collective-permute-start(f32[8,896]{1,0:T(8,128)S(1)} %ask.1), channel_id=1, source_target_pairs={{0,24},{4,28},{8,16},{12,20},{16,8},{20,12},{24,0},{28,4},{1,25},{... | collective-permute-start | bytes 86024 | tf_op jit(solution)/shard_map/ppermute | solution.py:47
  4.2 0.1 collective-permute-start.1
  4.3 0.5 %collective-permute-start = (f32[8,896]{1,0:T(8,128)S(1)}, f32[8,896]{1,0:T(8,128)S(1)}, u32[]{:S(2)}, u32[]{:S(2)}) collective-permute-start(f32[8,896]{1,0:T(8,128)S(1)} %ask.1), channel_id=1, source_target_pairs={{0,16},{4,20},{8,24},{12,28},{16,0},{20,4},{24,8},{28,12},{1,17},{... | collective-permute-start | bytes 86024 | tf_op jit(solution)/shard_map/ppermute | solution.py:47
  4.8 4.0 %prepare.1 = (f32[12288,128]{1,0:T(8,128)S(1)}, f32[5,3,16,48,128]{4,3,2,1,0:T(8,128)S(1)}, f32[2,5,3,16,128]{4,3,2,1,0:T(8,128)S(1)}, f32[2,5,3,16,128]{4,3,2,1...) custom-call(f32[1,16,32,384]{3,2,1,0:T(8,128)} %rho.1, ...), custom_call_target="tpu_custom_call" | custom-call | tf_op jit(solution)/shard_map/prepare/pallas_call | solution.py:220
  8.8 0.0 copy-start
  8.8 0.0 collective-permute-done.3.refs_3_
  8.8 0.0 collective-permute-done.2.refs_2_
  8.8 0.0 collective-permute-done.1.refs_1_
  8.8 0.0 collective-permute-done.refs_0_
  8.9 1.6 %collective-permute-start.10 = (f32[2,5,3,16,128]{4,3,2,1,0:T(8,128)S(1)}, f32[2,5,3,16,128]{4,3,2,1,0:T(8,128)S(1)}, u32[]{:S(2)}, u32[]{:S(2)}) collective-permute-start(f32[2,5,3,16,128]{4,3,2,1,0:T(8,128)S(1)} %get-tuple-element.57), channel_id=1, source_target_pairs={{0,4},{4,0},{8,12},{12,8},{1,5},{5,1},{9,13},{13,9},{2,6},{6,2},{1... | collective-permute-start | bytes 737288 | tf_op jit(solution)/shard_map/ppermute | solution.py:39
  10.5 1.4 %collective-permute-start.11 = (f32[2,5,3,16,128]{4,3,2,1,0:T(8,128)S(1)}, f32[2,5,3,16,128]{4,3,2,1,0:T(8,128)S(1)}, u32[]{:S(2)}, u32[]{:S(2)}) collective-permute-start(f32[2,5,3,16,128]{4,3,2,1,0:T(8,128)S(1)} %get-tuple-element.58), channel_id=1, source_target_pairs={{0,12},{4,8},{8,4},{12,0},{1,13},{5,9},{9,5},{13,1},{2,14},{6,10},... | collective-permute-start | bytes 737288 | tf_op jit(solution)/shard_map/ppermute | solution.py:39
  11.9 3.2 %donate.1 = (f32[96,256]{1,0:T(8,128)S(1)}, f32[96,256]{1,0:T(8,128)S(1)}, f32[96,256]{1,0:T(8,128)S(1)}, f32[96,256]{1,0:T(8,128)S(1)}) custom-call(f32[8,896]{1,0:T(8,128)S(1)} %collective-permute-done.refs_0_, f32[8,896]{1,0:T(8,128)S(1)} %collective-permute-done.1.refs_1_, f32[8,896]{1,0:T(8,128)S(1)} %collective-permute-done.2.refs_2_, ...), custom_call_target="tpu_custom_call" | custom-call | tf_op jit(solution)/shard_map/donate/pallas_call | solution.py:332
  15.2 0.1 collective-permute-start.4
  15.2 2.1 %collective-permute-start.8 = (f32[2,32,128]{2,1,0:T(8,128)S(1)}, f32[2,32,128]{2,1,0:T(8,128)S(1)}, u32[]{:S(2)}, u32[]{:S(2)}) collective-permute-start(f32[2,32,128]{2,1,0:T(8,128)S(1)} %get-tuple-element.52), channel_id=1, source_target_pairs={{0,1},{1,0},{2,3},{3,2},{4,5},{5,4},{6,7},{7,6},{8,9},{9,8},{10,11... | collective-permute-start | bytes 98312 | tf_op jit(solution)/shard_map/ppermute | solution.py:39
  17.4 1.9 %collective-permute-start.9 = (f32[2,32,128]{2,1,0:T(8,128)S(1)}, f32[2,32,128]{2,1,0:T(8,128)S(1)}, u32[]{:S(2)}, u32[]{:S(2)}) collective-permute-start(f32[2,32,128]{2,1,0:T(8,128)S(1)} %get-tuple-element.53), channel_id=1, source_target_pairs={{0,0},{1,2},{2,1},{3,3},{4,4},{5,6},{6,5},{7,7},{8,8},{9,10},{10,9... | collective-permute-start | bytes 98312 | tf_op jit(solution)/shard_map/ppermute | solution.py:39
  19.3 0.1 collective-permute-done.8.refs_6_
  19.4 1.4 %collective-permute-start.5 = (f32[96,256]{1,0:T(8,128)S(1)}, f32[96,256]{1,0:T(8,128)S(1)}, u32[]{:S(2)}, u32[]{:S(2)}) collective-permute-start(f32[96,256]{1,0:T(8,128)S(1)} %get-tuple-element.49), channel_id=1, source_target_pairs={{0,20},{4,16},{8,28},{12,24},{16,4},{20,0},{24,12},{28,8},{1,21},{... | collective-permute-start | bytes 294920 | tf_op jit(solution)/shard_map/ppermute | solution.py:47
  20.8 2.4 %collective-permute-done.9.refs_7_ = f32[2,32,128]{2,1,0:T(8,128)S(1)} collective-permute-done((f32[2,32,128]{2,1,0:T(8,128)S(1)}, f32[2,32,128]{2,1,0:T(8,128)S(1)}, u32[]{:S(2)}, u32[]{:S(2)}) %collective-permute-start.9) | collective-permute-done | bytes 32800 | tf_op jit(solution)/shard_map/ppermute | solution.py:39
  23.2 0.0 collective-permute-start.6
  23.2 0.0 collective-permute-done.4.refs_2_
  23.2 2.8 %collective-permute-start.7 = (f32[96,256]{1,0:T(8,128)S(1)}, f32[96,256]{1,0:T(8,128)S(1)}, u32[]{:S(2)}, u32[]{:S(2)}) collective-permute-start(f32[96,256]{1,0:T(8,128)S(1)} %get-tuple-element.51), channel_id=1, source_target_pairs={{0,28},{4,24},{8,20},{12,16},{16,12},{20,8},{24,4},{28,0},{1,29},{... | collective-permute-start | bytes 294920 | tf_op jit(solution)/shard_map/ppermute | solution.py:47
  26.0 8.5 %stencil.1 = (f32[1,5,16,32,384]{4,3,2,1,0:T(8,128)}, f32[1,5,16,32,384]{4,3,2,1,0:T(8,128)}, f32[5,16,32,384]{3,2,1,0:T(8,128)S(1)}, f32[5,16,32,384]{3,2,1,0:T(8,128)S(1)}) custom-call(f32[5,3,16,48,128]{4,3,2,1,0:T(8,128)S(1)} %get-tuple-element.59.block.refs_10_, f32[2,32,128]{2,1,0:T(8,128)S(1)} %get-tuple-element.60.row_box.refs_11_, ...), custom_call_target="tpu_custom_call" | custom-call | flops 49152000 | bytes 15728640 | tf_op jit(solution)/shard_map/stencil/pallas_call | solution.py:537
  34.5 0.0 collective-permute-done.5.refs_3_
  34.5 0.0 collective-permute-done.6.refs_4_
  34.5 0.0 collective-permute-done.7.refs_5_
  34.5 0.0 collective-permute-done.10.refs_8_
  34.5 0.0 collective-permute-done.11.refs_9_
  34.5 0.0 copy-done.1
  34.5 0.0 copy-done.2
  34.5 5.4 %edges.1 = (f32[1,5,16,32,384]{4,3,2,1,0:T(8,128)}, f32[1,5,16,32,384]{4,3,2,1,0:T(8,128)}) custom-call(s32[1,1,1,1664]{3,2,1,0:T(1,128)S(1)} %copy-done.1, f32[1,1,1,2,1664]{4,3,2,1,0:T(2,128)S(1)} %copy-done.2, f32[96,256]{1,0:T(8,128)S(1)} %collective-permute-done.4.refs_2_, ...), custom_call_target="tpu_custom_call", output_to_operand_aliasing={{0}: (14, {}), {1}: (15, {})} | custom-call | flops 7864320 | bytes 7864320 | tf_op jit(solution)/shard_map/edges/pallas_call | solution.py:794
  (3 shorter events, 0.0 us)
Async XLA Ops:
  1.4 7.4 %collective-permute-start.3 = (f32[8,896]{1,0:T(8,128)S(1)}, f32[8,896]{1,0:T(8,128)S(1)}, u32[]{:S(2)}, u32[]{:S(2)}) collective-permute-start(f32[8,896]{1,0:T(8,128)S(1)} %ask.1), channel_id=1, source_target_pairs={{0,28},{4,24},{8,20},{12,16},{16,12},{20,8},{24,4},{28,0},{1,29},{... | collective-permute-start | bytes 86024 | tf_op jit(solution)/shard_map/ppermute | solution.py:47
  3.4 5.4 %collective-permute-start.2 = (f32[8,896]{1,0:T(8,128)S(1)}, f32[8,896]{1,0:T(8,128)S(1)}, u32[]{:S(2)}, u32[]{:S(2)}) collective-permute-start(f32[8,896]{1,0:T(8,128)S(1)} %ask.1), channel_id=1, source_target_pairs={{0,24},{4,28},{8,16},{12,20},{16,8},{20,12},{24,0},{28,4},{1,25},{... | collective-permute-start | bytes 86024 | tf_op jit(solution)/shard_map/ppermute | solution.py:47
  4.2 4.7 %collective-permute-start.1 = (f32[8,896]{1,0:T(8,128)S(1)}, f32[8,896]{1,0:T(8,128)S(1)}, u32[]{:S(2)}, u32[]{:S(2)}) collective-permute-start(f32[8,896]{1,0:T(8,128)S(1)} %ask.1), channel_id=1, source_target_pairs={{0,20},{4,16},{8,28},{12,24},{16,4},{20,0},{24,12},{28,8},{1,21},{... | collective-permute-start | bytes 86024 | tf_op jit(solution)/shard_map/ppermute | solution.py:47
  4.3 4.5 %collective-permute-start = (f32[8,896]{1,0:T(8,128)S(1)}, f32[8,896]{1,0:T(8,128)S(1)}, u32[]{:S(2)}, u32[]{:S(2)}) collective-permute-start(f32[8,896]{1,0:T(8,128)S(1)} %ask.1), channel_id=1, source_target_pairs={{0,16},{4,20},{8,24},{12,28},{16,0},{20,4},{24,8},{28,12},{1,17},{... | collective-permute-start | bytes 86024 | tf_op jit(solution)/shard_map/ppermute | solution.py:47
  8.8 17.2 %copy-start = (f32[1,5,16,32,384]{4,3,2,1,0:T(8,128)S(1)}, f32[1,5,16,32,384]{4,3,2,1,0:T(8,128)}, u32[]{:S(2)}) copy-start(f32[1,5,16,32,384]{4,3,2,1,0:T(8,128)} %outset.1) | copy-start | bytes 11796484
  8.9 25.6 %collective-permute-start.10 = (f32[2,5,3,16,128]{4,3,2,1,0:T(8,128)S(1)}, f32[2,5,3,16,128]{4,3,2,1,0:T(8,128)S(1)}, u32[]{:S(2)}, u32[]{:S(2)}) collective-permute-start(f32[2,5,3,16,128]{4,3,2,1,0:T(8,128)S(1)} %get-tuple-element.57), channel_id=1, source_target_pairs={{0,4},{4,0},{8,12},{12,8},{1,5},{5,1},{9,13},{13,9},{2,6},{6,2},{1... | collective-permute-start | bytes 737288 | tf_op jit(solution)/shard_map/ppermute | solution.py:39
  10.5 24.0 %collective-permute-start.11 = (f32[2,5,3,16,128]{4,3,2,1,0:T(8,128)S(1)}, f32[2,5,3,16,128]{4,3,2,1,0:T(8,128)S(1)}, u32[]{:S(2)}, u32[]{:S(2)}) collective-permute-start(f32[2,5,3,16,128]{4,3,2,1,0:T(8,128)S(1)} %get-tuple-element.58), channel_id=1, source_target_pairs={{0,12},{4,8},{8,4},{12,0},{1,13},{5,9},{9,5},{13,1},{2,14},{6,10},... | collective-permute-start | bytes 737288 | tf_op jit(solution)/shard_map/ppermute | solution.py:39
  15.2 8.0 %collective-permute-start.4 = (f32[96,256]{1,0:T(8,128)S(1)}, f32[96,256]{1,0:T(8,128)S(1)}, u32[]{:S(2)}, u32[]{:S(2)}) collective-permute-start(f32[96,256]{1,0:T(8,128)S(1)} %get-tuple-element.48), channel_id=1, source_target_pairs={{0,16},{4,20},{8,24},{12,28},{16,0},{20,4},{24,8},{28,12},{1,17},{... | collective-permute-start | bytes 294920 | tf_op jit(solution)/shard_map/ppermute | solution.py:47
  15.2 4.1 %collective-permute-start.8 = (f32[2,32,128]{2,1,0:T(8,128)S(1)}, f32[2,32,128]{2,1,0:T(8,128)S(1)}, u32[]{:S(2)}, u32[]{:S(2)}) collective-permute-start(f32[2,32,128]{2,1,0:T(8,128)S(1)} %get-tuple-element.52), channel_id=1, source_target_pairs={{0,1},{1,0},{2,3},{3,2},{4,5},{5,4},{6,7},{7,6},{8,9},{9,8},{10,11... | collective-permute-start | bytes 98312 | tf_op jit(solution)/shard_map/ppermute | solution.py:39
  17.4 5.8 %collective-permute-start.9 = (f32[2,32,128]{2,1,0:T(8,128)S(1)}, f32[2,32,128]{2,1,0:T(8,128)S(1)}, u32[]{:S(2)}, u32[]{:S(2)}) collective-permute-start(f32[2,32,128]{2,1,0:T(8,128)S(1)} %get-tuple-element.53), channel_id=1, source_target_pairs={{0,0},{1,2},{2,1},{3,3},{4,4},{5,6},{6,5},{7,7},{8,8},{9,10},{10,9... | collective-permute-start | bytes 98312 | tf_op jit(solution)/shard_map/ppermute | solution.py:39
  19.4 15.1 %collective-permute-start.5 = (f32[96,256]{1,0:T(8,128)S(1)}, f32[96,256]{1,0:T(8,128)S(1)}, u32[]{:S(2)}, u32[]{:S(2)}) collective-permute-start(f32[96,256]{1,0:T(8,128)S(1)} %get-tuple-element.49), channel_id=1, source_target_pairs={{0,20},{4,16},{8,28},{12,24},{16,4},{20,0},{24,12},{28,8},{1,21},{... | collective-permute-start | bytes 294920 | tf_op jit(solution)/shard_map/ppermute | solution.py:47
  23.2 11.3 %collective-permute-start.6 = (f32[96,256]{1,0:T(8,128)S(1)}, f32[96,256]{1,0:T(8,128)S(1)}, u32[]{:S(2)}, u32[]{:S(2)}) collective-permute-start(f32[96,256]{1,0:T(8,128)S(1)} %get-tuple-element.50), channel_id=1, source_target_pairs={{0,24},{4,28},{8,16},{12,20},{16,8},{20,12},{24,0},{28,4},{1,25},{... | collective-permute-start | bytes 294920 | tf_op jit(solution)/shard_map/ppermute | solution.py:47
  23.2 11.3 %collective-permute-start.7 = (f32[96,256]{1,0:T(8,128)S(1)}, f32[96,256]{1,0:T(8,128)S(1)}, u32[]{:S(2)}, u32[]{:S(2)}) collective-permute-start(f32[96,256]{1,0:T(8,128)S(1)} %get-tuple-element.51), channel_id=1, source_target_pairs={{0,28},{4,24},{8,20},{12,16},{16,12},{20,8},{24,4},{28,0},{1,29},{... | collective-permute-start | bytes 294920 | tf_op jit(solution)/shard_map/ppermute | solution.py:47
  26.0 8.5 %copy-start.1 = (s32[1,1,1,1664]{3,2,1,0:T(1,128)S(1)}, s32[1,1,1,1664]{3,2,1,0:T(1,128)}, u32[]{:S(2)}) copy-start(s32[1,1,1,1664]{3,2,1,0:T(1,128)} %refs_0_.1) | copy-start | bytes 19972
  26.0 8.5 %copy-start.2 = (f32[1,1,1,2,1664]{4,3,2,1,0:T(2,128)S(1)}, f32[1,1,1,2,1664]{4,3,2,1,0:T(2,128)}, u32[]{:S(2)}) copy-start(f32[1,1,1,2,1664]{4,3,2,1,0:T(2,128)} %refs_1_.1) | copy-start | bytes 39940

commit v4 on v3

--- a/solution.py
+++ b/solution.py
@@ -396,7 +396,7 @@
         above = jnp.minimum(k + 1, levels - 1)
         radius = jnp.broadcast_to(1.0 / step_lat + k.astype(jnp.float32), (SUB, LANES))
         inv_radius = 1.0 / radius
-        for top in range(0, rows, SUB):
+        for top in range(SUB, rows - SUB, SUB):
             one_strip(k, below, above, inv_radius, inv_radius * by_lat, top)
 
     def one_strip(k, below, above, inv_radius, lat_scale, top):
@@ -542,7 +542,7 @@
         scratch_shapes=[pltpu.SemaphoreType.DMA((levels // chunk, 2))],
         compiler_params=pltpu.CompilerParams(vmem_limit_bytes=20 * MIB),
         cost_estimate=pl.CostEstimate(
-            flops=250 * levels * rows * cols,
+            flops=125 * levels * rows * cols,
             bytes_accessed=80 * levels * rows * cols,
             transcendentals=0,
         ),
@@ -563,6 +563,8 @@
         lat_odd,
         block,
         row_box,
+        spin_box,
+        outset,
         rate_in,
         state_in,
         _,
@@ -695,45 +697,162 @@
             mixed[row // levels, row % levels] = pltpu.roll(value, LANES - 2 - row, 1)
 
     def one_level(k):
+        below = jnp.maximum(k - 1, 0)
+        above = jnp.minimum(k + 1, levels - 1)
         radius = jnp.broadcast_to(1.0 / step_lat + k.astype(jnp.float32), (SUB, LANES))
         inv_radius = 1.0 / radius
         for top in range(0, rows, SUB):
+            if top in (0, rows - SUB):
+                one_strip(k, below, above, inv_radius, inv_radius * by_lat, top)
+            else:
+                for t in (0, tiles - 1):
+                    one_tile(k, inv_radius, top, t)
+
+    def one_strip(k, below, above, inv_radius, lat_scale, top):
+        strip = slice(top, top + SUB)
+        inv_sin, cot = row_box[0, strip], row_box[1, strip]
+        inv_arc = inv_radius * inv_sin
+        lon_scale = inv_arc * by_lon
+        cot_r = cot * inv_radius
+        two_r = 2.0 * inv_radius
+        curve_lat = (VISCOSITY / (12.0 * step_lat * step_lat)) * inv_radius * inv_radius
+        curve_lon = (VISCOSITY / (12.0 * step_lon * step_lon)) * inv_arc * inv_arc
+        slope_extra = (VISCOSITY * by_lat) * inv_radius * cot_r
+        radial_extra = VISCOSITY * inv_radius
+        center_weight = 2.0 * VISCOSITY + 30.0 * (curve_lat + curve_lon)
+        north, south = top == 0, top == rows - SUB
+
+        def derive(f, full):
+            here = [block[f, t, k, SUB + top : 2 * SUB + top] for t in range(tiles)]
+            ghost = mixed[f, k, strip]
+            ghost_w, ghost_e = pltpu.roll(ghost, LANES - 1, 1), pltpu.roll(ghost, 1, 1)
+            w1s = [pltpu.roll(x, 1, 1) for x in here]
+            w2s = [pltpu.roll(x, 2, 1) for x in here]
+            e1s = [pltpu.roll(x, LANES - 1, 1) for x in here]
+            e2s = [pltpu.roll(x, LANES - 2, 1) for x in here]
+            out = []
             for t in range(tiles):
-                if top in (0, rows - SUB) or t in (0, tiles - 1):
-                    one_tile(k, inv_radius, top, t)
+                at = SUB + top
+                n1, n2 = block[f, t, k, at - 1 : at + 7], block[f, t, k, at - 2 : at + 6]
+                s1, s2 = block[f, t, k, at + 1 : at + 9], block[f, t, k, at + 2 : at + 10]
+                if north:
+                    g2 = jnp.broadcast_to(halo[0, 0, f, t, pl.ds(k, 1), :], (SUB, LANES))
+                    g1 = jnp.broadcast_to(halo[0, 1, f, t, pl.ds(k, 1), :], (SUB, LANES))
+                    n1 = jnp.where(sub8 == 0, g1, n1)
+                    n2 = jnp.where(sub8 == 0, g2, jnp.where(sub8 == 1, g1, n2))
+                if south:
+                    g1 = jnp.broadcast_to(halo[1, 0, f, t, pl.ds(k, 1), :], (SUB, LANES))
+                    g2 = jnp.broadcast_to(halo[1, 1, f, t, pl.ds(k, 1), :], (SUB, LANES))
+                    s1 = jnp.where(sub8 == SUB - 1, g1, s1)
+                    s2 = jnp.where(sub8 == SUB - 1, g2, jnp.where(sub8 == SUB - 2, g1, s2))
+                w1 = jnp.where(lane8 == 0, w1s[t - 1] if t else ghost_w, w1s[t])
+                w2 = jnp.where(lane8 < 2, w2s[t - 1] if t else ghost, w2s[t])
+                last = t == tiles - 1
+                e1 = jnp.where(lane8 == LANES - 1, ghost_e if last else e1s[t + 1], e1s[t])
+                e2 = jnp.where(lane8 >= LANES - 2, ghost if last else e2s[t + 1], e2s[t])
+                low = block[f, t, below, SUB + top : 2 * SUB + top]
+                high = block[f, t, above, SUB + top : 2 * SUB + top]
+                rad = high - low
+                lat = 8.0 * (s1 - n1) - (s2 - n2)
+                lon = 8.0 * (e1 - w1) - (e2 - w2)
+                bend = None
+                if full:
+                    bend = (
+                        VISCOSITY * (high + low)
+                        + curve_lat * (16.0 * (s1 + n1) - (s2 + n2))
+                        + curve_lon * (16.0 * (e1 + w1) - (e2 + w2))
+                        - center_weight * here[t]
+                    )
+                out.append((rad, lat, lon, bend))
+            return here, out
+
+        wind_rad = [block[1, t, k, SUB + top : 2 * SUB + top] for t in range(tiles)]
+        wind_lat = [block[2, t, k, SUB + top : 2 * SUB + top] for t in range(tiles)]
+        wind_lon = [block[3, t, k, SUB + top : 2 * SUB + top] for t in range(tiles)]
+        go_rad = [0.5 * x for x in wind_rad]
+        go_lat = [lat_scale * x for x in wind_lat]
+        go_lon = [lon_scale * x for x in wind_lon]
+
+        def put(f, t, center, rate):
+            lanes = slice(t * LANES, (t + 1) * LANES)
+            rate_box[f, k, strip, lanes] = rate
+            state_box[f, k, strip, lanes] = (
+                0.75 * outset[0, f, k, strip, lanes] + 0.25 * center
+            ) + (0.25 * TIME_STEP) * rate
+
+        rho_here, rho_d = derive(0, False)
+        heat_here, heat_d = derive(4, True)
+        ratio = [heat_here[t] / rho_here[t] for t in range(tiles)]
+        press, rho_rate, heat_rate = [], [], []
+        for t in range(tiles):
+            (a, b, c, _), (d, e, g, bend) = rho_d[t], heat_d[t]
+            press.append(
+                (
+                    0.5 * (ratio[t] * a + d),
+                    lat_scale * (ratio[t] * b + e),
+                    lon_scale * (ratio[t] * c + g),
+                )
+            )
+            rho_rate.append(go_rad[t] * a + go_lat[t] * b + go_lon[t] * c)
+            heat_rate.append(
+                bend
+                + (radial_extra - go_rad[t]) * d
+                + (slope_extra - go_lat[t]) * e
+                - go_lon[t] * g
+            )
+        diverge = [two_r * wind_rad[t] + cot_r * wind_lat[t] for t in range(tiles)]
+        for f in (1, 2, 3):
+            here, d_all = derive(f, True)
+            for t in range(tiles):
+                d, e, g, bend = d_all[t]
+                spin_rad, spin_lat = spin_box[0, t, strip], spin_box[1, t, strip]
+                spin_lon = spin_box[2, t, strip]
+                rate = (
+                    bend
+                    + (radial_extra - go_rad[t]) * d
+                    + (slope_extra - go_lat[t]) * e
+                    - go_lon[t] * g
+                    - press[t][f - 1]
+                )
+                if f == 1:
+                    diverge[t] += 0.5 * d
+                    rate += inv_radius * (wind_lat[t] * wind_lat[t] + wind_lon[t] * wind_lon[t])
+                    rate += spin_lon * wind_lat[t] - spin_lat * wind_lon[t] - GRAVITY
+                elif f == 2:
+                    diverge[t] += lat_scale * e
+                    rate += cot_r * (wind_lon[t] * wind_lon[t])
+                    rate -= inv_radius * (wind_rad[t] * wind_lat[t])
+                    rate += spin_rad * wind_lon[t] - spin_lon * wind_rad[t]
+                else:
+                    diverge[t] += lon_scale * g
+                    rate -= (inv_radius * wind_rad[t] + cot_r * wind_lat[t]) * wind_lon[t]
+                    rate += spin_lat * wind_rad[t] - spin_rad * wind_lat[t]
+                put(f, t, here[t], rate)
+        for t in range(tiles):
+            put(0, t, rho_here[t], -rho_rate[t] - rho_here[t] * diverge[t])
+            put(
+                4,
+                t,
+                heat_here[t],
+                heat_rate[t] - (GAMMA - 1.0) * (heat_here[t] * diverge[t]),
+            )
 
     def one_tile(k, inv_radius, top, t):
         strip, lanes = slice(top, top + SUB), slice(t * LANES, (t + 1) * LANES)
         inv_arc = inv_radius * row_box[0, strip]
-        lat_scale, lon_scale = inv_radius * by_lat, inv_arc * by_lon
-        curve_lat = (VISCOSITY / (12.0 * step_lat * step_lat)) * inv_radius * inv_radius
+        lon_scale = inv_arc * by_lon
         curve_lon = (VISCOSITY / (12.0 * step_lon * step_lon)) * inv_arc * inv_arc
-        slope_extra = (VISCOSITY * by_lat) * inv_radius * (row_box[1, strip] * inv_radius)
-        rho, _, wind_lat, wind_lon, heat = (
+        rho, _, _, wind_lon, heat = (
             block[f, t, k, SUB + top : 2 * SUB + top] for f in range(5)
         )
-        go_lat, go_lon = lat_scale * wind_lat, lon_scale * wind_lon
+        go_lon = lon_scale * wind_lon
         ratio = heat / rho
 
         def add(total, value):
             return value if total is None else total + value
 
-        lat_d, lat_b, lon_d, lon_b = ([None] * 5 for _ in range(4))
+        lon_d, lon_b = ([None] * 5 for _ in range(2))
         for f in range(5):
-            if top == 0:
-                far = jnp.broadcast_to(halo[0, 0, f, t, pl.ds(k, 1), :], (SUB, LANES))
-                near = jnp.broadcast_to(halo[0, 1, f, t, pl.ds(k, 1), :], (SUB, LANES))
-                second = jnp.where(sub8 == 0, far, jnp.where(sub8 == 1, near, 0.0))
-                near = 8.0 * jnp.where(sub8 == 0, near, 0.0)
-                lat_d[f] = add(lat_d[f], second - near)
-                lat_b[f] = add(lat_b[f], 2.0 * near - second)
-            if top == rows - SUB:
-                near = jnp.broadcast_to(halo[1, 0, f, t, pl.ds(k, 1), :], (SUB, LANES))
-                far = jnp.broadcast_to(halo[1, 1, f, t, pl.ds(k, 1), :], (SUB, LANES))
-                second = jnp.where(sub8 == SUB - 1, far, jnp.where(sub8 == SUB - 2, near, 0.0))
-                near = 8.0 * jnp.where(sub8 == SUB - 1, near, 0.0)
-                lat_d[f] = add(lat_d[f], near - second)
-                lat_b[f] = add(lat_b[f], 2.0 * near - second)
             ghost = mixed[f, k, strip]
             if t == 0:
                 second = jnp.where(lane8 < 2, ghost, 0.0)
@@ -748,14 +867,6 @@
 
         rates = [None] * 5
         diverge = None
-        if lat_d[0] is not None:
-            diverge = add(diverge, lat_scale * lat_d[2])
-            rates[0] = add(rates[0], -go_lat * lat_d[0])
-            for f in range(1, 5):
-                rates[f] = add(
-                    rates[f], curve_lat * lat_b[f] + (slope_extra - go_lat) * lat_d[f]
-                )
-            rates[2] -= lat_scale * (ratio * lat_d[0] + lat_d[4])
         if lon_d[0] is not None:
             diverge = add(diverge, lon_scale * lon_d[3])
             rates[0] = add(rates[0], -go_lon * lon_d[0])
@@ -783,14 +894,16 @@
             copy.wait()
 
 
-def edges(partners, turning, replies, sides, halos, block, row_box, inner):
+def edges(
+    partners, turning, replies, sides, halos, block, row_box, spin_box, outset, inner
+):
     rate_out, state_out, rate_box, state_box = inner
     levels, rows, cols = rate_box.shape[1:]
     n_lat, n_lon = lax.axis_size("lat"), lax.axis_size("lon")
-    chunk = 2
+    chunk = 4
     out = jax.ShapeDtypeStruct(rate_out.shape, jnp.float32)
     box = pltpu.VMEM(rate_box.shape, jnp.float32)
-    n_in = n_lat + 10
+    n_in = n_lat + 12
     return pl.pallas_call(
         functools.partial(edges_kernel, (n_lat, n_lon, levels, rows, cols), chunk),
         out_shape=(out, out),
@@ -808,7 +921,7 @@
         ],
         compiler_params=pltpu.CompilerParams(vmem_limit_bytes=20 * MIB),
         cost_estimate=pl.CostEstimate(
-            flops=40 * levels * rows * cols,
+            flops=150 * levels * rows * cols,
             bytes_accessed=40 * levels * rows * cols,
             transcendentals=0,
         ),
@@ -821,6 +934,8 @@
         *halos,
         block,
         row_box,
+        spin_box,
+        outset,
         rate_box,
         state_box,
         rate_out,
@@ -846,7 +961,7 @@
     *sides, spin_box = lax.optimization_barrier((*sides, spin_box))
     replies = [swap_panels(reply, d) for d, reply in enumerate(replies)]
     inner = stencil(block, row_box, spin_box, outset)
-    return edges(opposite_block, turning, replies, sides, halos, block, row_box, inner)
+    return edges(opposite_block, turning, replies, sides, halos, block, row_box, spin_box, outset, inner)
 
 
 def solution(mesh):

time: 40.1 us -> 39.2 us (0.978)
  Pallas kernels: 21.9 us -> 20.9 us
    pallas_call x1, Pallas kernels: 8.46 us -> 4.84 us  [stencil(): pl.pallas_call(functools.partial(stencil_kernel, (n_lat, n_lon, levels, r...]
    pallas_call x1, Pallas kernels: 5.39 us -> 8.05 us  [edges(): pl.pallas_call(functools.partial(edges_kernel, (n_lat, n_lon, levels, row...]
  transfers between devices with their start and end apart: 12 -> 12, of which waited for: 2 -> 2; matrix products, arithmetic and copies ran while one was open for 0% -> 0% of each run, Pallas kernels for 39% -> 31%
where the time goes in v4:
time: 39.2 us; the launch traced here: 38.9 us
  Pallas kernels  20.9 us (53%)
  starting transfers between devices  14.8 us (38%)
  waiting for transfers between devices  2.51 us (6%)
  between operations  0.78 us (2%)
    pallas_call x1, Pallas kernels, edges(): pl.pallas_call(functools.partial(edges_kernel, (n_lat, n_lon, levels, row...  8.05 us
    ppermute x8, starting transfers between devices, swap_panels(): return lax.ppermute(value, ('panel', 'lat'), pairs)  7.66 us
    ppermute x4, starting transfers between devices, swap_pairs(): lax.ppermute(value, axis, [(i, pair_partner(i, count, odd, axis == 'lat')...  7.09 us
    pallas_call x1, Pallas kernels, stencil(): pl.pallas_call(functools.partial(stencil_kernel, (n_lat, n_lon, levels, r...  4.84 us
    pallas_call x1, Pallas kernels, prepare(): pl.pallas_call(functools.partial(prepare_kernel, lax.axis_size('lat'), la...  3.95 us
    pallas_call x1, Pallas kernels, donate(): pl.pallas_call(functools.partial(donate_kernel, n_lat, n_lon, rows, cols,...  3.23 us
    ppermute x4, waiting for transfers between devices, swap_pairs(): lax.ppermute(value, axis, [(i, pair_partner(i, count, odd, axis == 'lat')...  2.49 us
    pallas_call x1, Pallas kernels, ask(): pl.pallas_call(ask_kernel, out_shape=jax.ShapeDtypeStruct((SUB, 2 * cols...  0.81 us
  transfers between devices with their start and end apart: 12, of which 2 were waited for; matrix products, arithmetic and copies ran while one was open for 0% of the time, Pallas kernels for 31%

profile of v4, /device:TPU:16, one launch (start us, length us, event | category | flops | bytes accessed | tf_op | source)
XLA Modules:
  0.0 38.9 jit_solution(5880127436042203096)
XLA Ops:
  0.6 0.8 %ask.1 = f32[8,896]{1,0:T(8,128)S(1)} custom-call(s32[1,1,1,1664]{3,2,1,0:T(1,128)} %refs_0_.1, s32[1,1,1,1664]{3,2,1,0:T(1,128)} %corners.1, f32[1,1,1,4,1664]{4,3,2,1,0:T(4,128)} %blend.1), custom_call_target="tpu_custom_call" | custom-call | tf_op jit(solution)/shard_map/ask/pallas_call | solution.py:87
  1.4 2.0 %collective-permute-start.3 = (f32[8,896]{1,0:T(8,128)S(1)}, f32[8,896]{1,0:T(8,128)S(1)}, u32[]{:S(2)}, u32[]{:S(2)}) collective-permute-start(f32[8,896]{1,0:T(8,128)S(1)} %ask.1), channel_id=1, source_target_pairs={{0,28},{4,24},{8,20},{12,16},{16,12},{20,8},{24,4},{28,0},{1,29},{... | collective-permute-start | bytes 86024 | tf_op jit(solution)/shard_map/ppermute | solution.py:47
  3.4 0.8 %collective-permute-start.2 = (f32[8,896]{1,0:T(8,128)S(1)}, f32[8,896]{1,0:T(8,128)S(1)}, u32[]{:S(2)}, u32[]{:S(2)}) collective-permute-start(f32[8,896]{1,0:T(8,128)S(1)} %ask.1), channel_id=1, source_target_pairs={{0,24},{4,28},{8,16},{12,20},{16,8},{20,12},{24,0},{28,4},{1,25},{... | collective-permute-start | bytes 86024 | tf_op jit(solution)/shard_map/ppermute | solution.py:47
  4.2 0.1 collective-permute-start.1
  4.3 0.5 %collective-permute-start = (f32[8,896]{1,0:T(8,128)S(1)}, f32[8,896]{1,0:T(8,128)S(1)}, u32[]{:S(2)}, u32[]{:S(2)}) collective-permute-start(f32[8,896]{1,0:T(8,128)S(1)} %ask.1), channel_id=1, source_target_pairs={{0,16},{4,20},{8,24},{12,28},{16,0},{20,4},{24,8},{28,12},{1,17},{... | collective-permute-start | bytes 86024 | tf_op jit(solution)/shard_map/ppermute | solution.py:47
  4.8 4.0 %prepare.1 = (f32[12288,128]{1,0:T(8,128)S(1)}, f32[5,3,16,48,128]{4,3,2,1,0:T(8,128)S(1)}, f32[2,5,3,16,128]{4,3,2,1,0:T(8,128)S(1)}, f32[2,5,3,16,128]{4,3,2,1...) custom-call(f32[1,16,32,384]{3,2,1,0:T(8,128)} %rho.1, ...), custom_call_target="tpu_custom_call" | custom-call | tf_op jit(solution)/shard_map/prepare/pallas_call | solution.py:220
  8.8 0.0 copy-start
  8.8 0.0 collective-permute-done.3.refs_3_
  8.8 0.0 collective-permute-done.2.refs_2_
  8.8 0.0 collective-permute-done.1.refs_1_
  8.8 0.0 collective-permute-done.refs_0_
  8.9 1.6 %collective-permute-start.10 = (f32[2,5,3,16,128]{4,3,2,1,0:T(8,128)S(1)}, f32[2,5,3,16,128]{4,3,2,1,0:T(8,128)S(1)}, u32[]{:S(2)}, u32[]{:S(2)}) collective-permute-start(f32[2,5,3,16,128]{4,3,2,1,0:T(8,128)S(1)} %get-tuple-element.57), channel_id=1, source_target_pairs={{0,4},{4,0},{8,12},{12,8},{1,5},{5,1},{9,13},{13,9},{2,6},{6,2},{1... | collective-permute-start | bytes 737288 | tf_op jit(solution)/shard_map/ppermute | solution.py:39
  10.5 1.4 %collective-permute-start.11 = (f32[2,5,3,16,128]{4,3,2,1,0:T(8,128)S(1)}, f32[2,5,3,16,128]{4,3,2,1,0:T(8,128)S(1)}, u32[]{:S(2)}, u32[]{:S(2)}) collective-permute-start(f32[2,5,3,16,128]{4,3,2,1,0:T(8,128)S(1)} %get-tuple-element.58), channel_id=1, source_target_pairs={{0,12},{4,8},{8,4},{12,0},{1,13},{5,9},{9,5},{13,1},{2,14},{6,10},... | collective-permute-start | bytes 737288 | tf_op jit(solution)/shard_map/ppermute | solution.py:39
  11.9 3.2 %donate.1 = (f32[96,256]{1,0:T(8,128)S(1)}, f32[96,256]{1,0:T(8,128)S(1)}, f32[96,256]{1,0:T(8,128)S(1)}, f32[96,256]{1,0:T(8,128)S(1)}) custom-call(f32[8,896]{1,0:T(8,128)S(1)} %collective-permute-done.refs_0_, f32[8,896]{1,0:T(8,128)S(1)} %collective-permute-done.1.refs_1_, f32[8,896]{1,0:T(8,128)S(1)} %collective-permute-done.2.refs_2_, ...), custom_call_target="tpu_custom_call" | custom-call | tf_op jit(solution)/shard_map/donate/pallas_call | solution.py:332
  15.1 0.1 collective-permute-start.4
  15.2 2.1 %collective-permute-start.8 = (f32[2,32,128]{2,1,0:T(8,128)S(1)}, f32[2,32,128]{2,1,0:T(8,128)S(1)}, u32[]{:S(2)}, u32[]{:S(2)}) collective-permute-start(f32[2,32,128]{2,1,0:T(8,128)S(1)} %get-tuple-element.52), channel_id=1, source_target_pairs={{0,1},{1,0},{2,3},{3,2},{4,5},{5,4},{6,7},{7,6},{8,9},{9,8},{10,11... | collective-permute-start | bytes 98312 | tf_op jit(solution)/shard_map/ppermute | solution.py:39
  17.4 1.9 %collective-permute-start.9 = (f32[2,32,128]{2,1,0:T(8,128)S(1)}, f32[2,32,128]{2,1,0:T(8,128)S(1)}, u32[]{:S(2)}, u32[]{:S(2)}) collective-permute-start(f32[2,32,128]{2,1,0:T(8,128)S(1)} %get-tuple-element.53), channel_id=1, source_target_pairs={{0,0},{1,2},{2,1},{3,3},{4,4},{5,6},{6,5},{7,7},{8,8},{9,10},{10,9... | collective-permute-start | bytes 98312 | tf_op jit(solution)/shard_map/ppermute | solution.py:39
  19.3 0.1 collective-permute-done.8.refs_6_
  19.4 1.4 %collective-permute-start.5 = (f32[96,256]{1,0:T(8,128)S(1)}, f32[96,256]{1,0:T(8,128)S(1)}, u32[]{:S(2)}, u32[]{:S(2)}) collective-permute-start(f32[96,256]{1,0:T(8,128)S(1)} %get-tuple-element.49), channel_id=1, source_target_pairs={{0,20},{4,16},{8,28},{12,24},{16,4},{20,0},{24,12},{28,8},{1,21},{... | collective-permute-start | bytes 294920 | tf_op jit(solution)/shard_map/ppermute | solution.py:47
  20.7 2.4 %collective-permute-done.9.refs_7_ = f32[2,32,128]{2,1,0:T(8,128)S(1)} collective-permute-done((f32[2,32,128]{2,1,0:T(8,128)S(1)}, f32[2,32,128]{2,1,0:T(8,128)S(1)}, u32[]{:S(2)}, u32[]{:S(2)}) %collective-permute-start.9) | collective-permute-done | bytes 32800 | tf_op jit(solution)/shard_map/ppermute | solution.py:39
  23.2 0.0 collective-permute-start.6
  23.2 0.0 collective-permute-done.4.refs_2_
  23.2 2.8 %collective-permute-start.7 = (f32[96,256]{1,0:T(8,128)S(1)}, f32[96,256]{1,0:T(8,128)S(1)}, u32[]{:S(2)}, u32[]{:S(2)}) collective-permute-start(f32[96,256]{1,0:T(8,128)S(1)} %get-tuple-element.51), channel_id=1, source_target_pairs={{0,28},{4,24},{8,20},{12,16},{16,12},{20,8},{24,4},{28,0},{1,29},{... | collective-permute-start | bytes 294920 | tf_op jit(solution)/shard_map/ppermute | solution.py:47
  26.0 4.8 %stencil.1 = (f32[1,5,16,32,384]{4,3,2,1,0:T(8,128)}, f32[1,5,16,32,384]{4,3,2,1,0:T(8,128)}, f32[5,16,32,384]{3,2,1,0:T(8,128)S(1)}, f32[5,16,32,384]{3,2,1,0:T(8,128)S(1)}) custom-call(f32[5,3,16,48,128]{4,3,2,1,0:T(8,128)S(1)} %get-tuple-element.59.block.refs_10_, f32[2,32,128]{2,1,0:T(8,128)S(1)} %get-tuple-element.60.row_box.refs_11_, ...), custom_call_target="tpu_custom_call" | custom-call | flops 24576000 | bytes 15728640 | tf_op jit(solution)/shard_map/stencil/pallas_call | solution.py:537
  30.8 0.0 collective-permute-done.5.refs_3_
  30.8 0.0 collective-permute-done.6.refs_4_
  30.8 0.0 collective-permute-done.7.refs_5_
  30.9 0.0 collective-permute-done.10.refs_8_
  30.9 0.0 collective-permute-done.11.refs_9_
  30.9 0.0 copy-done.1
  30.9 0.0 copy-done.2
  30.9 8.0 %edges.1 = (f32[1,5,16,32,384]{4,3,2,1,0:T(8,128)}, f32[1,5,16,32,384]{4,3,2,1,0:T(8,128)}) custom-call(s32[1,1,1,1664]{3,2,1,0:T(1,128)S(1)} %copy-done.1, f32[1,1,1,2,1664]{4,3,2,1,0:T(2,128)S(1)} %copy-done.2, f32[96,256]{1,0:T(8,128)S(1)} %collective-permute-done.4.refs_2_, ...), custom_call_target="tpu_custom_call", output_to_operand_aliasing={{0}: (16, {}), {1}: (17, {})} | custom-call | flops 29491200 | bytes 7864320 | tf_op jit(solution)/shard_map/edges/pallas_call | solution.py:907
  (3 shorter events, 0.0 us)
Async XLA Ops:
  1.4 7.4 %collective-permute-start.3 = (f32[8,896]{1,0:T(8,128)S(1)}, f32[8,896]{1,0:T(8,128)S(1)}, u32[]{:S(2)}, u32[]{:S(2)}) collective-permute-start(f32[8,896]{1,0:T(8,128)S(1)} %ask.1), channel_id=1, source_target_pairs={{0,28},{4,24},{8,20},{12,16},{16,12},{20,8},{24,4},{28,0},{1,29},{... | collective-permute-start | bytes 86024 | tf_op jit(solution)/shard_map/ppermute | solution.py:47
  3.4 5.4 %collective-permute-start.2 = (f32[8,896]{1,0:T(8,128)S(1)}, f32[8,896]{1,0:T(8,128)S(1)}, u32[]{:S(2)}, u32[]{:S(2)}) collective-permute-start(f32[8,896]{1,0:T(8,128)S(1)} %ask.1), channel_id=1, source_target_pairs={{0,24},{4,28},{8,16},{12,20},{16,8},{20,12},{24,0},{28,4},{1,25},{... | collective-permute-start | bytes 86024 | tf_op jit(solution)/shard_map/ppermute | solution.py:47
  4.2 4.6 %collective-permute-start.1 = (f32[8,896]{1,0:T(8,128)S(1)}, f32[8,896]{1,0:T(8,128)S(1)}, u32[]{:S(2)}, u32[]{:S(2)}) collective-permute-start(f32[8,896]{1,0:T(8,128)S(1)} %ask.1), channel_id=1, source_target_pairs={{0,20},{4,16},{8,28},{12,24},{16,4},{20,0},{24,12},{28,8},{1,21},{... | collective-permute-start | bytes 86024 | tf_op jit(solution)/shard_map/ppermute | solution.py:47
  4.3 4.5 %collective-permute-start = (f32[8,896]{1,0:T(8,128)S(1)}, f32[8,896]{1,0:T(8,128)S(1)}, u32[]{:S(2)}, u32[]{:S(2)}) collective-permute-start(f32[8,896]{1,0:T(8,128)S(1)} %ask.1), channel_id=1, source_target_pairs={{0,16},{4,20},{8,24},{12,28},{16,0},{20,4},{24,8},{28,12},{1,17},{... | collective-permute-start | bytes 86024 | tf_op jit(solution)/shard_map/ppermute | solution.py:47
  8.8 17.2 %copy-start = (f32[1,5,16,32,384]{4,3,2,1,0:T(8,128)S(1)}, f32[1,5,16,32,384]{4,3,2,1,0:T(8,128)}, u32[]{:S(2)}) copy-start(f32[1,5,16,32,384]{4,3,2,1,0:T(8,128)} %refs_13_.1) | copy-start | bytes 11796484
  8.9 22.0 %collective-permute-start.10 = (f32[2,5,3,16,128]{4,3,2,1,0:T(8,128)S(1)}, f32[2,5,3,16,128]{4,3,2,1,0:T(8,128)S(1)}, u32[]{:S(2)}, u32[]{:S(2)}) collective-permute-start(f32[2,5,3,16,128]{4,3,2,1,0:T(8,128)S(1)} %get-tuple-element.57), channel_id=1, source_target_pairs={{0,4},{4,0},{8,12},{12,8},{1,5},{5,1},{9,13},{13,9},{2,6},{6,2},{1... | collective-permute-start | bytes 737288 | tf_op jit(solution)/shard_map/ppermute | solution.py:39
  10.5 20.4 %collective-permute-start.11 = (f32[2,5,3,16,128]{4,3,2,1,0:T(8,128)S(1)}, f32[2,5,3,16,128]{4,3,2,1,0:T(8,128)S(1)}, u32[]{:S(2)}, u32[]{:S(2)}) collective-permute-start(f32[2,5,3,16,128]{4,3,2,1,0:T(8,128)S(1)} %get-tuple-element.58), channel_id=1, source_target_pairs={{0,12},{4,8},{8,4},{12,0},{1,13},{5,9},{9,5},{13,1},{2,14},{6,10},... | collective-permute-start | bytes 737288 | tf_op jit(solution)/shard_map/ppermute | solution.py:39
  15.1 8.0 %collective-permute-start.4 = (f32[96,256]{1,0:T(8,128)S(1)}, f32[96,256]{1,0:T(8,128)S(1)}, u32[]{:S(2)}, u32[]{:S(2)}) collective-permute-start(f32[96,256]{1,0:T(8,128)S(1)} %get-tuple-element.48), channel_id=1, source_target_pairs={{0,16},{4,20},{8,24},{12,28},{16,0},{20,4},{24,8},{28,12},{1,17},{... | collective-permute-start | bytes 294920 | tf_op jit(solution)/shard_map/ppermute | solution.py:47
  15.2 4.1 %collective-permute-start.8 = (f32[2,32,128]{2,1,0:T(8,128)S(1)}, f32[2,32,128]{2,1,0:T(8,128)S(1)}, u32[]{:S(2)}, u32[]{:S(2)}) collective-permute-start(f32[2,32,128]{2,1,0:T(8,128)S(1)} %get-tuple-element.52), channel_id=1, source_target_pairs={{0,1},{1,0},{2,3},{3,2},{4,5},{5,4},{6,7},{7,6},{8,9},{9,8},{10,11... | collective-permute-start | bytes 98312 | tf_op jit(solution)/shard_map/ppermute | solution.py:39
  17.4 5.8 %collective-permute-start.9 = (f32[2,32,128]{2,1,0:T(8,128)S(1)}, f32[2,32,128]{2,1,0:T(8,128)S(1)}, u32[]{:S(2)}, u32[]{:S(2)}) collective-permute-start(f32[2,32,128]{2,1,0:T(8,128)S(1)} %get-tuple-element.53), channel_id=1, source_target_pairs={{0,0},{1,2},{2,1},{3,3},{4,4},{5,6},{6,5},{7,7},{8,8},{9,10},{10,9... | collective-permute-start | bytes 98312 | tf_op jit(solution)/shard_map/ppermute | solution.py:39
  19.4 11.5 %collective-permute-start.5 = (f32[96,256]{1,0:T(8,128)S(1)}, f32[96,256]{1,0:T(8,128)S(1)}, u32[]{:S(2)}, u32[]{:S(2)}) collective-permute-start(f32[96,256]{1,0:T(8,128)S(1)} %get-tuple-element.49), channel_id=1, source_target_pairs={{0,20},{4,16},{8,28},{12,24},{16,4},{20,0},{24,12},{28,8},{1,21},{... | collective-permute-start | bytes 294920 | tf_op jit(solution)/shard_map/ppermute | solution.py:47
  23.2 7.7 %collective-permute-start.6 = (f32[96,256]{1,0:T(8,128)S(1)}, f32[96,256]{1,0:T(8,128)S(1)}, u32[]{:S(2)}, u32[]{:S(2)}) collective-permute-start(f32[96,256]{1,0:T(8,128)S(1)} %get-tuple-element.50), channel_id=1, source_target_pairs={{0,24},{4,28},{8,16},{12,20},{16,8},{20,12},{24,0},{28,4},{1,25},{... | collective-permute-start | bytes 294920 | tf_op jit(solution)/shard_map/ppermute | solution.py:47
  23.2 7.7 %collective-permute-start.7 = (f32[96,256]{1,0:T(8,128)S(1)}, f32[96,256]{1,0:T(8,128)S(1)}, u32[]{:S(2)}, u32[]{:S(2)}) collective-permute-start(f32[96,256]{1,0:T(8,128)S(1)} %get-tuple-element.51), channel_id=1, source_target_pairs={{0,28},{4,24},{8,20},{12,16},{16,12},{20,8},{24,4},{28,0},{1,29},{... | collective-permute-start | bytes 294920 | tf_op jit(solution)/shard_map/ppermute | solution.py:47
  26.0 4.9 %copy-start.1 = (s32[1,1,1,1664]{3,2,1,0:T(1,128)S(1)}, s32[1,1,1,1664]{3,2,1,0:T(1,128)}, u32[]{:S(2)}) copy-start(s32[1,1,1,1664]{3,2,1,0:T(1,128)} %refs_0_.1) | copy-start | bytes 19972
  26.0 4.9 %copy-start.2 = (f32[1,1,1,2,1664]{4,3,2,1,0:T(2,128)S(1)}, f32[1,1,1,2,1664]{4,3,2,1,0:T(2,128)}, u32[]{:S(2)}) copy-start(f32[1,1,1,2,1664]{4,3,2,1,0:T(2,128)} %refs_1_.1) | copy-start | bytes 39940

commit v5 on v4

--- a/solution.py
+++ b/solution.py
@@ -140,12 +140,6 @@
 
     def level_rows(field, tile, row):
         return flat[field, tile, pl.ds(SUB + row, levels, stride=pitch), :]
-
-    zero = jnp.zeros((levels, SUB, LANES), jnp.float32)
-    for field in range(5):
-        for tile in range(tiles):
-            block[field, tile, :, 0:SUB] = zero
-            block[field, tile, :, rows + SUB :] = zero
 
     step_lat = math.pi / 2.0 / (rows * n_lat)
     step_lon = 1.5 * math.pi / (cols * n_lon)
@@ -531,7 +525,7 @@
 def stencil(block, row_box, spin_box, outset):
     levels, rows, cols = outset.shape[2:]
     n_lat, n_lon = lax.axis_size("lat"), lax.axis_size("lon")
-    chunk = 4
+    chunk = 8
     out = jax.ShapeDtypeStruct(outset.shape, jnp.float32)
     box = jax.ShapeDtypeStruct(outset.shape[1:], jnp.float32)
     return pl.pallas_call(

time: 39.2 us -> 39.1 us (level)
  no operation moved by 1% of the time
where the time goes in v5:
time: 39.1 us; the launch traced here: 38.9 us
  Pallas kernels  20.8 us (53%)
  starting transfers between devices  14.7 us (38%)
  waiting for transfers between devices  2.51 us (6%)
  between operations  0.78 us (2%)
    pallas_call x1, Pallas kernels, edges(): pl.pallas_call(functools.partial(edges_kernel, (n_lat, n_lon, levels, row...  8.05 us
    ppermute x8, starting transfers between devices, swap_panels(): return lax.ppermute(value, ('panel', 'lat'), pairs)  7.66 us
    ppermute x4, starting transfers between devices, swap_pairs(): lax.ppermute(value, axis, [(i, pair_partner(i, count, odd, axis == 'lat')...  7.09 us
    pallas_call x1, Pallas kernels, stencil(): pl.pallas_call(functools.partial(stencil_kernel, (n_lat, n_lon, levels, r...  4.92 us
    pallas_call x1, Pallas kernels, prepare(): pl.pallas_call(functools.partial(prepare_kernel, lax.axis_size('lat'), la...  3.83 us
    pallas_call x1, Pallas kernels, donate(): pl.pallas_call(functools.partial(donate_kernel, n_lat, n_lon, rows, cols,...  3.24 us
    ppermute x4, waiting for transfers between devices, swap_pairs(): lax.ppermute(value, axis, [(i, pair_partner(i, count, odd, axis == 'lat')...  2.49 us
    pallas_call x1, Pallas kernels, ask(): pl.pallas_call(ask_kernel, out_shape=jax.ShapeDtypeStruct((SUB, 2 * cols...  0.81 us
  transfers between devices with their start and end apart: 12, of which 2 were waited for; matrix products, arithmetic and copies ran while one was open for 0% of the time, Pallas kernels for 31%

profile of v5, /device:TPU:16, one launch (start us, length us, event | category | flops | bytes accessed | tf_op | source)
XLA Modules:
  0.0 38.9 jit_solution(16590583148100500888)
XLA Ops:
  0.6 0.8 %ask.1 = f32[8,896]{1,0:T(8,128)S(1)} custom-call(s32[1,1,1,1664]{3,2,1,0:T(1,128)} %refs_0_.1, s32[1,1,1,1664]{3,2,1,0:T(1,128)} %corners.1, f32[1,1,1,4,1664]{4,3,2,1,0:T(4,128)} %blend.1), custom_call_target="tpu_custom_call" | custom-call | tf_op jit(solution)/shard_map/ask/pallas_call | solution.py:87
  1.4 2.0 %collective-permute-start.3 = (f32[8,896]{1,0:T(8,128)S(1)}, f32[8,896]{1,0:T(8,128)S(1)}, u32[]{:S(2)}, u32[]{:S(2)}) collective-permute-start(f32[8,896]{1,0:T(8,128)S(1)} %ask.1), channel_id=1, source_target_pairs={{0,28},{4,24},{8,20},{12,16},{16,12},{20,8},{24,4},{28,0},{1,29},{... | collective-permute-start | bytes 86024 | tf_op jit(solution)/shard_map/ppermute | solution.py:47
  3.4 0.8 %collective-permute-start.2 = (f32[8,896]{1,0:T(8,128)S(1)}, f32[8,896]{1,0:T(8,128)S(1)}, u32[]{:S(2)}, u32[]{:S(2)}) collective-permute-start(f32[8,896]{1,0:T(8,128)S(1)} %ask.1), channel_id=1, source_target_pairs={{0,24},{4,28},{8,16},{12,20},{16,8},{20,12},{24,0},{28,4},{1,25},{... | collective-permute-start | bytes 86024 | tf_op jit(solution)/shard_map/ppermute | solution.py:47
  4.2 0.1 collective-permute-start.1
  4.3 0.5 %collective-permute-start = (f32[8,896]{1,0:T(8,128)S(1)}, f32[8,896]{1,0:T(8,128)S(1)}, u32[]{:S(2)}, u32[]{:S(2)}) collective-permute-start(f32[8,896]{1,0:T(8,128)S(1)} %ask.1), channel_id=1, source_target_pairs={{0,16},{4,20},{8,24},{12,28},{16,0},{20,4},{24,8},{28,12},{1,17},{... | collective-permute-start | bytes 86024 | tf_op jit(solution)/shard_map/ppermute | solution.py:47
  4.8 3.8 %prepare.1 = (f32[12288,128]{1,0:T(8,128)S(1)}, f32[5,3,16,48,128]{4,3,2,1,0:T(8,128)S(1)}, f32[2,5,3,16,128]{4,3,2,1,0:T(8,128)S(1)}, f32[2,5,3,16,128]{4,3,2,1...) custom-call(f32[1,16,32,384]{3,2,1,0:T(8,128)} %rho.1, ...), custom_call_target="tpu_custom_call" | custom-call | tf_op jit(solution)/shard_map/prepare/pallas_call | solution.py:214
  8.7 0.0 copy-start
  8.7 0.0 collective-permute-done.3.refs_3_
  8.7 0.0 collective-permute-done.2.refs_2_
  8.7 0.0 collective-permute-done.1.refs_1_
  8.7 0.0 collective-permute-done.refs_0_
  8.7 1.6 %collective-permute-start.10 = (f32[2,5,3,16,128]{4,3,2,1,0:T(8,128)S(1)}, f32[2,5,3,16,128]{4,3,2,1,0:T(8,128)S(1)}, u32[]{:S(2)}, u32[]{:S(2)}) collective-permute-start(f32[2,5,3,16,128]{4,3,2,1,0:T(8,128)S(1)} %get-tuple-element.57), channel_id=1, source_target_pairs={{0,4},{4,0},{8,12},{12,8},{1,5},{5,1},{9,13},{13,9},{2,6},{6,2},{1... | collective-permute-start | bytes 737288 | tf_op jit(solution)/shard_map/ppermute | solution.py:39
  10.3 1.4 %collective-permute-start.11 = (f32[2,5,3,16,128]{4,3,2,1,0:T(8,128)S(1)}, f32[2,5,3,16,128]{4,3,2,1,0:T(8,128)S(1)}, u32[]{:S(2)}, u32[]{:S(2)}) collective-permute-start(f32[2,5,3,16,128]{4,3,2,1,0:T(8,128)S(1)} %get-tuple-element.58), channel_id=1, source_target_pairs={{0,12},{4,8},{8,4},{12,0},{1,13},{5,9},{9,5},{13,1},{2,14},{6,10},... | collective-permute-start | bytes 737288 | tf_op jit(solution)/shard_map/ppermute | solution.py:39
  11.8 3.2 %donate.1 = (f32[96,256]{1,0:T(8,128)S(1)}, f32[96,256]{1,0:T(8,128)S(1)}, f32[96,256]{1,0:T(8,128)S(1)}, f32[96,256]{1,0:T(8,128)S(1)}) custom-call(f32[8,896]{1,0:T(8,128)S(1)} %collective-permute-done.refs_0_, f32[8,896]{1,0:T(8,128)S(1)} %collective-permute-done.1.refs_1_, f32[8,896]{1,0:T(8,128)S(1)} %collective-permute-done.2.refs_2_, ...), custom_call_target="tpu_custom_call" | custom-call | tf_op jit(solution)/shard_map/donate/pallas_call | solution.py:326
  15.0 0.1 collective-permute-start.4
  15.1 2.1 %collective-permute-start.8 = (f32[2,32,128]{2,1,0:T(8,128)S(1)}, f32[2,32,128]{2,1,0:T(8,128)S(1)}, u32[]{:S(2)}, u32[]{:S(2)}) collective-permute-start(f32[2,32,128]{2,1,0:T(8,128)S(1)} %get-tuple-element.52), channel_id=1, source_target_pairs={{0,1},{1,0},{2,3},{3,2},{4,5},{5,4},{6,7},{7,6},{8,9},{9,8},{10,11... | collective-permute-start | bytes 98312 | tf_op jit(solution)/shard_map/ppermute | solution.py:39
  17.2 1.9 %collective-permute-start.9 = (f32[2,32,128]{2,1,0:T(8,128)S(1)}, f32[2,32,128]{2,1,0:T(8,128)S(1)}, u32[]{:S(2)}, u32[]{:S(2)}) collective-permute-start(f32[2,32,128]{2,1,0:T(8,128)S(1)} %get-tuple-element.53), channel_id=1, source_target_pairs={{0,0},{1,2},{2,1},{3,3},{4,4},{5,6},{6,5},{7,7},{8,8},{9,10},{10,9... | collective-permute-start | bytes 98312 | tf_op jit(solution)/shard_map/ppermute | solution.py:39
  19.2 0.1 collective-permute-done.8.refs_6_
  19.2 1.4 %collective-permute-start.5 = (f32[96,256]{1,0:T(8,128)S(1)}, f32[96,256]{1,0:T(8,128)S(1)}, u32[]{:S(2)}, u32[]{:S(2)}) collective-permute-start(f32[96,256]{1,0:T(8,128)S(1)} %get-tuple-element.49), channel_id=1, source_target_pairs={{0,20},{4,16},{8,28},{12,24},{16,4},{20,0},{24,12},{28,8},{1,21},{... | collective-permute-start | bytes 294920 | tf_op jit(solution)/shard_map/ppermute | solution.py:47
  20.6 2.4 %collective-permute-done.9.refs_7_ = f32[2,32,128]{2,1,0:T(8,128)S(1)} collective-permute-done((f32[2,32,128]{2,1,0:T(8,128)S(1)}, f32[2,32,128]{2,1,0:T(8,128)S(1)}, u32[]{:S(2)}, u32[]{:S(2)}) %collective-permute-start.9) | collective-permute-done | bytes 32800 | tf_op jit(solution)/shard_map/ppermute | solution.py:39
  23.0 0.0 collective-permute-start.6
  23.0 0.0 collective-permute-done.4.refs_2_
  23.0 2.8 %collective-permute-start.7 = (f32[96,256]{1,0:T(8,128)S(1)}, f32[96,256]{1,0:T(8,128)S(1)}, u32[]{:S(2)}, u32[]{:S(2)}) collective-permute-start(f32[96,256]{1,0:T(8,128)S(1)} %get-tuple-element.51), channel_id=1, source_target_pairs={{0,28},{4,24},{8,20},{12,16},{16,12},{20,8},{24,4},{28,0},{1,29},{... | collective-permute-start | bytes 294920 | tf_op jit(solution)/shard_map/ppermute | solution.py:47
  25.9 4.9 %stencil.1 = (f32[1,5,16,32,384]{4,3,2,1,0:T(8,128)}, f32[1,5,16,32,384]{4,3,2,1,0:T(8,128)}, f32[5,16,32,384]{3,2,1,0:T(8,128)S(1)}, f32[5,16,32,384]{3,2,1,0:T(8,128)S(1)}) custom-call(f32[5,3,16,48,128]{4,3,2,1,0:T(8,128)S(1)} %get-tuple-element.59.block.refs_10_, f32[2,32,128]{2,1,0:T(8,128)S(1)} %get-tuple-element.60.row_box.refs_11_, ...), custom_call_target="tpu_custom_call" | custom-call | flops 24576000 | bytes 15728640 | tf_op jit(solution)/shard_map/stencil/pallas_call | solution.py:531
  30.8 0.0 collective-permute-done.5.refs_3_
  30.8 0.0 collective-permute-done.6.refs_4_
  30.8 0.0 collective-permute-done.7.refs_5_
  30.8 0.0 collective-permute-done.10.refs_8_
  30.8 0.0 collective-permute-done.11.refs_9_
  30.8 0.0 copy-done.1
  30.8 0.0 copy-done.2
  30.8 8.0 %edges.1 = (f32[1,5,16,32,384]{4,3,2,1,0:T(8,128)}, f32[1,5,16,32,384]{4,3,2,1,0:T(8,128)}) custom-call(s32[1,1,1,1664]{3,2,1,0:T(1,128)S(1)} %copy-done.1, f32[1,1,1,2,1664]{4,3,2,1,0:T(2,128)S(1)} %copy-done.2, f32[96,256]{1,0:T(8,128)S(1)} %collective-permute-done.4.refs_2_, ...), custom_call_target="tpu_custom_call", output_to_operand_aliasing={{0}: (16, {}), {1}: (17, {})} | custom-call | flops 29491200 | bytes 7864320 | tf_op jit(solution)/shard_map/edges/pallas_call | solution.py:901
  (3 shorter events, 0.0 us)
Async XLA Ops:
  1.4 7.2 %collective-permute-start.3 = (f32[8,896]{1,0:T(8,128)S(1)}, f32[8,896]{1,0:T(8,128)S(1)}, u32[]{:S(2)}, u32[]{:S(2)}) collective-permute-start(f32[8,896]{1,0:T(8,128)S(1)} %ask.1), channel_id=1, source_target_pairs={{0,28},{4,24},{8,20},{12,16},{16,12},{20,8},{24,4},{28,0},{1,29},{... | collective-permute-start | bytes 86024 | tf_op jit(solution)/shard_map/ppermute | solution.py:47
  3.4 5.3 %collective-permute-start.2 = (f32[8,896]{1,0:T(8,128)S(1)}, f32[8,896]{1,0:T(8,128)S(1)}, u32[]{:S(2)}, u32[]{:S(2)}) collective-permute-start(f32[8,896]{1,0:T(8,128)S(1)} %ask.1), channel_id=1, source_target_pairs={{0,24},{4,28},{8,16},{12,20},{16,8},{20,12},{24,0},{28,4},{1,25},{... | collective-permute-start | bytes 86024 | tf_op jit(solution)/shard_map/ppermute | solution.py:47
  4.2 4.5 %collective-permute-start.1 = (f32[8,896]{1,0:T(8,128)S(1)}, f32[8,896]{1,0:T(8,128)S(1)}, u32[]{:S(2)}, u32[]{:S(2)}) collective-permute-start(f32[8,896]{1,0:T(8,128)S(1)} %ask.1), channel_id=1, source_target_pairs={{0,20},{4,16},{8,28},{12,24},{16,4},{20,0},{24,12},{28,8},{1,21},{... | collective-permute-start | bytes 86024 | tf_op jit(solution)/shard_map/ppermute | solution.py:47
  4.3 4.4 %collective-permute-start = (f32[8,896]{1,0:T(8,128)S(1)}, f32[8,896]{1,0:T(8,128)S(1)}, u32[]{:S(2)}, u32[]{:S(2)}) collective-permute-start(f32[8,896]{1,0:T(8,128)S(1)} %ask.1), channel_id=1, source_target_pairs={{0,16},{4,20},{8,24},{12,28},{16,0},{20,4},{24,8},{28,12},{1,17},{... | collective-permute-start | bytes 86024 | tf_op jit(solution)/shard_map/ppermute | solution.py:47
  8.7 17.2 %copy-start = (f32[1,5,16,32,384]{4,3,2,1,0:T(8,128)S(1)}, f32[1,5,16,32,384]{4,3,2,1,0:T(8,128)}, u32[]{:S(2)}) copy-start(f32[1,5,16,32,384]{4,3,2,1,0:T(8,128)} %refs_13_.1) | copy-start | bytes 11796484
  8.7 22.1 %collective-permute-start.10 = (f32[2,5,3,16,128]{4,3,2,1,0:T(8,128)S(1)}, f32[2,5,3,16,128]{4,3,2,1,0:T(8,128)S(1)}, u32[]{:S(2)}, u32[]{:S(2)}) collective-permute-start(f32[2,5,3,16,128]{4,3,2,1,0:T(8,128)S(1)} %get-tuple-element.57), channel_id=1, source_target_pairs={{0,4},{4,0},{8,12},{12,8},{1,5},{5,1},{9,13},{13,9},{2,6},{6,2},{1... | collective-permute-start | bytes 737288 | tf_op jit(solution)/shard_map/ppermute | solution.py:39
  10.3 20.5 %collective-permute-start.11 = (f32[2,5,3,16,128]{4,3,2,1,0:T(8,128)S(1)}, f32[2,5,3,16,128]{4,3,2,1,0:T(8,128)S(1)}, u32[]{:S(2)}, u32[]{:S(2)}) collective-permute-start(f32[2,5,3,16,128]{4,3,2,1,0:T(8,128)S(1)} %get-tuple-element.58), channel_id=1, source_target_pairs={{0,12},{4,8},{8,4},{12,0},{1,13},{5,9},{9,5},{13,1},{2,14},{6,10},... | collective-permute-start | bytes 737288 | tf_op jit(solution)/shard_map/ppermute | solution.py:39
  15.0 8.0 %collective-permute-start.4 = (f32[96,256]{1,0:T(8,128)S(1)}, f32[96,256]{1,0:T(8,128)S(1)}, u32[]{:S(2)}, u32[]{:S(2)}) collective-permute-start(f32[96,256]{1,0:T(8,128)S(1)} %get-tuple-element.48), channel_id=1, source_target_pairs={{0,16},{4,20},{8,24},{12,28},{16,0},{20,4},{24,8},{28,12},{1,17},{... | collective-permute-start | bytes 294920 | tf_op jit(solution)/shard_map/ppermute | solution.py:47
  15.1 4.1 %collective-permute-start.8 = (f32[2,32,128]{2,1,0:T(8,128)S(1)}, f32[2,32,128]{2,1,0:T(8,128)S(1)}, u32[]{:S(2)}, u32[]{:S(2)}) collective-permute-start(f32[2,32,128]{2,1,0:T(8,128)S(1)} %get-tuple-element.52), channel_id=1, source_target_pairs={{0,1},{1,0},{2,3},{3,2},{4,5},{5,4},{6,7},{7,6},{8,9},{9,8},{10,11... | collective-permute-start | bytes 98312 | tf_op jit(solution)/shard_map/ppermute | solution.py:39
  17.2 5.8 %collective-permute-start.9 = (f32[2,32,128]{2,1,0:T(8,128)S(1)}, f32[2,32,128]{2,1,0:T(8,128)S(1)}, u32[]{:S(2)}, u32[]{:S(2)}) collective-permute-start(f32[2,32,128]{2,1,0:T(8,128)S(1)} %get-tuple-element.53), channel_id=1, source_target_pairs={{0,0},{1,2},{2,1},{3,3},{4,4},{5,6},{6,5},{7,7},{8,8},{9,10},{10,9... | collective-permute-start | bytes 98312 | tf_op jit(solution)/shard_map/ppermute | solution.py:39
  19.2 11.6 %collective-permute-start.5 = (f32[96,256]{1,0:T(8,128)S(1)}, f32[96,256]{1,0:T(8,128)S(1)}, u32[]{:S(2)}, u32[]{:S(2)}) collective-permute-start(f32[96,256]{1,0:T(8,128)S(1)} %get-tuple-element.49), channel_id=1, source_target_pairs={{0,20},{4,16},{8,28},{12,24},{16,4},{20,0},{24,12},{28,8},{1,21},{... | collective-permute-start | bytes 294920 | tf_op jit(solution)/shard_map/ppermute | solution.py:47
  23.0 7.7 %collective-permute-start.6 = (f32[96,256]{1,0:T(8,128)S(1)}, f32[96,256]{1,0:T(8,128)S(1)}, u32[]{:S(2)}, u32[]{:S(2)}) collective-permute-start(f32[96,256]{1,0:T(8,128)S(1)} %get-tuple-element.50), channel_id=1, source_target_pairs={{0,24},{4,28},{8,16},{12,20},{16,8},{20,12},{24,0},{28,4},{1,25},{... | collective-permute-start | bytes 294920 | tf_op jit(solution)/shard_map/ppermute | solution.py:47
  23.0 7.8 %collective-permute-start.7 = (f32[96,256]{1,0:T(8,128)S(1)}, f32[96,256]{1,0:T(8,128)S(1)}, u32[]{:S(2)}, u32[]{:S(2)}) collective-permute-start(f32[96,256]{1,0:T(8,128)S(1)} %get-tuple-element.51), channel_id=1, source_target_pairs={{0,28},{4,24},{8,20},{12,16},{16,12},{20,8},{24,4},{28,0},{1,29},{... | collective-permute-start | bytes 294920 | tf_op jit(solution)/shard_map/ppermute | solution.py:47
  25.8 5.0 %copy-start.1 = (s32[1,1,1,1664]{3,2,1,0:T(1,128)S(1)}, s32[1,1,1,1664]{3,2,1,0:T(1,128)}, u32[]{:S(2)}) copy-start(s32[1,1,1,1664]{3,2,1,0:T(1,128)} %refs_0_.1) | copy-start | bytes 19972
  25.8 5.0 %copy-start.2 = (f32[1,1,1,2,1664]{4,3,2,1,0:T(2,128)S(1)}, f32[1,1,1,2,1664]{4,3,2,1,0:T(2,128)}, u32[]{:S(2)}) copy-start(f32[1,1,1,2,1664]{4,3,2,1,0:T(2,128)} %refs_1_.1) | copy-start | bytes 39940
